TPU v7x, 32 devices: a whole 2x2x4 slice. The times are simulated.
32 devices in a mesh: dap: 8 (over z, core), ch: 4 (over y, x).
Axes of the slice: x: 2, y: 2, z: 4, core: 2. Of those that a mesh axis runs over, the one named last changes fastest.
Arguments:
- pair_rep: bfloat16 [120, 120, 128], P('dap', 'ch'), may hold values from -400 to 400
- residue_mask: int32 [120], replicated, may hold values 0 or 1
- w_proj: bfloat16 [128, 512], replicated, may hold values from -0.5 to 0.5
- w_gate: bfloat16 [128, 128], replicated, may hold values from -0.5 to 0.5
- w_out: bfloat16 [128, 128], replicated, may hold values from -0.5 to 0.5
- cotangent: bfloat16 [120, 120, 128], P('dap', 'ch'), may hold values from -6 to 6
Outputs:
- pair_update: bfloat16 [120, 120, 128], P('dap', 'ch')
- grad_pair: bfloat16 [120, 120, 128], P('dap', 'ch')
Inputs may be any that keep to these rules, and one draw needn't show every extreme that they name: `residue_mask`: 1 marks a residue of the crop, 0 a padding position.
All inputs are finite; a program needn't handle non-finite values.
Results may differ from a plain program's by a relative error of at most 0.0085.
Values may be sent and summed in bfloat16 or wider, within the bound.
No kernel may reach another device: no remote copies, remote signals or barrier semaphores. Data moves between devices by JAX's collectives and lax.ppermute only.
A program may use at most 64 MiB of HBM per device.

v0:
```python
import jax
import jax.numpy as jnp
from jax import lax
from jax.sharding import PartitionSpec as P

EPSILON = 1e-05


def normalize(values, axis):
    center = jnp.mean(values, axis=axis, keepdims=True)
    spread = values - center
    scale_inv = lax.rsqrt(jnp.mean(spread * spread, axis=axis, keepdims=True) + EPSILON)
    return (spread * scale_inv, scale_inv)


def norm_back(grad_in, normed, scale_inv, axis):
    first = jnp.mean(grad_in, axis=axis, keepdims=True)
    second = jnp.mean(grad_in * normed, axis=axis, keepdims=True)
    return scale_inv * (grad_in - first - normed * second)


def on_device(pair_rep, residue_mask, w_proj, w_gate, w_out, cotangent):
    row_count, columns, channels = pair_rep.shape
    hidden_width = w_out.shape[0]
    row_start = lax.axis_index("dap") * row_count
    col_start = lax.axis_index("ch") * columns
    live_flags = residue_mask.astype(jnp.float32)
    row_live = lax.dynamic_slice_in_dim(live_flags, row_start, row_count, 0)
    col_live = lax.dynamic_slice_in_dim(live_flags, col_start, columns, 0)
    cell_mask = row_live[:, None] * col_live[None, :]
    normed, pair_scale = normalize(pair_rep.astype(jnp.float32), 2)
    normed_half = normed.astype(jnp.bfloat16)
    projected = jnp.einsum("rkd,de->erk", normed_half, w_proj, preferred_element_type=jnp.float32)
    left_sig = jax.nn.sigmoid(projected[:hidden_width])
    left_val = projected[hidden_width : 2 * hidden_width]
    right_sig = jax.nn.sigmoid(projected[2 * hidden_width : 3 * hidden_width])
    right_val = projected[3 * hidden_width :]
    left_cells = (left_sig * left_val * cell_mask).astype(jnp.bfloat16)
    right_cells = (right_sig * right_val * cell_mask).astype(jnp.bfloat16)
    gate_values = jax.nn.sigmoid(
        jnp.einsum("rkd,de->rke", normed_half, w_gate, preferred_element_type=jnp.float32)
    )
    left_rows, right_rows = (
        lax.all_to_all(left_cells, "ch", split_axis=0, concat_axis=2, tiled=True),
        lax.all_to_all(right_cells, "ch", split_axis=0, concat_axis=2, tiled=True),
    )
    product = jnp.einsum(
        "cik,cjk->cij",
        left_rows,
        lax.all_gather(right_rows, "dap", axis=1, tiled=True),
        preferred_element_type=jnp.float32,
    ).astype(jnp.bfloat16)
    product_cells = lax.all_to_all(product, "ch", split_axis=2, concat_axis=0, tiled=True)
    hidden_norm, hidden_scale = normalize(product_cells.astype(jnp.float32), 0)
    hidden_half = hidden_norm.astype(jnp.bfloat16)
    projected_out = jnp.einsum(
        "hrk,hd->rkd", hidden_half, w_out, preferred_element_type=jnp.float32
    )
    pair_update = (gate_values * projected_out).astype(jnp.bfloat16)
    upstream = cotangent.astype(jnp.float32)
    grad_out = (upstream * gate_values).astype(jnp.bfloat16)
    grad_logit = (upstream * projected_out * gate_values * (1.0 - gate_values)).astype(jnp.bfloat16)
    grad_hidden = jnp.einsum("rkd,hd->hrk", grad_out, w_out, preferred_element_type=jnp.float32)
    grad_product = norm_back(grad_hidden, hidden_norm, hidden_scale, 0).astype(jnp.bfloat16)
    grad_rows = lax.all_to_all(grad_product, "ch", split_axis=0, concat_axis=2, tiled=True)
    piece_left = lax.all_gather(left_rows, "dap", axis=1, tiled=True)
    piece_right = lax.all_gather(right_rows, "dap", axis=1, tiled=True)
    piece_grad = lax.all_gather(grad_rows, "dap", axis=1, tiled=True)
    cross_slab = lax.dynamic_slice_in_dim(piece_grad, row_start, row_count, 2)
    new_left = jnp.einsum(
        "cij,cjk->cik", grad_rows, piece_right, preferred_element_type=jnp.float32
    )
    new_right = jnp.einsum(
        "cij,cik->cjk", cross_slab, piece_left, preferred_element_type=jnp.float32
    )
    left_back, right_back = (
        lax.all_to_all(
            new_left.astype(jnp.bfloat16), "ch", split_axis=2, concat_axis=0, tiled=True
        ),
        lax.all_to_all(
            new_right.astype(jnp.bfloat16), "ch", split_axis=2, concat_axis=0, tiled=True
        ),
    )
    masked_left = left_back.astype(jnp.float32) * cell_mask
    masked_right = right_back.astype(jnp.float32) * cell_mask
    grad_proj = jnp.concatenate(
        [
            masked_left * left_val * left_sig * (1.0 - left_sig),
            masked_left * left_sig,
            masked_right * right_val * right_sig * (1.0 - right_sig),
            masked_right * right_sig,
        ],
        axis=0,
    ).astype(jnp.bfloat16)
    grad_normed = jnp.einsum("erk,de->rkd", grad_proj, w_proj, preferred_element_type=jnp.float32)
    grad_normed = grad_normed + jnp.einsum(
        "rke,de->rkd", grad_logit, w_gate, preferred_element_type=jnp.float32
    )
    grad_pair = norm_back(grad_normed, normed, pair_scale, 2).astype(jnp.bfloat16)
    return (pair_update, grad_pair)


def solution(mesh):
    return jax.shard_map(
        on_device,
        mesh=mesh,
        in_specs=(P("dap", "ch", None), P(), P(), P(), P(), P("dap", "ch", None)),
        out_specs=(P("dap", "ch", None), P("dap", "ch", None)),
        check_vma=False,
    )
```

profile of v0, /device:TPU:0, one launch (start us, length us, event | category | flops | bytes accessed | tf_op | source)
XLA Modules:
  0.0 124.0 jit_solution(5858120735575920195)
XLA Ops:
  0.7 1.1 convert_reduce_fusion
  3.9 1.3 %reshape.95 = bf16[4,2,7200]{2,1,0:T(2,128)(2,1)} reshape(bf16[128,15,30]{2,1,0:T(8,128)(2,1)S(1)} %copy.73) | data formatting | bytes 230400
  5.2 5.2 %all-to-all-start.1 = ((bf16[4,2,7200]{2,1,0:T(2,128)(2,1)}), bf16[4,2,7200]{2,1,0:T(2,128)(2,1)S(1)}, u32[]{:S(2)}, u32[]{:S(2)}) async-start(bf16[4,2,7200]{2,1,0:T(2,128)(2,1)} %reshape.95), calls=%async_computation.1 | async-start | bytes 233472 | tf_op jit(solution)/shard_map/all_to_all | solution.py:45
  10.9 1.3 %reshape.97 = bf16[4,2,7200]{2,1,0:T(2,128)(2,1)} reshape(bf16[128,15,30]{2,1,0:T(8,128)(2,1)S(1)} %copy.71) | data formatting | bytes 230400
  12.2 3.2 %all-to-all-done.1 = bf16[4,2,7200]{2,1,0:T(2,128)(2,1)S(1)} async-done(((bf16[4,2,7200]{2,1,0:T(2,128)(2,1)}), bf16[4,2,7200]{2,1,0:T(2,128)(2,1)S(1)}, u32[]{:S(2)}, u32[]{:S(2)}) %all-to-all-start.1) | async-done | bytes 115232 | tf_op jit(solution)/shard_map/all_to_all | solution.py:45
  15.4 3.3 %all-to-all-start = ((bf16[4,2,7200]{2,1,0:T(2,128)(2,1)}), bf16[4,2,7200]{2,1,0:T(2,128)(2,1)S(1)}, u32[]{:S(2)}, u32[]{:S(2)}) async-start(bf16[4,2,7200]{2,1,0:T(2,128)(2,1)} %reshape.97), calls=%async_computation | async-start | bytes 233472 | tf_op jit(solution)/shard_map/all_to_all | solution.py:44
  20.0 17.0 %all_gather.10 = bf16[32,120,120]{2,0,1:T(8,128)(2,1)S(1)} all-gather(bf16[32,15,120]{2,0,1:T(8,128)(2,1)S(1)} %all_to_all.67), channel_id=1, replica_groups=mesh['dap'=8,'ch'=4] {'dap'}, dimensions={1}, use_global_device_ids=true | all-gather | bytes 1036800 | tf_op jit(solution)/shard_map/all_gather | solution.py:50
  39.7 8.9 %all_to_all.81 = bf16[4,2,7200]{2,1,0:T(2,128)(2,1)S(1)} all-to-all(bf16[4,2,7200]{2,1,0:T(2,128)(2,1)S(1)} %reshape.99), channel_id=1, replica_groups=mesh['dap'=8,'ch'=4] {'ch'}, dimensions={0} | all-to-all | bytes 230400 | tf_op jit(solution)/shard_map/all_to_all | solution.py:53
  49.2 1.0 copy.78
  50.2 1.3 %reshape.89 = f32[32,15,4,30]{3,2,0,1:T(4,128)S(1)} reshape(bf16[32,15,120]{2,0,1:T(8,128)(2,1)} %copy.78) | data formatting | bytes 345600 | tf_op jit(solution)/shard_map/convert_element_type | solution.py:54
  51.7 1.7 %copy.79 = f32[4,32,15,30]{1,0,3,2:T(4,128)} copy(f32[4,32,15,30]{3,0,1,2:T(4,128)S(1)} %bitcast.66) | data formatting | bytes 460800 | tf_op jit(solution)/shard_map/convert_element_type | solution.py:54
  53.5 1.6 %reshape.85 = f32[128,15,30]{0,2,1:T(8,128)S(1)} reshape(f32[4,32,15,30]{1,0,3,2:T(4,128)} %copy.79) | data formatting | bytes 460800 | tf_op jit(solution)/shard_map/convert_element_type | solution.py:54
  59.1 1.3 %reshape.101 = bf16[4,2,7200]{2,1,0:T(2,128)(2,1)} reshape(bf16[128,15,30]{2,1,0:T(8,128)(2,1)S(1)} %copy.80) | data formatting | bytes 230400
  60.4 3.4 %all-to-all-start.3 = ((bf16[4,2,7200]{2,1,0:T(2,128)(2,1)}), bf16[4,2,7200]{2,1,0:T(2,128)(2,1)S(1)}, u32[]{:S(2)}, u32[]{:S(2)}) async-start(bf16[4,2,7200]{2,1,0:T(2,128)(2,1)} %reshape.101), calls=%async_computation.3 | async-start | bytes 233472 | tf_op jit(solution)/shard_map/all_to_all | solution.py:65
  63.8 16.8 %all_gather.12 = bf16[32,120,120]{2,0,1:T(8,128)(2,1)} all-gather(bf16[32,15,120]{2,0,1:T(8,128)(2,1)S(1)} %copy-done.3), channel_id=1, replica_groups=mesh['dap'=8,'ch'=4] {'dap'}, dimensions={1}, use_global_device_ids=true | all-gather | bytes 1036800 | tf_op jit(solution)/shard_map/all_gather | solution.py:66
  82.4 16.5 %all_gather.11 = bf16[32,120,120]{2,0,1:T(8,128)(2,1)S(1)} all-gather(bf16[32,15,120]{2,0,1:T(8,128)(2,1)S(1)} %all_to_all.72), channel_id=1, replica_groups=mesh['dap'=8,'ch'=4] {'dap'}, dimensions={1}, use_global_device_ids=true | all-gather | bytes 1036800 | tf_op jit(solution)/shard_map/all_gather | solution.py:68
  99.4 1.1 reshape.105
  100.5 4.2 %all-to-all-start.4 = ((bf16[4,2,7200]{2,1,0:T(2,128)(2,1)}), bf16[4,2,7200]{2,1,0:T(2,128)(2,1)S(1)}, u32[]{:S(2)}, u32[]{:S(2)}) async-start(bf16[4,2,7200]{2,1,0:T(2,128)(2,1)} %reshape.105), calls=%async_computation.4 | async-start | bytes 233472 | tf_op jit(solution)/shard_map/all_to_all | solution.py:77
  107.0 1.1 reshape.103
  108.1 1.5 %all-to-all-done.4 = bf16[4,2,7200]{2,1,0:T(2,128)(2,1)S(1)} async-done(((bf16[4,2,7200]{2,1,0:T(2,128)(2,1)}), bf16[4,2,7200]{2,1,0:T(2,128)(2,1)S(1)}, u32[]{:S(2)}, u32[]{:S(2)}) %all-to-all-start.4) | async-done | bytes 115232 | tf_op jit(solution)/shard_map/all_to_all | solution.py:77
  109.7 3.5 %all-to-all-start.5 = ((bf16[4,2,7200]{2,1,0:T(2,128)(2,1)}), bf16[4,2,7200]{2,1,0:T(2,128)(2,1)S(1)}, u32[]{:S(2)}, u32[]{:S(2)}) async-start(bf16[4,2,7200]{2,1,0:T(2,128)(2,1)} %reshape.103), calls=%async_computation.5 | async-start | bytes 233472 | tf_op jit(solution)/shard_map/all_to_all | solution.py:80
  114.5 1.5 %copy.86 = f32[4,32,15,30]{1,0,3,2:T(4,128)S(1)} copy(f32[4,32,15,30]{3,0,1,2:T(4,128)S(1)} %bitcast.67) | data formatting | bytes 460800 | tf_op jit(solution)/shard_map/convert_element_type | solution.py:84
  116.5 1.5 %all-to-all-done.5 = bf16[4,2,7200]{2,1,0:T(2,128)(2,1)S(1)} async-done(((bf16[4,2,7200]{2,1,0:T(2,128)(2,1)}), bf16[4,2,7200]{2,1,0:T(2,128)(2,1)S(1)}, u32[]{:S(2)}, u32[]{:S(2)}) %all-to-all-start.5) | async-done | bytes 115232 | tf_op jit(solution)/shard_map/all_to_all | solution.py:80
  119.3 1.5 %copy.91 = f32[4,32,15,30]{1,0,3,2:T(4,128)S(1)} copy(f32[4,32,15,30]{3,0,1,2:T(4,128)S(1)} %bitcast.68) | data formatting | bytes 460800 | tf_op jit(solution)/shard_map/convert_element_type | solution.py:85
  (83 shorter events, 21.9 us)
Async XLA Ops:
  0.6 2.2 %copy-start = (bf16[128,512]{1,0:T(8,128)(2,1)S(1)}, bf16[128,512]{1,0:T(8,128)(2,1)}, u32[]{:S(2)}) copy-start(bf16[128,512]{1,0:T(8,128)(2,1)} %param.8) | copy-start | bytes 393220
  0.6 1.1 copy-start.1
  2.0 0.7 copy-start.13
  5.2 10.2 %all-to-all-start.1 = ((bf16[4,2,7200]{2,1,0:T(2,128)(2,1)}), bf16[4,2,7200]{2,1,0:T(2,128)(2,1)S(1)}, u32[]{:S(2)}, u32[]{:S(2)}) async-start(bf16[4,2,7200]{2,1,0:T(2,128)(2,1)} %reshape.95), calls=%async_computation.1 | async-start | bytes 233472 | tf_op jit(solution)/shard_map/all_to_all | solution.py:45
  15.4 21.6 %all-to-all-start = ((bf16[4,2,7200]{2,1,0:T(2,128)(2,1)}), bf16[4,2,7200]{2,1,0:T(2,128)(2,1)S(1)}, u32[]{:S(2)}, u32[]{:S(2)}) async-start(bf16[4,2,7200]{2,1,0:T(2,128)(2,1)} %reshape.97), calls=%async_computation | async-start | bytes 233472 | tf_op jit(solution)/shard_map/all_to_all | solution.py:44
  38.2 0.6 copy-start.2
  55.1 0.8 copy-start.11
  55.8 0.8 copy-start.12
  56.6 1.0 copy-start.6
  56.6 1.0 copy-start.9
  57.6 0.7 copy-start.4
  60.4 3.5 %copy-start.3 = (bf16[32,15,120]{2,0,1:T(8,128)(2,1)S(1)}, bf16[32,15,120]{2,0,1:T(8,128)(2,1)}, u32[]{:S(2)}) copy-start(bf16[32,15,120]{2,0,1:T(8,128)(2,1)} %copy-done.2) | copy-start | bytes 345604
  60.4 20.2 %all-to-all-start.3 = ((bf16[4,2,7200]{2,1,0:T(2,128)(2,1)}), bf16[4,2,7200]{2,1,0:T(2,128)(2,1)S(1)}, u32[]{:S(2)}, u32[]{:S(2)}) async-start(bf16[4,2,7200]{2,1,0:T(2,128)(2,1)} %reshape.101), calls=%async_computation.3 | async-start | bytes 233472 | tf_op jit(solution)/shard_map/all_to_all | solution.py:65
  100.5 9.2 %all-to-all-start.4 = ((bf16[4,2,7200]{2,1,0:T(2,128)(2,1)}), bf16[4,2,7200]{2,1,0:T(2,128)(2,1)S(1)}, u32[]{:S(2)}, u32[]{:S(2)}) async-start(bf16[4,2,7200]{2,1,0:T(2,128)(2,1)} %reshape.105), calls=%async_computation.4 | async-start | bytes 233472 | tf_op jit(solution)/shard_map/all_to_all | solution.py:77
  104.7 1.2 copy-start.8
  109.7 8.3 %all-to-all-start.5 = ((bf16[4,2,7200]{2,1,0:T(2,128)(2,1)}), bf16[4,2,7200]{2,1,0:T(2,128)(2,1)S(1)}, u32[]{:S(2)}, u32[]{:S(2)}) async-start(bf16[4,2,7200]{2,1,0:T(2,128)(2,1)} %reshape.103), calls=%async_computation.5 | async-start | bytes 233472 | tf_op jit(solution)/shard_map/all_to_all | solution.py:80
  121.5 0.9 copy-start.5
  121.5 1.1 copy-start.7
  121.5 1.1 copy-start.10
where the time goes:
time: 125 us; the launch traced here: 124 us
  blocking collectives  59.2 us (47%)
  local copies, waits for them, and re-layouts  29.6 us (24%)
  starting transfers between devices  19.7 us (16%)
  waiting for transfers between devices  6.2 us (5%)
  matrix products  4.56 us (4%)
  other arithmetic  3.66 us (3%)
    all_gather x1, blocking collectives, on_device(): lax.all_gather(right_rows, 'dap', axis=1, tiled=True)  17 us
    all_gather x1, blocking collectives, on_device(): piece_left = lax.all_gather(left_rows, 'dap', axis=1, tiled=True)  16.8 us
    all_gather x1, blocking collectives, on_device(): piece_grad = lax.all_gather(grad_rows, 'dap', axis=1, tiled=True)  16.5 us
    unnamed x40, local copies, waits for them, and re-layouts  13.1 us
    all_to_all x1, blocking collectives, on_device(): lax.all_to_all(product, 'ch', split_axis=2, concat_axis=0, tiled=True)  8.94 us
    all_to_all x1, starting transfers between devices, on_device(): lax.all_to_all(right_cells, 'ch', split_axis=0, concat_axis=2, tiled=True)  5.19 us
    convert_element_type x3, local copies, waits for them, and re-layouts, on_device(): hidden_norm, hidden_scale = normalize(product_cells.astype(jnp.float32), 0)  4.68 us
    all_to_all x1, starting transfers between devices, on_device(): lax.all_to_all(new_left.astype(jnp.bfloat16), 'ch', split_axis=2, concat_...  4.21 us
  transfers between devices with their start and end apart: 5, of which 3 were waited for; matrix products, arithmetic and copies ran while one was open for 7% of the time, Pallas kernels for 0%

commit v1 on v0

v1 whole, which is shorter than its diff:
```python
import functools

import jax
import jax.numpy as jnp
from jax import lax
from jax.experimental import pallas as pl
from jax.experimental.pallas import tpu as pltpu
from jax.sharding import PartitionSpec as P

EPSILON = 1e-05
F32 = jnp.float32
BF16 = jnp.bfloat16
EARLY = 2
JB = 5


def pad_to(count, tile):
    return (count + tile - 1) // tile * tile


def normalize(values):
    center = jnp.mean(values, axis=-1, keepdims=True)
    spread = values - center
    scale = lax.rsqrt(jnp.mean(spread * spread, axis=-1, keepdims=True) + EPSILON)
    return spread * scale, scale


def norm_back(grad, normed, scale):
    first = jnp.mean(grad, axis=-1, keepdims=True)
    second = jnp.mean(grad * normed, axis=-1, keepdims=True)
    return scale * (grad - first - normed * second)


def matmul(a, b):
    return lax.dot_general(a, b, (((1,), (0,)), ((), ())), preferred_element_type=F32)


def matmul_t(a, b):
    return lax.dot_general(a, b, (((1,), (1,)), ((), ())), preferred_element_type=F32)


def col_mask(mask_ref, start, count, pitch, channels):
    row = lax.broadcasted_iota(jnp.int32, (pitch, channels), 0)
    flags = jnp.zeros((pitch, channels), F32)
    for k in range(count):
        flags = jnp.where(row == k, mask_ref[start + k].astype(F32), flags)
    return flags


def load_cells(cells_ref, scratch, first):
    rows, cols, channels = cells_ref.shape
    pitch = pad_to(cols, 16)
    for i in range(rows):
        at = (first + i) * pitch
        scratch[at : at + cols, :] = cells_ref[i].astype(F32)
        if pitch > cols:
            scratch[at + cols : at + pitch, :] = jnp.zeros((pitch - cols, channels), F32)


def row_of(ref, row):
    return ref[pl.ds(row, 8, stride=0), :]


def tiles(value):
    return value.reshape(value.shape[0] // 8, 8, value.shape[1])


def right_kernel(mask_ref, x_ref, w_ref, out_ref, xs):
    rows, cols, channels = x_ref.shape
    pitch = pad_to(cols, 16)
    hidden = w_ref.shape[1] // 2
    load_cells(x_ref, xs, 0)
    normed, _ = normalize(xs[...])
    projected = matmul(normed.astype(BF16), w_ref[...])
    right = jax.nn.sigmoid(projected[:, :hidden]) * projected[:, hidden:]
    flags = col_mask(mask_ref, lax.axis_index("ch") * cols, cols, pitch, hidden)
    start = lax.axis_index("dap") * rows
    for i in range(rows):
        block = slice(i * pitch, (i + 1) * pitch)
        live = flags * mask_ref[start + i].astype(F32)
        out_ref[block, :] = (right[block] * live).astype(BF16)


def left_kernel(mask_ref, x_ref, xp_ref, cot_ref, cotp_ref, w_ref, wg_ref,
                l_ref, lt_ref, gate_ref, cotm_ref, xs, ls, gs):
    rows, cols, channels = x_ref.shape
    pitch = pad_to(cols, 16)
    half = pad_to(rows, 16)
    hidden = w_ref.shape[1] // 2
    dap = lax.axis_index("dap")
    core = lax.rem(dap, 2)
    load_cells(x_ref, xs, 0)
    load_cells(xp_ref, xs, rows)
    normed, _ = normalize(xs[...])
    normed_half = normed.astype(BF16)
    projected = matmul(normed_half, w_ref[...])
    left = jax.nn.sigmoid(projected[:, :hidden]) * projected[:, hidden:]
    flags = col_mask(mask_ref, lax.axis_index("ch") * cols, cols, pitch, hidden)
    for i in range(2 * rows):
        owner = dap if i < rows else dap + 1 - 2 * core
        block = slice(i * pitch, (i + 1) * pitch)
        live = flags * mask_ref[owner * rows + i % rows].astype(F32)
        value = (left[block] * live).astype(BF16).astype(F32)
        l_ref[block, :] = value
        ls[block, :] = value
    tall = pad_to(2 * rows, 16)
    ls[2 * rows * pitch :, :] = jnp.zeros(((tall - 2 * rows) * pitch, hidden), F32)
    for k in range(cols):
        lt_ref[k * tall : (k + 1) * tall, :] = ls[pl.ds(k, tall, stride=pitch), :]
    gs[...] = jax.nn.sigmoid(matmul(normed_half, wg_ref[...]))

    def pick(out_ref):
        for i in range(2 * rows):
            low = gs[i * pitch : i * pitch + rows, :]
            high = gs[i * pitch + rows : i * pitch + 2 * rows, :]
            out_ref[i * half : i * half + rows, :] = jnp.where(core == 0, low, high)
            if half > rows:
                out_ref[i * half + rows : (i + 1) * half, :] = jnp.zeros((half - rows, channels), F32)

    pick(gate_ref)
    load_cells(cot_ref, gs, 0)
    load_cells(cotp_ref, gs, rows)
    pick(cotm_ref)


def factor_kernel(mask_ref, x_ref, w_ref, normed_ref, scale_ref, l1_ref, l2_ref, r1_ref, r2_ref, xs):
    rows, cols, channels = x_ref.shape
    pitch = pad_to(cols, 16)
    hidden = w_ref.shape[1] // 4
    load_cells(x_ref, xs, 0)
    normed, scale = normalize(xs[...])
    normed_ref[...] = normed
    scale_ref[...] = jnp.broadcast_to(scale, normed.shape)
    projected = matmul(normed.astype(BF16), w_ref[...])
    left_sig = jax.nn.sigmoid(projected[:, :hidden])
    right_sig = jax.nn.sigmoid(projected[:, 2 * hidden : 3 * hidden])
    left_in = projected[:, hidden : 2 * hidden] * left_sig * (1.0 - left_sig)
    right_in = projected[:, 3 * hidden :] * right_sig * (1.0 - right_sig)
    flags = col_mask(mask_ref, lax.axis_index("ch") * cols, cols, pitch, hidden)
    start = lax.axis_index("dap") * rows
    for i in range(rows):
        block = slice(i * pitch, (i + 1) * pitch)
        live = flags * mask_ref[start + i].astype(F32)
        l1_ref[block, :] = left_in[block] * live
        l2_ref[block, :] = left_sig[block] * live
        r1_ref[block, :] = right_in[block] * live
        r2_ref[block, :] = right_sig[block] * live


def product_part(lt_ref, r_ref, rs, out, rows, cols):
    pitch, half, tall = pad_to(cols, 16), pad_to(rows, 16), pad_to(2 * rows, 16)
    rs[...] = r_ref[...].astype(F32)

    def step(b, _):
        sums = [jnp.zeros((tall // 8, 8, rs.shape[1]), F32) for _ in range(JB)]
        for k in range(cols):
            left = tiles(lt_ref[k * tall : (k + 1) * tall, :])
            for n in range(JB):
                sums[n] = sums[n] + left * row_of(rs, (b * JB + n) * pitch + k)[None]
        for n in range(JB):
            out[pl.ds(b * JB + n, tall, stride=half), :] = sums[n].reshape(tall, rs.shape[1])
        return 0

    lax.fori_loop(0, rows // JB, step, 0)


def early_kernel(rows, cols, count, *refs):
    lt_ref, shards = refs[0], refs[1 : 1 + count]
    out_ref, rs = refs[1 + count :]
    for s in range(count):
        product_part(lt_ref, shards[s], rs, out_ref.at[s], rows, cols)


def late_kernel(rows, cols, blocks, early, *refs):
    lt_ref, early_ref = refs[:2]
    shards = refs[2 : 2 + blocks - early]
    outs = refs[2 + blocks - early : 2 + 2 * blocks - early]
    rs, ps = refs[2 + 2 * blocks - early :]
    chip, column = lax.axis_index("dap") // 2, lax.axis_index("ch")
    used = 2 * rows * pad_to(rows, 16)
    for s in range(early):
        ps[chip ^ s] = early_ref[s]
    for s in range(early, blocks):
        product_part(lt_ref, shards[s - early], rs, ps.at[chip ^ s], rows, cols)
    for t in range(blocks):
        outs[t][...] = ps[column ^ t, :used, :].astype(outs[t].dtype)


def middle_kernel(blocks, *refs):
    parts = refs[:blocks]
    gate_ref, cot_ref, w_ref, upd_ref, back_ref, logit_ref, gp_ref = refs[blocks:]
    total = parts[0][...]
    for t in range(1, blocks):
        total = total + parts[t][...].astype(F32)
    product = total.astype(BF16).astype(F32)
    hidden_norm, hidden_scale = normalize(product)
    out = matmul(hidden_norm.astype(BF16), w_ref[...])
    gate, upstream = gate_ref[...], cot_ref[...]
    grad_out = (upstream * gate).astype(BF16)
    grad_hidden = matmul_t(grad_out, w_ref[...])
    gp_ref[...] = norm_back(grad_hidden, hidden_norm, hidden_scale).astype(BF16)
    update = (gate * out).astype(BF16)
    logit = (upstream * out * gate * (1.0 - gate)).astype(BF16)
    own = upd_ref.shape[0]
    upd_ref[...] = update[:own]
    logit_ref[...] = logit[:own]
    back_ref[:own, :] = update[own:]
    back_ref[own:, :] = logit[own:]


def grad_right_part(l_ref, gs, block, store, rows, cols):
    pitch, half = pad_to(cols, 16), pad_to(rows, 16)
    piece = gs.at[block]

    def step(b, _):
        sums = [jnp.zeros((pitch // 8, 8, gs.shape[2]), F32) for _ in range(JB)]
        for i in range(2 * rows):
            left = tiles(l_ref[i * pitch : (i + 1) * pitch, :])
            for n in range(JB):
                sums[n] = sums[n] + left * row_of(piece, i * half + b * JB + n)[None]
        for n in range(JB):
            at = pl.multiple_of((b * JB + n) * pitch, pitch)
            store(pl.ds(at, pitch), sums[n].reshape(pitch, gs.shape[2]))
        return 0

    lax.fori_loop(0, rows // JB, step, 0)


def stage_pieces(pieces, gs):
    column = lax.axis_index("ch")
    for t, piece in enumerate(pieces):
        gs[column ^ t] = piece[...].astype(F32)


def send_right_kernel(rows, cols, blocks, *refs):
    l_ref, pieces = refs[0], refs[1 : 1 + blocks]
    outs, gs = refs[1 + blocks : 2 * blocks], refs[2 * blocks]
    chip = lax.axis_index("dap") // 2
    stage_pieces(pieces, gs)
    for s in range(1, blocks):
        def store(where, value, s=s):
            outs[s - 1][where, :] = value.astype(BF16)
        grad_right_part(l_ref, gs, chip ^ s, store, rows, cols)


def grad_left_kernel(rows, cols, blocks, *refs):
    l_ref, pieces, shards = refs[0], refs[1 : 1 + blocks], refs[1 + blocks : 1 + 2 * blocks]
    own_ref, send_ref, right_ref, gs, rs = refs[1 + 2 * blocks :]
    pitch, half = pad_to(cols, 16), pad_to(rows, 16)
    chip = lax.axis_index("dap") // 2
    stage_pieces(pieces, gs)
    for s in range(blocks):
        rs[chip ^ s] = shards[s][...].astype(F32)

    def left_rows(first, ref):
        def step(b, _):
            def block_step(m, sums):
                piece, shard = gs.at[m], rs.at[m]
                sums = list(sums)
                for j in range(rows):
                    right = tiles(shard[j * pitch : (j + 1) * pitch, :])
                    for n in range(JB):
                        row = (first + b * JB + n) * half + j
                        sums[n] = sums[n] + right * row_of(piece, row)[None]
                return tuple(sums)

            zero = jnp.zeros((pitch // 8, 8, gs.shape[2]), F32)
            sums = lax.fori_loop(0, blocks, block_step, (zero,) * JB)
            for n in range(JB):
                at = pl.multiple_of((b * JB + n) * pitch, pitch)
                ref[pl.ds(at, pitch), :] = sums[n].reshape(pitch, gs.shape[2]).astype(ref.dtype)
            return 0

        lax.fori_loop(0, rows // JB, step, 0)

    left_rows(rows, send_ref)
    left_rows(0, own_ref)

    def store(where, value):
        right_ref[where, :] = value

    grad_right_part(l_ref, gs, chip, store, rows, cols)


def finish_left_kernel(own_ref, got_ref, l1_ref, l2_ref, w_ref, wg_ref, upd_ref, logit_ref, back_ref,
                       out_ref, acc_ref, us, gs):
    rows, cols, channels = out_ref.shape
    pitch, half = pad_to(cols, 16), pad_to(rows, 16)
    mine = lax.rem(lax.axis_index("dap"), 2) == 0
    for i in range(rows):
        for scratch, ref, base in ((us, upd_ref, 0), (gs, logit_ref, rows * half)):
            here = ref[i * half : (i + 1) * half, :].astype(F32)[:rows]
            there = back_ref[base + i * half : base + (i + 1) * half, :].astype(F32)[:rows]
            scratch[i * pitch : i * pitch + rows, :] = jnp.where(mine, here, there)
            scratch[i * pitch + rows : i * pitch + 2 * rows, :] = jnp.where(mine, there, here)
            if pitch > cols:
                scratch[i * pitch + cols : (i + 1) * pitch, :] = jnp.zeros((pitch - cols, channels), F32)
        out_ref[i] = us[i * pitch : i * pitch + cols, :].astype(BF16)
    grad_left = (own_ref[...] + got_ref[...].astype(F32)).astype(BF16).astype(F32)
    hidden = own_ref.shape[1]
    acc = matmul_t((grad_left * l1_ref[...]).astype(BF16), w_ref[:, :hidden])
    acc = acc + matmul_t((grad_left * l2_ref[...]).astype(BF16), w_ref[:, hidden:])
    acc_ref[...] = acc + matmul_t(gs[...].astype(BF16), wg_ref[...])


def finish_kernel(blocks, *refs):
    parts = refs[:blocks]
    r1_ref, r2_ref, w_ref, acc_ref, normed_ref, scale_ref, out_ref = refs[blocks:]
    rows, cols, _ = out_ref.shape
    pitch = pad_to(cols, 16)
    total = parts[0][...]
    for s in range(1, blocks):
        total = total + parts[s][...].astype(F32)
    grad_right = total.astype(BF16).astype(F32)
    hidden = total.shape[1]
    grad = acc_ref[...] + matmul_t((grad_right * r1_ref[...]).astype(BF16), w_ref[:, :hidden])
    grad = grad + matmul_t((grad_right * r2_ref[...]).astype(BF16), w_ref[:, hidden:])
    result = norm_back(grad, normed_ref[...], scale_ref[...]).astype(BF16)
    for i in range(rows):
        out_ref[i] = result[i * pitch : i * pitch + cols]


VMEM = pl.BlockSpec(memory_space=pltpu.VMEM)
SMEM = pl.BlockSpec(memory_space=pltpu.SMEM)


def call(body, name, outs, args, scratch=(), smem=0, flops=10**7):
    outs = [jax.ShapeDtypeStruct(shape, dtype) for shape, dtype in outs]
    moved = sum(a.size * a.dtype.itemsize for a in list(args) + outs)
    return pl.pallas_call(
        body,
        name=name,
        out_shape=outs,
        in_specs=[SMEM] * smem + [VMEM] * (len(args) - smem),
        out_specs=[VMEM] * len(outs),
        scratch_shapes=[pltpu.VMEM(shape, F32) for shape in scratch],
        compiler_params=pltpu.CompilerParams(vmem_limit_bytes=60 << 20),
        cost_estimate=pl.CostEstimate(flops=flops, bytes_accessed=moved, transcendentals=0),
    )(*args)


def on_device(devices, blocks, x, mask, w_proj, w_gate, w_out, cot):
    rows, cols, channels = x.shape
    hidden = w_out.shape[0]
    pitch, half, tall = pad_to(cols, 16), pad_to(rows, 16), pad_to(2 * rows, 16)
    cells, wide, mids = rows * pitch, 2 * rows * pitch, 2 * rows * half
    if devices != 2 * blocks or cols != 2 * rows or blocks & (blocks - 1) or rows % JB:
        raise ValueError("unsupported split")
    w_left, w_right = w_proj[:, : 2 * hidden], w_proj[:, 2 * hidden :]

    def along_dap(value, s):
        return lax.ppermute(value, "dap", [(d, d ^ (2 * s)) for d in range(devices)])

    def along_ch(value, t):
        return lax.ppermute(value, "ch", [(h, h ^ t) for h in range(blocks)])

    def to_partner(value):
        return lax.ppermute(value, "dap", [(d, d ^ 1) for d in range(devices)])

    (right,) = call(right_kernel, "right", [((cells, hidden), BF16)], (mask, x, w_right),
                    [(cells, channels)], smem=1)
    shards = [right] + [along_dap(right, s) for s in range(1, blocks)]
    x_late, cot_late, _ = lax.optimization_barrier((x, cot, right))
    x_pair, cot_pair = to_partner(x_late), to_partner(cot_late)
    left, left_t, gate, upstream = call(
        left_kernel, "left",
        [((wide, hidden), F32), ((cols * tall, hidden), F32), ((mids, channels), F32), ((mids, channels), F32)],
        (mask, x_late, x_pair, cot_late, cot_pair, w_left, w_gate),
        [(wide, channels), (tall * pitch, hidden), (wide, channels)], smem=1)
    normed, scale, l1, l2, r1, r2 = call(
        factor_kernel, "factor", [((cells, hidden), F32)] * 6, (mask, x_late, w_proj),
        [(cells, channels)], smem=1)
    early = min(EARLY, blocks)
    (started,) = call(functools.partial(early_kernel, rows, cols, early), "early",
                      [((early, tall * half, hidden), F32)], (left_t, *shards[:early]), [(cells, hidden)])
    parts = call(functools.partial(late_kernel, rows, cols, blocks, early), "late",
                 [((mids, hidden), F32)] + [((mids, hidden), BF16)] * (blocks - 1),
                 (left_t, started, *shards[early:]),
                 [(cells, hidden), (blocks, tall * half, hidden)])
    parts = [parts[0]] + [along_ch(parts[t], t) for t in range(1, blocks)]
    update, back, logit, grad_product = call(
        functools.partial(middle_kernel, blocks), "middle",
        [((mids // 2, channels), BF16), ((mids, channels), BF16), ((mids // 2, channels), BF16), ((mids, hidden), BF16)],
        (*parts, gate, upstream, w_out))
    pieces = [grad_product] + [along_ch(grad_product, t) for t in range(1, blocks)]
    back = to_partner(back)
    sends = call(functools.partial(send_right_kernel, rows, cols, blocks), "send_right",
                 [((cells, hidden), BF16)] * (blocks - 1), (left, *pieces), [(blocks, mids, hidden)])
    gots = [along_dap(sends[s - 1], s) for s in range(1, blocks)]
    left_own, left_send, right_own = call(
        functools.partial(grad_left_kernel, rows, cols, blocks), "grad_left",
        [((cells, hidden), F32), ((cells, hidden), BF16), ((cells, hidden), F32)],
        (left, *pieces, *shards), [(blocks, mids, hidden), (blocks, cells, hidden)])
    left_got = to_partner(left_send)
    pair_update, acc = call(
        finish_left_kernel, "finish_left", [((rows, cols, channels), BF16), ((cells, channels), F32)],
        (left_own, left_got, l1, l2, w_left, w_gate, update, logit, back),
        [(cells, channels), (cells, channels)])
    (grad_pair,) = call(functools.partial(finish_kernel, blocks), "finish", [((rows, cols, channels), BF16)],
                        (right_own, *gots, r1, r2, w_right, acc, normed, scale))
    return pair_update, grad_pair


def solution(mesh):
    return jax.shard_map(
        functools.partial(on_device, mesh.shape["dap"], mesh.shape["ch"]),
        mesh=mesh,
        in_specs=(P("dap", "ch", None), P(), P(), P(), P(), P("dap", "ch", None)),
        out_specs=(P("dap", "ch", None), P("dap", "ch", None)),
        check_vma=False,
    )
```

time: 125 us -> 72 us (0.58)
  blocking collectives: 59.2 us -> 0 us
  Pallas kernels: 0 us -> 30.2 us
  local copies, waits for them, and re-layouts: 29.6 us -> 6.22 us
  waiting for transfers between devices: 6.2 us -> 17 us
  matrix products: 4.56 us -> 0 us
  other arithmetic: 3.66 us -> 0 us
  starting transfers between devices: 19.7 us -> 17.5 us
    all_gather x3 -> x0, blocking collectives: 50.3 us -> none  [the longest x1 17 us: on_device(): lax.all_gather(right_rows, 'dap', axis=1, tiled=True)]
    pallas_call x0 -> x10, Pallas kernels: none -> 30.2 us  [call(): pl.pallas_call(body, name=name, out_shape=outs, in_specs=[SMEM] * smem +...]
    all_to_all x5 -> x0, starting transfers between devices: 19.7 us -> none  [the longest x1 5.19 us: on_device(): lax.all_to_all(right_cells, 'ch', split_axis=0, concat_axis=2, tiled=True)]
    ppermute x0 -> x16, starting transfers between devices: none -> 17.5 us  [the longest x6 10 us: along_dap(): return lax.ppermute(value, 'dap', [(d, d ^ 2 * s) for d in range(devices)])]
    ppermute x0 -> x16, waiting for transfers between devices: none -> 17 us  [the longest x6 9.54 us: along_ch(): return lax.ppermute(value, 'ch', [(h, h ^ t) for h in range(blocks)])]
    convert_element_type x15 -> x0, local copies, waits for them, and re-layouts: 12.1 us -> none  [the longest x3 4.68 us: on_device(): hidden_norm, hidden_scale = normalize(product_cells.astype(jnp.float32), 0)]
    all_to_all x1 -> x0, blocking collectives: 8.94 us -> none  [on_device(): lax.all_to_all(product, 'ch', split_axis=2, concat_axis=0, tiled=True)]
    unnamed x40 -> x36, local copies, waits for them, and re-layouts: 13.1 us -> 4.69 us
  transfers between devices with their start and end apart: 5 -> 16, of which waited for: 3 -> 8; matrix products, arithmetic and copies ran while one was open for 7% -> 0% of each run, Pallas kernels for 0% -> 28%
where the time goes in v1:
time: 72 us; the launch traced here: 71.6 us
  Pallas kernels  30.2 us (42%)
  starting transfers between devices  17.5 us (24%)
  waiting for transfers between devices  17 us (24%)
  local copies, waits for them, and re-layouts  6.22 us (9%)
    pallas_call x10, Pallas kernels, call(): pl.pallas_call(body, name=name, out_shape=outs, in_specs=[SMEM] * smem +...  30.2 us
    ppermute x6, starting transfers between devices, along_dap(): return lax.ppermute(value, 'dap', [(d, d ^ 2 * s) for d in range(devices)])  10 us
    ppermute x6, waiting for transfers between devices, along_ch(): return lax.ppermute(value, 'ch', [(h, h ^ t) for h in range(blocks)])  9.54 us
    ppermute x6, starting transfers between devices, along_ch(): return lax.ppermute(value, 'ch', [(h, h ^ t) for h in range(blocks)])  6.98 us
    ppermute x6, waiting for transfers between devices, along_dap(): return lax.ppermute(value, 'dap', [(d, d ^ 2 * s) for d in range(devices)])  6.48 us
    unnamed x36, local copies, waits for them, and re-layouts  4.69 us
    slice x1, local copies, waits for them, and re-layouts, on_device(): w_left, w_right = (w_proj[:, :2 * hidden], w_proj[:, 2 * hidden:])  1.53 us
  transfers between devices with their start and end apart: 16, of which 8 were waited for; matrix products, arithmetic and copies ran while one was open for 0% of the time, Pallas kernels for 28%

profile of v1, /device:TPU:0, one launch (start us, length us, event | category | flops | bytes accessed | tf_op | source)
XLA Modules:
  0.0 71.6 jit_solution(9887082323388541421)
XLA Ops:
  0.6 1.5 %fusion = (bf16[128,256]{1,0:T(8,128)(2,1)}, bf16[128,256]{1,0:T(8,128)(2,1)}) fusion(bf16[128,512]{1,0:T(8,128)(2,1)} %w_ref.1), kind=kLoop, calls=%fused_computation | loop fusion | bytes 262144 | tf_op jit(solution)/shard_map/slice | solution.py:349
  2.2 2.0 %right.1.refs_1_.refs_5_ = bf16[480,128]{1,0:T(8,128)(2,1)} custom-call(s32[120]{0:T(128)} %mask_ref.5, bf16[15,30,128]{2,1,0:T(8,128)(2,1)} %x_ref.3, bf16[128,256]{1,0:T(8,128)(2,1)} %get-tuple-element.59.w_ref.refs_6_), custom_call_target="tpu_custom_call" | custom-call | flops 10000000 | bytes 304096 | tf_op jit(solution)/shard_map/right/pallas_call | solution.py:330
  4.2 3.1 %collective-permute-start.2 = (bf16[480,128]{1,0:T(8,128)(2,1)}, bf16[480,128]{1,0:T(8,128)(2,1)S(1)}, u32[]{:S(2)}, u32[]{:S(2)}) collective-permute-start(bf16[480,128]{1,0:T(8,128)(2,1)} %right.1.refs_1_.refs_5_), channel_id=1, source_target_pairs={{0,8},{4,12},{8,0},{12,4},{16,24},{20,28},{24,16},{28,20},{1,9},{5... | collective-permute-start | bytes 368648 | tf_op jit(solution)/shard_map/ppermute | solution.py:352
  7.2 2.5 %collective-permute-start.4 = (bf16[480,128]{1,0:T(8,128)(2,1)}, bf16[480,128]{1,0:T(8,128)(2,1)S(1)}, u32[]{:S(2)}, u32[]{:S(2)}) collective-permute-start(bf16[480,128]{1,0:T(8,128)(2,1)} %right.1.refs_1_.refs_5_), channel_id=1, source_target_pairs={{0,24},{4,28},{8,16},{12,20},{16,8},{20,12},{24,0},{28,4},{1,25},{... | collective-permute-start | bytes 368648 | tf_op jit(solution)/shard_map/ppermute | solution.py:352
  12.0 3.2 %left.1 = (f32[960,128]{1,0:T(8,128)}, f32[960,128]{1,0:T(8,128)}, f32[480,128]{1,0:T(8,128)}, f32[480,128]{1,0:T(8,128)}) custom-call(s32[120]{0:T(128)} %mask_ref.5, bf16[15,30,128]{2,1,0:T(8,128)(2,1)} %x_ref.3, bf16[15,30,128]{2,1,0:T(8,128)(2,1)} %copy-done.17, bf16[15,30,128]{2,1,0:T(8,128)(2,1)} %cot_ref, bf16[15,30,128]{2,1,0:T(8,128)(2,1)} %copy-done.16, ...), custom_call_target="tpu_custom_call" | custom-call | flops 10000000 | bytes 2034144 | tf_op jit(solution)/shard_map/left/pallas_call | solution.py:330
  15.8 3.1 %early.1.refs_1_ = f32[2,512,128]{2,1,0:T(8,128)} custom-call(f32[960,128]{1,0:T(8,128)} %get-tuple-element.33.refs_0_, bf16[480,128]{1,0:T(8,128)(2,1)} %right.1.refs_1_.refs_5_, bf16[480,128]{1,0:T(8,128)(2,1)} %copy-done.1), custom_call_target="tpu_custom_call" | custom-call | flops 10000000 | bytes 1261568 | tf_op jit(solution)/shard_map/early/pallas_call | solution.py:330
  18.9 2.1 %collective-permute-done.3.refs_2_.refs_7_ = bf16[480,128]{1,0:T(8,128)(2,1)S(1)} collective-permute-done((bf16[480,128]{1,0:T(8,128)(2,1)}, bf16[480,128]{1,0:T(8,128)(2,1)S(1)}, u32[]{:S(2)}, u32[]{:S(2)}) %collective-permute-start.3) | collective-permute-done | bytes 122912 | tf_op jit(solution)/shard_map/ppermute | solution.py:352
  21.7 3.4 %late.1 = (f32[480,128]{1,0:T(8,128)}, bf16[480,128]{1,0:T(8,128)(2,1)}, bf16[480,128]{1,0:T(8,128)(2,1)}, bf16[480,128]{1,0:T(8,128)(2,1)}) custom-call(f32[960,128]{1,0:T(8,128)} %get-tuple-element.33.refs_0_, f32[2,512,128]{2,1,0:T(8,128)} %early.1.refs_1_, bf16[480,128]{1,0:T(8,128)(2,1)} %copy-done.3, bf16[480,128]{1,0:T(8,128)(2,1)} %copy-done.2), custom_call_target="tpu_custom_call" | custom-call | flops 10000000 | bytes 1875968 | tf_op jit(solution)/shard_map/late/pallas_call | solution.py:330
  25.0 1.5 %collective-permute-start.5 = (bf16[480,128]{1,0:T(8,128)(2,1)}, bf16[480,128]{1,0:T(8,128)(2,1)S(1)}, u32[]{:S(2)}, u32[]{:S(2)}) collective-permute-start(bf16[480,128]{1,0:T(8,128)(2,1)} %get-tuple-element.35), channel_id=1, source_target_pairs={{0,1},{1,0},{2,3},{3,2},{4,5},{5,4},{6,7},{7,6},{8,9},{9,8},{10,11... | collective-permute-start | bytes 368648 | tf_op jit(solution)/shard_map/ppermute | solution.py:355
  26.5 1.5 %collective-permute-start.6 = (bf16[480,128]{1,0:T(8,128)(2,1)}, bf16[480,128]{1,0:T(8,128)(2,1)S(1)}, u32[]{:S(2)}, u32[]{:S(2)}) collective-permute-start(bf16[480,128]{1,0:T(8,128)(2,1)} %get-tuple-element.36), channel_id=1, source_target_pairs={{0,2},{1,3},{2,0},{3,1},{4,6},{5,7},{6,4},{7,5},{8,10},{9,11},{10,... | collective-permute-start | bytes 368648 | tf_op jit(solution)/shard_map/ppermute | solution.py:355
  28.5 2.2 %collective-permute-done.5.refs_1_ = bf16[480,128]{1,0:T(8,128)(2,1)S(1)} collective-permute-done((bf16[480,128]{1,0:T(8,128)(2,1)}, bf16[480,128]{1,0:T(8,128)(2,1)S(1)}, u32[]{:S(2)}, u32[]{:S(2)}) %collective-permute-start.5) | collective-permute-done | bytes 122912 | tf_op jit(solution)/shard_map/ppermute | solution.py:355
  30.7 3.5 %collective-permute-done.6.refs_2_ = bf16[480,128]{1,0:T(8,128)(2,1)S(1)} collective-permute-done((bf16[480,128]{1,0:T(8,128)(2,1)}, bf16[480,128]{1,0:T(8,128)(2,1)S(1)}, u32[]{:S(2)}, u32[]{:S(2)}) %collective-permute-start.6) | collective-permute-done | bytes 122912 | tf_op jit(solution)/shard_map/ppermute | solution.py:355
  35.0 2.5 %middle.1 = (bf16[240,128]{1,0:T(8,128)(2,1)}, bf16[480,128]{1,0:T(8,128)(2,1)}, bf16[240,128]{1,0:T(8,128)(2,1)}, bf16[480,128]{1,0:T(8,128)(2,1)}) custom-call(f32[480,128]{1,0:T(8,128)} %get-tuple-element.34.refs_0_, bf16[480,128]{1,0:T(8,128)(2,1)} %copy-done.13, bf16[480,128]{1,0:T(8,128)(2,1)} %copy-done.14, bf16[480,128]{1,0:T(8,128)(2,1)} %copy-done.15, ...), custom_call_target="tpu_custom_call" | custom-call | flops 10000000 | bytes 1507328 | tf_op jit(solution)/shard_map/middle/pallas_call | solution.py:330
  39.5 1.4 %collective-permute-start.8 = (bf16[480,128]{1,0:T(8,128)(2,1)}, bf16[480,128]{1,0:T(8,128)(2,1)S(1)}, u32[]{:S(2)}, u32[]{:S(2)}) collective-permute-start(bf16[480,128]{1,0:T(8,128)(2,1)} %get-tuple-element.40.refs_1_), channel_id=1, source_target_pairs={{0,1},{1,0},{2,3},{3,2},{4,5},{5,4},{6,7},{7,6},{8,9},{9,8},{10,11... | collective-permute-start | bytes 368648 | tf_op jit(solution)/shard_map/ppermute | solution.py:355
  40.9 2.6 %collective-permute-done.10.refs_4_ = bf16[480,128]{1,0:T(8,128)(2,1)S(1)} collective-permute-done((bf16[480,128]{1,0:T(8,128)(2,1)}, bf16[480,128]{1,0:T(8,128)(2,1)S(1)}, u32[]{:S(2)}, u32[]{:S(2)}) %collective-permute-start.10) | collective-permute-done | bytes 122912 | tf_op jit(solution)/shard_map/ppermute | solution.py:355
  45.4 5.0 %grad_left.1 = (f32[480,128]{1,0:T(8,128)}, bf16[480,128]{1,0:T(8,128)(2,1)}, f32[480,128]{1,0:T(8,128)}) custom-call(f32[960,128]{1,0:T(8,128)} %get-tuple-element.32.refs_0_, bf16[480,128]{1,0:T(8,128)(2,1)} %get-tuple-element.40.refs_1_, bf16[480,128]{1,0:T(8,128)(2,1)} %copy-done.6, bf16[480,128]{1,0:T(8,128)(2,1)} %copy-done.5, ...), custom_call_target="tpu_custom_call" | custom-call | flops 10000000 | bytes 2088960 | tf_op jit(solution)/shard_map/grad_left/pallas_call | solution.py:330
  50.4 3.6 %send_right.1 = (bf16[480,128]{1,0:T(8,128)(2,1)}, bf16[480,128]{1,0:T(8,128)(2,1)}, bf16[480,128]{1,0:T(8,128)(2,1)}) custom-call(f32[960,128]{1,0:T(8,128)} %get-tuple-element.32.refs_0_, bf16[480,128]{1,0:T(8,128)(2,1)} %get-tuple-element.40.refs_1_, bf16[480,128]{1,0:T(8,128)(2,1)} %copy-done.6, bf16[480,128]{1,0:T(8,128)(2,1)} %copy-done.5, ...), custom_call_target="tpu_custom_call" | custom-call | flops 10000000 | bytes 1351680 | tf_op jit(solution)/shard_map/send_right/pallas_call | solution.py:330
  54.0 1.7 %collective-permute-start.13 = (bf16[480,128]{1,0:T(8,128)(2,1)}, bf16[480,128]{1,0:T(8,128)(2,1)S(1)}, u32[]{:S(2)}, u32[]{:S(2)}) collective-permute-start(bf16[480,128]{1,0:T(8,128)(2,1)} %get-tuple-element.50), channel_id=1, source_target_pairs={{0,8},{4,12},{8,0},{12,4},{16,24},{20,28},{24,16},{28,20},{1,9},{5... | collective-permute-start | bytes 368648 | tf_op jit(solution)/shard_map/ppermute | solution.py:352
  55.7 1.4 %collective-permute-start.14 = (bf16[480,128]{1,0:T(8,128)(2,1)}, bf16[480,128]{1,0:T(8,128)(2,1)S(1)}, u32[]{:S(2)}, u32[]{:S(2)}) collective-permute-start(bf16[480,128]{1,0:T(8,128)(2,1)} %get-tuple-element.51), channel_id=1, source_target_pairs={{0,16},{4,20},{8,24},{12,28},{16,0},{20,4},{24,8},{28,12},{1,17},{... | collective-permute-start | bytes 368648 | tf_op jit(solution)/shard_map/ppermute | solution.py:352
  57.1 1.3 %collective-permute-start.15 = (bf16[480,128]{1,0:T(8,128)(2,1)}, bf16[480,128]{1,0:T(8,128)(2,1)S(1)}, u32[]{:S(2)}, u32[]{:S(2)}) collective-permute-start(bf16[480,128]{1,0:T(8,128)(2,1)} %get-tuple-element.52), channel_id=1, source_target_pairs={{0,24},{4,28},{8,16},{12,20},{16,8},{20,12},{24,0},{28,4},{1,25},{... | collective-permute-start | bytes 368648 | tf_op jit(solution)/shard_map/ppermute | solution.py:352
  58.4 2.5 %factor.1 = (f32[480,128]{1,0:T(8,128)}, f32[480,128]{1,0:T(8,128)}, f32[480,128]{1,0:T(8,128)}, f32[480,128]{1,0:T(8,128)}, f32[480,128]{1,0:T(8,128)}, /*index=5*/f32[480,128]{1,0:T(8,128)}) custom-call(s32[120]{0:T(128)} %mask_ref.5, bf16[15,30,128]{2,1,0:T(8,128)(2,1)} %x_ref.3, bf16[128,512]{1,0:T(8,128)(2,1)} %w_ref.1), custom_call_target="tpu_custom_call" | custom-call | flops 10000000 | bytes 1721312 | tf_op jit(solution)/shard_map/factor/pallas_call | solution.py:330
  61.6 2.3 %finish_left.1 = (bf16[15,30,128]{2,1,0:T(8,128)(2,1)}, f32[480,128]{1,0:T(8,128)}) custom-call(f32[480,128]{1,0:T(8,128)} %get-tuple-element.41.own_ref, bf16[480,128]{1,0:T(8,128)(2,1)} %copy-done.11, f32[480,128]{1,0:T(8,128)} %get-tuple-element.43.l1_ref, f32[480,128]{1,0:T(8,128)} %get-tuple-element.44.l2_ref, ...), custom_call_target="tpu_custom_call" | custom-call | flops 10000000 | bytes 1565184 | tf_op jit(solution)/shard_map/finish_left/pallas_call | solution.py:330
  63.9 4.4 %collective-permute-done.14.refs_2_ = bf16[480,128]{1,0:T(8,128)(2,1)S(1)} collective-permute-done((bf16[480,128]{1,0:T(8,128)(2,1)}, bf16[480,128]{1,0:T(8,128)(2,1)S(1)}, u32[]{:S(2)}, u32[]{:S(2)}) %collective-permute-start.14) | collective-permute-done | bytes 122912 | tf_op jit(solution)/shard_map/ppermute | solution.py:352
  69.0 2.6 %finish.1 = bf16[15,30,128]{2,1,0:T(8,128)(2,1)} custom-call(f32[480,128]{1,0:T(8,128)} %get-tuple-element.49.refs_0_, bf16[480,128]{1,0:T(8,128)(2,1)} %copy-done.9, bf16[480,128]{1,0:T(8,128)(2,1)} %copy-done.10, bf16[480,128]{1,0:T(8,128)(2,1)} %copy-done.12, f32[480,128]{1,0:T(8,128)} %get-tuple-element.53.refs_4_, ...), custom_call_target="tpu_custom_call" | custom-call | flops 10000000 | bytes 2023936 | tf_op jit(solution)/shard_map/finish/pallas_call | solution.py:330
  (55 shorter events, 10.1 us)
Async XLA Ops:
  2.2 7.7 %copy-start.7 = (bf16[15,30,128]{2,1,0:T(8,128)(2,1)S(1)}, bf16[15,30,128]{2,1,0:T(8,128)(2,1)}, u32[]{:S(2)}) copy-start(bf16[15,30,128]{2,1,0:T(8,128)(2,1)} %cot_ref) | copy-start | bytes 345604
  2.2 7.7 %copy-start = (bf16[15,30,128]{2,1,0:T(8,128)(2,1)S(1)}, bf16[15,30,128]{2,1,0:T(8,128)(2,1)}, u32[]{:S(2)}) copy-start(bf16[15,30,128]{2,1,0:T(8,128)(2,1)} %x_ref.3) | copy-start | bytes 345604
  4.2 11.0 %collective-permute-start.2 = (bf16[480,128]{1,0:T(8,128)(2,1)}, bf16[480,128]{1,0:T(8,128)(2,1)S(1)}, u32[]{:S(2)}, u32[]{:S(2)}) collective-permute-start(bf16[480,128]{1,0:T(8,128)(2,1)} %right.1.refs_1_.refs_5_), channel_id=1, source_target_pairs={{0,8},{4,12},{8,0},{12,4},{16,24},{20,28},{24,16},{28,20},{1,9},{5... | collective-permute-start | bytes 368648 | tf_op jit(solution)/shard_map/ppermute | solution.py:352
  7.2 11.7 %collective-permute-start.4 = (bf16[480,128]{1,0:T(8,128)(2,1)}, bf16[480,128]{1,0:T(8,128)(2,1)S(1)}, u32[]{:S(2)}, u32[]{:S(2)}) collective-permute-start(bf16[480,128]{1,0:T(8,128)(2,1)} %right.1.refs_1_.refs_5_), channel_id=1, source_target_pairs={{0,24},{4,28},{8,16},{12,20},{16,8},{20,12},{24,0},{28,4},{1,25},{... | collective-permute-start | bytes 368648 | tf_op jit(solution)/shard_map/ppermute | solution.py:352
  9.7 11.3 %collective-permute-start.3 = (bf16[480,128]{1,0:T(8,128)(2,1)}, bf16[480,128]{1,0:T(8,128)(2,1)S(1)}, u32[]{:S(2)}, u32[]{:S(2)}) collective-permute-start(bf16[480,128]{1,0:T(8,128)(2,1)} %right.1.refs_1_.refs_5_), channel_id=1, source_target_pairs={{0,16},{4,20},{8,24},{12,28},{16,0},{20,4},{24,8},{28,12},{1,17},{... | collective-permute-start | bytes 368648 | tf_op jit(solution)/shard_map/ppermute | solution.py:352
  9.8 1.3 %collective-permute-start.1 = (bf16[15,30,128]{2,1,0:T(8,128)(2,1)S(1)}, bf16[15,30,128]{2,1,0:T(8,128)(2,1)S(1)}, u32[]{:S(2)}, u32[]{:S(2)}) collective-permute-start(bf16[15,30,128]{2,1,0:T(8,128)(2,1)S(1)} %copy-done.7), channel_id=1, source_target_pairs={{0,4},{4,0},{8,12},{12,8},{16,20},{20,16},{24,28},{28,24},{1,5},{5... | collective-permute-start | bytes 345608 | tf_op jit(solution)/shard_map/ppermute | solution.py:358
  9.8 1.5 %collective-permute-start = (bf16[15,30,128]{2,1,0:T(8,128)(2,1)S(1)}, bf16[15,30,128]{2,1,0:T(8,128)(2,1)S(1)}, u32[]{:S(2)}, u32[]{:S(2)}) collective-permute-start(bf16[15,30,128]{2,1,0:T(8,128)(2,1)S(1)} %copy-done), channel_id=1, source_target_pairs={{0,4},{4,0},{8,12},{12,8},{16,20},{20,16},{24,28},{28,24},{1,5},{5... | collective-permute-start | bytes 345608 | tf_op jit(solution)/shard_map/ppermute | solution.py:358
  18.9 2.1 %copy-start.2 = (bf16[480,128]{1,0:T(8,128)(2,1)}, bf16[480,128]{1,0:T(8,128)(2,1)S(1)}, u32[]{:S(2)}) copy-start(bf16[480,128]{1,0:T(8,128)(2,1)S(1)} %collective-permute-done.4.refs_3_.refs_8_) | copy-start | bytes 368644
  25.0 5.7 %collective-permute-start.5 = (bf16[480,128]{1,0:T(8,128)(2,1)}, bf16[480,128]{1,0:T(8,128)(2,1)S(1)}, u32[]{:S(2)}, u32[]{:S(2)}) collective-permute-start(bf16[480,128]{1,0:T(8,128)(2,1)} %get-tuple-element.35), channel_id=1, source_target_pairs={{0,1},{1,0},{2,3},{3,2},{4,5},{5,4},{6,7},{7,6},{8,9},{9,8},{10,11... | collective-permute-start | bytes 368648 | tf_op jit(solution)/shard_map/ppermute | solution.py:355
  26.5 7.7 %collective-permute-start.6 = (bf16[480,128]{1,0:T(8,128)(2,1)}, bf16[480,128]{1,0:T(8,128)(2,1)S(1)}, u32[]{:S(2)}, u32[]{:S(2)}) collective-permute-start(bf16[480,128]{1,0:T(8,128)(2,1)} %get-tuple-element.36), channel_id=1, source_target_pairs={{0,2},{1,3},{2,0},{3,1},{4,6},{5,7},{6,4},{7,5},{8,10},{9,11},{10,... | collective-permute-start | bytes 368648 | tf_op jit(solution)/shard_map/ppermute | solution.py:355
  28.0 6.2 %collective-permute-start.7 = (bf16[480,128]{1,0:T(8,128)(2,1)}, bf16[480,128]{1,0:T(8,128)(2,1)S(1)}, u32[]{:S(2)}, u32[]{:S(2)}) collective-permute-start(bf16[480,128]{1,0:T(8,128)(2,1)} %get-tuple-element.37), channel_id=1, source_target_pairs={{0,3},{1,2},{2,1},{3,0},{4,7},{5,6},{6,5},{7,4},{8,11},{9,10},{10,... | collective-permute-start | bytes 368648 | tf_op jit(solution)/shard_map/ppermute | solution.py:355
  30.7 3.5 %copy-start.13 = (bf16[480,128]{1,0:T(8,128)(2,1)}, bf16[480,128]{1,0:T(8,128)(2,1)S(1)}, u32[]{:S(2)}) copy-start(bf16[480,128]{1,0:T(8,128)(2,1)S(1)} %collective-permute-done.5.refs_1_) | copy-start | bytes 368644
  34.2 0.7 copy-start.15
  37.4 6.1 %collective-permute-start.10 = (bf16[480,128]{1,0:T(8,128)(2,1)}, bf16[480,128]{1,0:T(8,128)(2,1)S(1)}, u32[]{:S(2)}, u32[]{:S(2)}) collective-permute-start(bf16[480,128]{1,0:T(8,128)(2,1)} %get-tuple-element.40.refs_1_), channel_id=1, source_target_pairs={{0,3},{1,2},{2,1},{3,0},{4,7},{5,6},{6,5},{7,4},{8,11},{9,10},{10,... | collective-permute-start | bytes 368648 | tf_op jit(solution)/shard_map/ppermute | solution.py:355
  38.3 6.4 %collective-permute-start.9 = (bf16[480,128]{1,0:T(8,128)(2,1)}, bf16[480,128]{1,0:T(8,128)(2,1)S(1)}, u32[]{:S(2)}, u32[]{:S(2)}) collective-permute-start(bf16[480,128]{1,0:T(8,128)(2,1)} %get-tuple-element.40.refs_1_), channel_id=1, source_target_pairs={{0,2},{1,3},{2,0},{3,1},{4,6},{5,7},{6,4},{7,5},{8,10},{9,11},{10,... | collective-permute-start | bytes 368648 | tf_op jit(solution)/shard_map/ppermute | solution.py:355
  39.5 5.2 %collective-permute-start.8 = (bf16[480,128]{1,0:T(8,128)(2,1)}, bf16[480,128]{1,0:T(8,128)(2,1)S(1)}, u32[]{:S(2)}, u32[]{:S(2)}) collective-permute-start(bf16[480,128]{1,0:T(8,128)(2,1)} %get-tuple-element.40.refs_1_), channel_id=1, source_target_pairs={{0,1},{1,0},{2,3},{3,2},{4,5},{5,4},{6,7},{7,6},{8,9},{9,8},{10,11... | collective-permute-start | bytes 368648 | tf_op jit(solution)/shard_map/ppermute | solution.py:355
  40.9 20.0 %collective-permute-start.12 = (bf16[480,128]{1,0:T(8,128)(2,1)}, bf16[480,128]{1,0:T(8,128)(2,1)S(1)}, u32[]{:S(2)}, u32[]{:S(2)}) collective-permute-start(bf16[480,128]{1,0:T(8,128)(2,1)} %get-tuple-element.47), channel_id=1, source_target_pairs={{0,4},{4,0},{8,12},{12,8},{16,20},{20,16},{24,28},{28,24},{1,5},{5... | collective-permute-start | bytes 368648 | tf_op jit(solution)/shard_map/ppermute | solution.py:358
  43.5 1.2 %copy-start.4 = (bf16[480,128]{1,0:T(8,128)(2,1)}, bf16[480,128]{1,0:T(8,128)(2,1)S(1)}, u32[]{:S(2)}) copy-start(bf16[480,128]{1,0:T(8,128)(2,1)S(1)} %collective-permute-done.10.refs_4_) | copy-start | bytes 368644
  44.7 0.7 copy-start.6
  50.4 10.5 %collective-permute-start.11 = (bf16[480,128]{1,0:T(8,128)(2,1)}, bf16[480,128]{1,0:T(8,128)(2,1)S(1)}, u32[]{:S(2)}, u32[]{:S(2)}) collective-permute-start(bf16[480,128]{1,0:T(8,128)(2,1)} %get-tuple-element.42), channel_id=1, source_target_pairs={{0,4},{4,0},{8,12},{12,8},{16,20},{20,16},{24,28},{28,24},{1,5},{5... | collective-permute-start | bytes 368648 | tf_op jit(solution)/shard_map/ppermute | solution.py:358
  54.0 9.9 %collective-permute-start.13 = (bf16[480,128]{1,0:T(8,128)(2,1)}, bf16[480,128]{1,0:T(8,128)(2,1)S(1)}, u32[]{:S(2)}, u32[]{:S(2)}) collective-permute-start(bf16[480,128]{1,0:T(8,128)(2,1)} %get-tuple-element.50), channel_id=1, source_target_pairs={{0,8},{4,12},{8,0},{12,4},{16,24},{20,28},{24,16},{28,20},{1,9},{5... | collective-permute-start | bytes 368648 | tf_op jit(solution)/shard_map/ppermute | solution.py:352
  55.7 12.6 %collective-permute-start.14 = (bf16[480,128]{1,0:T(8,128)(2,1)}, bf16[480,128]{1,0:T(8,128)(2,1)S(1)}, u32[]{:S(2)}, u32[]{:S(2)}) collective-permute-start(bf16[480,128]{1,0:T(8,128)(2,1)} %get-tuple-element.51), channel_id=1, source_target_pairs={{0,16},{4,20},{8,24},{12,28},{16,0},{20,4},{24,8},{28,12},{1,17},{... | collective-permute-start | bytes 368648 | tf_op jit(solution)/shard_map/ppermute | solution.py:352
  57.1 11.2 %collective-permute-start.15 = (bf16[480,128]{1,0:T(8,128)(2,1)}, bf16[480,128]{1,0:T(8,128)(2,1)S(1)}, u32[]{:S(2)}, u32[]{:S(2)}) collective-permute-start(bf16[480,128]{1,0:T(8,128)(2,1)} %get-tuple-element.52), channel_id=1, source_target_pairs={{0,24},{4,28},{8,16},{12,20},{16,8},{20,12},{24,0},{28,4},{1,25},{... | collective-permute-start | bytes 368648 | tf_op jit(solution)/shard_map/ppermute | solution.py:352
  63.9 4.4 %copy-start.9 = (bf16[480,128]{1,0:T(8,128)(2,1)}, bf16[480,128]{1,0:T(8,128)(2,1)S(1)}, u32[]{:S(2)}) copy-start(bf16[480,128]{1,0:T(8,128)(2,1)S(1)} %collective-permute-done.13.refs_1_) | copy-start | bytes 368644
  (10 other events, 6.6 us)

commit v2 on v1

--- a/solution.py
+++ b/solution.py
@@ -68,10 +68,10 @@
 def right_kernel(mask_ref, x_ref, w_ref, out_ref, xs):
     rows, cols, channels = x_ref.shape
     pitch = pad_to(cols, 16)
-    hidden = w_ref.shape[1] // 2
+    hidden = w_ref.shape[1] // 4
     load_cells(x_ref, xs, 0)
     normed, _ = normalize(xs[...])
-    projected = matmul(normed.astype(BF16), w_ref[...])
+    projected = matmul(normed.astype(BF16), w_ref[:, 2 * hidden :])
     right = jax.nn.sigmoid(projected[:, :hidden]) * projected[:, hidden:]
     flags = col_mask(mask_ref, lax.axis_index("ch") * cols, cols, pitch, hidden)
     start = lax.axis_index("dap") * rows
@@ -86,14 +86,14 @@
     rows, cols, channels = x_ref.shape
     pitch = pad_to(cols, 16)
     half = pad_to(rows, 16)
-    hidden = w_ref.shape[1] // 2
+    hidden = w_ref.shape[1] // 4
     dap = lax.axis_index("dap")
     core = lax.rem(dap, 2)
     load_cells(x_ref, xs, 0)
     load_cells(xp_ref, xs, rows)
     normed, _ = normalize(xs[...])
     normed_half = normed.astype(BF16)
-    projected = matmul(normed_half, w_ref[...])
+    projected = matmul(normed_half, w_ref[:, : 2 * hidden])
     left = jax.nn.sigmoid(projected[:, :hidden]) * projected[:, hidden:]
     flags = col_mask(mask_ref, lax.axis_index("ch") * cols, cols, pitch, hidden)
     for i in range(2 * rows):
@@ -166,30 +166,31 @@
 
 def early_kernel(rows, cols, count, *refs):
     lt_ref, shards = refs[0], refs[1 : 1 + count]
-    out_ref, rs = refs[1 + count :]
+    out_ref, rs, ps = refs[1 + count :]
     for s in range(count):
-        product_part(lt_ref, shards[s], rs, out_ref.at[s], rows, cols)
+        product_part(lt_ref, shards[s], rs, ps, rows, cols)
+        out_ref[s] = ps[: out_ref.shape[1], :].astype(BF16)
 
 
 def late_kernel(rows, cols, blocks, early, *refs):
     lt_ref, early_ref = refs[:2]
     shards = refs[2 : 2 + blocks - early]
     outs = refs[2 + blocks - early : 2 + 2 * blocks - early]
-    rs, ps = refs[2 + 2 * blocks - early :]
+    rs, ps, held = refs[2 + 2 * blocks - early :]
     chip, column = lax.axis_index("dap") // 2, lax.axis_index("ch")
-    used = 2 * rows * pad_to(rows, 16)
     for s in range(early):
-        ps[chip ^ s] = early_ref[s]
+        held[s] = early_ref[s]
     for s in range(early, blocks):
-        product_part(lt_ref, shards[s - early], rs, ps.at[chip ^ s], rows, cols)
+        product_part(lt_ref, shards[s - early], rs, ps, rows, cols)
+        held[s] = ps[: held.shape[1], :].astype(BF16)
     for t in range(blocks):
-        outs[t][...] = ps[column ^ t, :used, :].astype(outs[t].dtype)
+        outs[t][...] = held[chip ^ column ^ t]
 
 
 def middle_kernel(blocks, *refs):
     parts = refs[:blocks]
     gate_ref, cot_ref, w_ref, upd_ref, back_ref, logit_ref, gp_ref = refs[blocks:]
-    total = parts[0][...]
+    total = parts[0][...].astype(F32)
     for t in range(1, blocks):
         total = total + parts[t][...].astype(F32)
     product = total.astype(BF16).astype(F32)
@@ -208,39 +209,35 @@
     back_ref[own:, :] = logit[own:]
 
 
-def grad_right_part(l_ref, gs, block, store, rows, cols):
+def grad_right_part(l_ref, piece, store, rows, cols):
     pitch, half = pad_to(cols, 16), pad_to(rows, 16)
-    piece = gs.at[block]
 
     def step(b, _):
-        sums = [jnp.zeros((pitch // 8, 8, gs.shape[2]), F32) for _ in range(JB)]
+        sums = [jnp.zeros((pitch // 8, 8, l_ref.shape[1]), F32) for _ in range(JB)]
         for i in range(2 * rows):
             left = tiles(l_ref[i * pitch : (i + 1) * pitch, :])
             for n in range(JB):
                 sums[n] = sums[n] + left * row_of(piece, i * half + b * JB + n)[None]
         for n in range(JB):
             at = pl.multiple_of((b * JB + n) * pitch, pitch)
-            store(pl.ds(at, pitch), sums[n].reshape(pitch, gs.shape[2]))
+            store(pl.ds(at, pitch), sums[n].reshape(pitch, l_ref.shape[1]))
         return 0
 
     lax.fori_loop(0, rows // JB, step, 0)
 
 
-def stage_pieces(pieces, gs):
-    column = lax.axis_index("ch")
-    for t, piece in enumerate(pieces):
-        gs[column ^ t] = piece[...].astype(F32)
-
-
-def send_right_kernel(rows, cols, blocks, *refs):
-    l_ref, pieces = refs[0], refs[1 : 1 + blocks]
-    outs, gs = refs[1 + blocks : 2 * blocks], refs[2 * blocks]
-    chip = lax.axis_index("dap") // 2
-    stage_pieces(pieces, gs)
-    for s in range(1, blocks):
-        def store(where, value, s=s):
-            outs[s - 1][where, :] = value.astype(BF16)
-        grad_right_part(l_ref, gs, chip ^ s, store, rows, cols)
+def send_right_kernel(rows, cols, blocks, s, *refs):
+    l_ref, pieces, (out_ref, gs) = refs[0], refs[1 : 1 + blocks], refs[1 + blocks :]
+    chip, column = lax.axis_index("dap") // 2, lax.axis_index("ch")
+    for t in range(blocks):
+        @pl.when(chip ^ column ^ s == t)
+        def _(t=t):
+            gs[...] = pieces[t][...].astype(F32)
+
+    def store(where, value):
+        out_ref[where, :] = value.astype(BF16)
+
+    grad_right_part(l_ref, gs, store, rows, cols)
 
 
 def grad_left_kernel(rows, cols, blocks, *refs):
@@ -248,7 +245,9 @@
     own_ref, send_ref, right_ref, gs, rs = refs[1 + 2 * blocks :]
     pitch, half = pad_to(cols, 16), pad_to(rows, 16)
     chip = lax.axis_index("dap") // 2
-    stage_pieces(pieces, gs)
+    column = lax.axis_index("ch")
+    for t in range(blocks):
+        gs[column ^ t] = pieces[t][...].astype(F32)
     for s in range(blocks):
         rs[chip ^ s] = shards[s][...].astype(F32)
 
@@ -279,7 +278,7 @@
     def store(where, value):
         right_ref[where, :] = value
 
-    grad_right_part(l_ref, gs, chip, store, rows, cols)
+    grad_right_part(l_ref, gs.at[chip], store, rows, cols)
 
 
 def finish_left_kernel(own_ref, got_ref, l1_ref, l2_ref, w_ref, wg_ref, upd_ref, logit_ref, back_ref,
@@ -299,7 +298,7 @@
     grad_left = (own_ref[...] + got_ref[...].astype(F32)).astype(BF16).astype(F32)
     hidden = own_ref.shape[1]
     acc = matmul_t((grad_left * l1_ref[...]).astype(BF16), w_ref[:, :hidden])
-    acc = acc + matmul_t((grad_left * l2_ref[...]).astype(BF16), w_ref[:, hidden:])
+    acc = acc + matmul_t((grad_left * l2_ref[...]).astype(BF16), w_ref[:, hidden : 2 * hidden])
     acc_ref[...] = acc + matmul_t(gs[...].astype(BF16), wg_ref[...])
 
 
@@ -313,8 +312,8 @@
         total = total + parts[s][...].astype(F32)
     grad_right = total.astype(BF16).astype(F32)
     hidden = total.shape[1]
-    grad = acc_ref[...] + matmul_t((grad_right * r1_ref[...]).astype(BF16), w_ref[:, :hidden])
-    grad = grad + matmul_t((grad_right * r2_ref[...]).astype(BF16), w_ref[:, hidden:])
+    grad = acc_ref[...] + matmul_t((grad_right * r1_ref[...]).astype(BF16), w_ref[:, 2 * hidden : 3 * hidden])
+    grad = grad + matmul_t((grad_right * r2_ref[...]).astype(BF16), w_ref[:, 3 * hidden :])
     result = norm_back(grad, normed_ref[...], scale_ref[...]).astype(BF16)
     for i in range(rows):
         out_ref[i] = result[i * pitch : i * pitch + cols]
@@ -324,7 +323,7 @@
 SMEM = pl.BlockSpec(memory_space=pltpu.SMEM)
 
 
-def call(body, name, outs, args, scratch=(), smem=0, flops=10**7):
+def call(body, name, outs, args, scratch=(), smem=0, flops=10**7, limit=20):
     outs = [jax.ShapeDtypeStruct(shape, dtype) for shape, dtype in outs]
     moved = sum(a.size * a.dtype.itemsize for a in list(args) + outs)
     return pl.pallas_call(
@@ -333,8 +332,8 @@
         out_shape=outs,
         in_specs=[SMEM] * smem + [VMEM] * (len(args) - smem),
         out_specs=[VMEM] * len(outs),
-        scratch_shapes=[pltpu.VMEM(shape, F32) for shape in scratch],
-        compiler_params=pltpu.CompilerParams(vmem_limit_bytes=60 << 20),
+        scratch_shapes=[pltpu.VMEM(shape[:-1], BF16) if shape[-1] is None else pltpu.VMEM(shape, F32) for shape in scratch],
+        compiler_params=pltpu.CompilerParams(vmem_limit_bytes=limit << 20),
         cost_estimate=pl.CostEstimate(flops=flops, bytes_accessed=moved, transcendentals=0),
     )(*args)
 
@@ -346,7 +345,6 @@
     cells, wide, mids = rows * pitch, 2 * rows * pitch, 2 * rows * half
     if devices != 2 * blocks or cols != 2 * rows or blocks & (blocks - 1) or rows % JB:
         raise ValueError("unsupported split")
-    w_left, w_right = w_proj[:, : 2 * hidden], w_proj[:, 2 * hidden :]
 
     def along_dap(value, s):
         return lax.ppermute(value, "dap", [(d, d ^ (2 * s)) for d in range(devices)])
@@ -357,7 +355,7 @@
     def to_partner(value):
         return lax.ppermute(value, "dap", [(d, d ^ 1) for d in range(devices)])
 
-    (right,) = call(right_kernel, "right", [((cells, hidden), BF16)], (mask, x, w_right),
+    (right,) = call(right_kernel, "right", [((cells, hidden), BF16)], (mask, x, w_proj),
                     [(cells, channels)], smem=1)
     shards = [right] + [along_dap(right, s) for s in range(1, blocks)]
     x_late, cot_late, _ = lax.optimization_barrier((x, cot, right))
@@ -365,18 +363,18 @@
     left, left_t, gate, upstream = call(
         left_kernel, "left",
         [((wide, hidden), F32), ((cols * tall, hidden), F32), ((mids, channels), F32), ((mids, channels), F32)],
-        (mask, x_late, x_pair, cot_late, cot_pair, w_left, w_gate),
+        (mask, x_late, x_pair, cot_late, cot_pair, w_proj, w_gate),
         [(wide, channels), (tall * pitch, hidden), (wide, channels)], smem=1)
     normed, scale, l1, l2, r1, r2 = call(
         factor_kernel, "factor", [((cells, hidden), F32)] * 6, (mask, x_late, w_proj),
         [(cells, channels)], smem=1)
     early = min(EARLY, blocks)
     (started,) = call(functools.partial(early_kernel, rows, cols, early), "early",
-                      [((early, tall * half, hidden), F32)], (left_t, *shards[:early]), [(cells, hidden)])
+                      [((early, mids, hidden), BF16)], (left_t, *shards[:early]), [(cells, hidden), (tall * half, hidden)])
     parts = call(functools.partial(late_kernel, rows, cols, blocks, early), "late",
-                 [((mids, hidden), F32)] + [((mids, hidden), BF16)] * (blocks - 1),
+                 [((mids, hidden), BF16)] * blocks,
                  (left_t, started, *shards[early:]),
-                 [(cells, hidden), (blocks, tall * half, hidden)])
+                 [(cells, hidden), (tall * half, hidden), (blocks, mids, hidden, None)])
     parts = [parts[0]] + [along_ch(parts[t], t) for t in range(1, blocks)]
     update, back, logit, grad_product = call(
         functools.partial(middle_kernel, blocks), "middle",
@@ -384,20 +382,23 @@
         (*parts, gate, upstream, w_out))
     pieces = [grad_product] + [along_ch(grad_product, t) for t in range(1, blocks)]
     back = to_partner(back)
-    sends = call(functools.partial(send_right_kernel, rows, cols, blocks), "send_right",
-                 [((cells, hidden), BF16)] * (blocks - 1), (left, *pieces), [(blocks, mids, hidden)])
-    gots = [along_dap(sends[s - 1], s) for s in range(1, blocks)]
+    gots = [None] * blocks
+    for s in [*range(2, blocks), 1]:
+        (send,) = call(functools.partial(send_right_kernel, rows, cols, blocks, s), "send_right",
+                       [((cells, hidden), BF16)], (left, *pieces), [(mids, hidden)])
+        gots[s] = along_dap(send, s)
+    left_late, _ = lax.optimization_barrier((left, send))
     left_own, left_send, right_own = call(
         functools.partial(grad_left_kernel, rows, cols, blocks), "grad_left",
         [((cells, hidden), F32), ((cells, hidden), BF16), ((cells, hidden), F32)],
-        (left, *pieces, *shards), [(blocks, mids, hidden), (blocks, cells, hidden)])
+        (left_late, *pieces, *shards), [(blocks, mids, hidden), (blocks, cells, hidden)])
     left_got = to_partner(left_send)
     pair_update, acc = call(
         finish_left_kernel, "finish_left", [((rows, cols, channels), BF16), ((cells, channels), F32)],
-        (left_own, left_got, l1, l2, w_left, w_gate, update, logit, back),
+        (left_own, left_got, l1, l2, w_proj, w_gate, update, logit, back),
         [(cells, channels), (cells, channels)])
     (grad_pair,) = call(functools.partial(finish_kernel, blocks), "finish", [((rows, cols, channels), BF16)],
-                        (right_own, *gots, r1, r2, w_right, acc, normed, scale))
+                        (right_own, *gots[1:], r1, r2, w_proj, acc, normed, scale))
     return pair_update, grad_pair
 
 

time: 72 us -> 58.1 us (0.81)
  Pallas kernels: 30.2 us -> 13.5 us
  waiting for transfers between devices: 17 us -> 24.1 us
  local copies, waits for them, and re-layouts: 6.22 us -> 2.48 us
    pallas_call x10 -> x12, Pallas kernels: 30.2 us -> 13.5 us  [call(): pl.pallas_call(body, name=name, out_shape=outs, in_specs=[SMEM] * smem +...]
    ppermute x6, waiting for transfers between devices: 6.48 us -> 14 us  [along_dap(): return lax.ppermute(value, 'dap', [(d, d ^ 2 * s) for d in range(devices)])]
    unnamed x36 -> x18, local copies, waits for them, and re-layouts: 4.69 us -> 2.48 us
    slice x1 -> x0, local copies, waits for them, and re-layouts: 1.53 us -> none  [on_device(): w_left, w_right = (w_proj[:, :2 * hidden], w_proj[:, 2 * hidden:])]
    ppermute x6, starting transfers between devices: 10 us -> 9.29 us  [along_dap(): return lax.ppermute(value, 'dap', [(d, d ^ 2 * s) for d in range(devices)])]
  transfers between devices with their start and end apart: 16 -> 16, of which waited for: 8 -> 10; matrix products, arithmetic and copies ran while one was open for 0% -> 0% of each run, Pallas kernels for 28% -> 17%
where the time goes in v2:
time: 58.1 us; the launch traced here: 57.9 us
  waiting for transfers between devices  24.1 us (41%)
  starting transfers between devices  17 us (29%)
  Pallas kernels  13.5 us (23%)
  local copies, waits for them, and re-layouts  2.48 us (4%)
  between operations  0.76 us (1%)
    ppermute x6, waiting for transfers between devices, along_dap(): return lax.ppermute(value, 'dap', [(d, d ^ 2 * s) for d in range(devices)])  14 us
    pallas_call x12, Pallas kernels, call(): pl.pallas_call(body, name=name, out_shape=outs, in_specs=[SMEM] * smem +...  13.5 us
    ppermute x6, starting transfers between devices, along_dap(): return lax.ppermute(value, 'dap', [(d, d ^ 2 * s) for d in range(devices)])  9.29 us
    ppermute x6, waiting for transfers between devices, along_ch(): return lax.ppermute(value, 'ch', [(h, h ^ t) for h in range(blocks)])  9.12 us
    ppermute x6, starting transfers between devices, along_ch(): return lax.ppermute(value, 'ch', [(h, h ^ t) for h in range(blocks)])  7.11 us
    unnamed x18, local copies, waits for them, and re-layouts  2.48 us
  transfers between devices with their start and end apart: 16, of which 10 were waited for; matrix products, arithmetic and copies ran while one was open for 0% of the time, Pallas kernels for 17%

profile of v2, /device:TPU:0, one launch (start us, length us, event | category | flops | bytes accessed | tf_op | source)
XLA Modules:
  0.0 57.9 jit_solution(10605860900488785061)
XLA Ops:
  3.1 0.9 %right.1.refs_1_.refs_5_ = bf16[480,128]{1,0:T(8,128)(2,1)S(1)} custom-call(s32[120]{0:T(128)S(1)} %copy-done.7, bf16[15,30,128]{2,1,0:T(8,128)(2,1)S(1)} %copy-done.2, bf16[128,512]{1,0:T(8,128)(2,1)S(1)} %copy-done), custom_call_target="tpu_custom_call" | custom-call | flops 10000000 | bytes 369632 | tf_op jit(solution)/shard_map/right/pallas_call | solution.py:329
  4.0 3.1 %collective-permute-start.2 = (bf16[480,128]{1,0:T(8,128)(2,1)S(1)}, bf16[480,128]{1,0:T(8,128)(2,1)S(1)}, u32[]{:S(2)}, u32[]{:S(2)}) collective-permute-start(bf16[480,128]{1,0:T(8,128)(2,1)S(1)} %right.1.refs_1_.refs_5_), channel_id=1, source_target_pairs={{0,8},{4,12},{8,0},{12,4},{16,24},{20,28},{24,16},{28,20},{1,9},{5... | collective-permute-start | bytes 368648 | tf_op jit(solution)/shard_map/ppermute | solution.py:350
  7.1 2.5 %collective-permute-start.4 = (bf16[480,128]{1,0:T(8,128)(2,1)S(1)}, bf16[480,128]{1,0:T(8,128)(2,1)S(1)}, u32[]{:S(2)}, u32[]{:S(2)}) collective-permute-start(bf16[480,128]{1,0:T(8,128)(2,1)S(1)} %right.1.refs_1_.refs_5_), channel_id=1, source_target_pairs={{0,24},{4,28},{8,16},{12,20},{16,8},{20,12},{24,0},{28,4},{1,25},{... | collective-permute-start | bytes 368648 | tf_op jit(solution)/shard_map/ppermute | solution.py:350
  11.3 1.5 %left.1 = (f32[960,128]{1,0:T(8,128)S(1)}, f32[960,128]{1,0:T(8,128)S(1)}, f32[480,128]{1,0:T(8,128)S(1)}, f32[480,128]{1,0:T(8,128)S(1)}) custom-call(s32[120]{0:T(128)S(1)} %copy-done.7, bf16[15,30,128]{2,1,0:T(8,128)(2,1)S(1)} %copy-done.2, bf16[15,30,128]{2,1,0:T(8,128)(2,1)S(1)} %collective-permute-done.xp_ref, bf16[15,30,128]{2,1,0:T(8,128)(2,1)S(1)} %copy-done.5, ...), custom_call_target="tpu_custom_call" | custom-call | flops 10000000 | bytes 2099680 | tf_op jit(solution)/shard_map/left/pallas_call | solution.py:329
  12.8 1.4 %early.1.refs_1_ = bf16[2,480,128]{2,1,0:T(8,128)(2,1)S(1)} custom-call(f32[960,128]{1,0:T(8,128)S(1)} %get-tuple-element.31.refs_0_, bf16[480,128]{1,0:T(8,128)(2,1)S(1)} %right.1.refs_1_.refs_5_, bf16[480,128]{1,0:T(8,128)(2,1)S(1)} %collective-permute-done.2.refs_2_.refs_6_), custom_call_target="tpu_custom_call" | custom-call | flops 10000000 | bytes 983040 | tf_op jit(solution)/shard_map/early/pallas_call | solution.py:329
  14.2 2.3 %collective-permute-done.4.refs_3_.refs_8_ = bf16[480,128]{1,0:T(8,128)(2,1)S(1)} collective-permute-done((bf16[480,128]{1,0:T(8,128)(2,1)S(1)}, bf16[480,128]{1,0:T(8,128)(2,1)S(1)}, u32[]{:S(2)}, u32[]{:S(2)}) %collective-permute-start.4) | collective-permute-done | bytes 122912 | tf_op jit(solution)/shard_map/ppermute | solution.py:350
  16.5 4.2 %collective-permute-done.3.refs_2_.refs_7_ = bf16[480,128]{1,0:T(8,128)(2,1)S(1)} collective-permute-done((bf16[480,128]{1,0:T(8,128)(2,1)S(1)}, bf16[480,128]{1,0:T(8,128)(2,1)S(1)}, u32[]{:S(2)}, u32[]{:S(2)}) %collective-permute-start.3) | collective-permute-done | bytes 122912 | tf_op jit(solution)/shard_map/ppermute | solution.py:350
  20.7 1.4 %late.1 = (bf16[480,128]{1,0:T(8,128)(2,1)S(1)}, bf16[480,128]{1,0:T(8,128)(2,1)S(1)}, bf16[480,128]{1,0:T(8,128)(2,1)S(1)}, bf16[480,128]{1,0:T(8,128)(2,1)S(1)}) custom-call(f32[960,128]{1,0:T(8,128)S(1)} %get-tuple-element.31.refs_0_, bf16[2,480,128]{2,1,0:T(8,128)(2,1)S(1)} %early.1.refs_1_, bf16[480,128]{1,0:T(8,128)(2,1)S(1)} %collective-permute-done.3.refs_2_.refs_7_, ...), custom_call_target="tpu_custom_call" | custom-call | flops 10000000 | bytes 1474560 | tf_op jit(solution)/shard_map/late/pallas_call | solution.py:329
  22.1 1.6 %collective-permute-start.5 = (bf16[480,128]{1,0:T(8,128)(2,1)S(1)}, bf16[480,128]{1,0:T(8,128)(2,1)S(1)}, u32[]{:S(2)}, u32[]{:S(2)}) collective-permute-start(bf16[480,128]{1,0:T(8,128)(2,1)S(1)} %get-tuple-element.33), channel_id=1, source_target_pairs={{0,1},{1,0},{2,3},{3,2},{4,5},{5,4},{6,7},{7,6},{8,9},{9,8},{10,11... | collective-permute-start | bytes 368648 | tf_op jit(solution)/shard_map/ppermute | solution.py:353
  23.7 1.5 %collective-permute-start.6 = (bf16[480,128]{1,0:T(8,128)(2,1)S(1)}, bf16[480,128]{1,0:T(8,128)(2,1)S(1)}, u32[]{:S(2)}, u32[]{:S(2)}) collective-permute-start(bf16[480,128]{1,0:T(8,128)(2,1)S(1)} %get-tuple-element.34), channel_id=1, source_target_pairs={{0,2},{1,3},{2,0},{3,1},{4,6},{5,7},{6,4},{7,5},{8,10},{9,11},{10,... | collective-permute-start | bytes 368648 | tf_op jit(solution)/shard_map/ppermute | solution.py:353
  25.7 2.0 %collective-permute-done.5.refs_1_ = bf16[480,128]{1,0:T(8,128)(2,1)S(1)} collective-permute-done((bf16[480,128]{1,0:T(8,128)(2,1)S(1)}, bf16[480,128]{1,0:T(8,128)(2,1)S(1)}, u32[]{:S(2)}, u32[]{:S(2)}) %collective-permute-start.5) | collective-permute-done | bytes 122912 | tf_op jit(solution)/shard_map/ppermute | solution.py:353
  27.7 3.5 %collective-permute-done.6.refs_2_ = bf16[480,128]{1,0:T(8,128)(2,1)S(1)} collective-permute-done((bf16[480,128]{1,0:T(8,128)(2,1)S(1)}, bf16[480,128]{1,0:T(8,128)(2,1)S(1)}, u32[]{:S(2)}, u32[]{:S(2)}) %collective-permute-start.6) | collective-permute-done | bytes 122912 | tf_op jit(solution)/shard_map/ppermute | solution.py:353
  31.7 1.0 %collective-permute-start.10 = (bf16[480,128]{1,0:T(8,128)(2,1)S(1)}, bf16[480,128]{1,0:T(8,128)(2,1)S(1)}, u32[]{:S(2)}, u32[]{:S(2)}) collective-permute-start(bf16[480,128]{1,0:T(8,128)(2,1)S(1)} %get-tuple-element.38.refs_1_), channel_id=1, source_target_pairs={{0,3},{1,2},{2,1},{3,0},{4,7},{5,6},{6,5},{7,4},{8,11},{9,10},{10,... | collective-permute-start | bytes 368648 | tf_op jit(solution)/shard_map/ppermute | solution.py:353
  32.7 1.2 %collective-permute-start.9 = (bf16[480,128]{1,0:T(8,128)(2,1)S(1)}, bf16[480,128]{1,0:T(8,128)(2,1)S(1)}, u32[]{:S(2)}, u32[]{:S(2)}) collective-permute-start(bf16[480,128]{1,0:T(8,128)(2,1)S(1)} %get-tuple-element.38.refs_1_), channel_id=1, source_target_pairs={{0,2},{1,3},{2,0},{3,1},{4,6},{5,7},{6,4},{7,5},{8,10},{9,11},{10,... | collective-permute-start | bytes 368648 | tf_op jit(solution)/shard_map/ppermute | solution.py:353
  33.9 1.3 %collective-permute-start.8 = (bf16[480,128]{1,0:T(8,128)(2,1)S(1)}, bf16[480,128]{1,0:T(8,128)(2,1)S(1)}, u32[]{:S(2)}, u32[]{:S(2)}) collective-permute-start(bf16[480,128]{1,0:T(8,128)(2,1)S(1)} %get-tuple-element.38.refs_1_), channel_id=1, source_target_pairs={{0,1},{1,0},{2,3},{3,2},{4,5},{5,4},{6,7},{7,6},{8,9},{9,8},{10,11... | collective-permute-start | bytes 368648 | tf_op jit(solution)/shard_map/ppermute | solution.py:353
  35.2 2.4 %collective-permute-done.10.refs_4_ = bf16[480,128]{1,0:T(8,128)(2,1)S(1)} collective-permute-done((bf16[480,128]{1,0:T(8,128)(2,1)S(1)}, bf16[480,128]{1,0:T(8,128)(2,1)S(1)}, u32[]{:S(2)}, u32[]{:S(2)}) %collective-permute-start.10) | collective-permute-done | bytes 122912 | tf_op jit(solution)/shard_map/ppermute | solution.py:353
  37.6 1.2 %collective-permute-done.9.refs_3_ = bf16[480,128]{1,0:T(8,128)(2,1)S(1)} collective-permute-done((bf16[480,128]{1,0:T(8,128)(2,1)S(1)}, bf16[480,128]{1,0:T(8,128)(2,1)S(1)}, u32[]{:S(2)}, u32[]{:S(2)}) %collective-permute-start.9) | collective-permute-done | bytes 122912 | tf_op jit(solution)/shard_map/ppermute | solution.py:353
  39.4 2.9 %grad_left.1 = (f32[480,128]{1,0:T(8,128)S(1)}, bf16[480,128]{1,0:T(8,128)(2,1)S(1)}, f32[480,128]{1,0:T(8,128)S(1)}) custom-call(f32[960,128]{1,0:T(8,128)S(1)} %get-tuple-element.39.refs_0_, bf16[480,128]{1,0:T(8,128)(2,1)S(1)} %get-tuple-element.38.refs_1_, bf16[480,128]{1,0:T(8,128)(2,1)S(1)} %collective-permute-done.8.refs_2_, ...), custom_call_target="tpu_custom_call" | custom-call | flops 10000000 | bytes 2088960 | tf_op jit(solution)/shard_map/grad_left/pallas_call | solution.py:329
  43.8 2.5 %collective-permute-start.15 = (bf16[480,128]{1,0:T(8,128)(2,1)S(1)}, bf16[480,128]{1,0:T(8,128)(2,1)S(1)}, u32[]{:S(2)}, u32[]{:S(2)}) collective-permute-start(bf16[480,128]{1,0:T(8,128)(2,1)S(1)} %send_right.5), channel_id=1, source_target_pairs={{0,24},{4,28},{8,16},{12,20},{16,8},{20,12},{24,0},{28,4},{1,25},{... | collective-permute-start | bytes 368648 | tf_op jit(solution)/shard_map/ppermute | solution.py:350
  46.3 1.0 %collective-permute-start.13 = (bf16[480,128]{1,0:T(8,128)(2,1)S(1)}, bf16[480,128]{1,0:T(8,128)(2,1)S(1)}, u32[]{:S(2)}, u32[]{:S(2)}) collective-permute-start(bf16[480,128]{1,0:T(8,128)(2,1)S(1)} %send_right.3), channel_id=1, source_target_pairs={{0,8},{4,12},{8,0},{12,4},{16,24},{20,28},{24,16},{28,20},{1,9},{5... | collective-permute-start | bytes 368648 | tf_op jit(solution)/shard_map/ppermute | solution.py:350
  47.3 1.1 %factor.1 = (f32[480,128]{1,0:T(8,128)S(1)}, f32[480,128]{1,0:T(8,128)S(1)}, f32[480,128]{1,0:T(8,128)S(1)}, f32[480,128]{1,0:T(8,128)S(1)}, f32[480,128]{1,0:T(8,128)S(1)}, /*index=5*/f32[480,128]{1,0:T(8,128)S(1)}) custom-call(s32[120]{0:T(128)S(1)} %copy-done.8, bf16[15,30,128]{2,1,0:T(8,128)(2,1)S(1)} %copy-done.3, bf16[128,512]{1,0:T(8,128)(2,1)S(1)} %copy-done.1), custom_call_target="tpu_custom_call" | custom-call | flops 10000000 | bytes 1721312 | tf_op jit(solution)/shard_map/factor/pallas_call | solution.py:329
  49.3 5.6 %collective-permute-done.14.refs_2_ = bf16[480,128]{1,0:T(8,128)(2,1)S(1)} collective-permute-done((bf16[480,128]{1,0:T(8,128)(2,1)S(1)}, bf16[480,128]{1,0:T(8,128)(2,1)S(1)}, u32[]{:S(2)}, u32[]{:S(2)}) %collective-permute-start.14) | collective-permute-done | bytes 122912 | tf_op jit(solution)/shard_map/ppermute | solution.py:350
  54.9 2.0 %collective-permute-done.13.refs_1_ = bf16[480,128]{1,0:T(8,128)(2,1)S(1)} collective-permute-done((bf16[480,128]{1,0:T(8,128)(2,1)S(1)}, bf16[480,128]{1,0:T(8,128)(2,1)S(1)}, u32[]{:S(2)}, u32[]{:S(2)}) %collective-permute-start.13) | collective-permute-done | bytes 122912 | tf_op jit(solution)/shard_map/ppermute | solution.py:350
  56.9 1.0 %finish.1 = bf16[15,30,128]{2,1,0:T(8,128)(2,1)} custom-call(f32[480,128]{1,0:T(8,128)S(1)} %get-tuple-element.48.refs_0_, bf16[480,128]{1,0:T(8,128)(2,1)S(1)} %collective-permute-done.13.refs_1_, bf16[480,128]{1,0:T(8,128)(2,1)S(1)} %collective-permute-done.14.refs_2_, bf16[480,128]{1,0:T(8,128)(2,1)S(1)} %collective-permute-done.15.refs_3_, ...), custom_call_target="tpu_custom_call" | custom-call | flops 10000000 | bytes 2089472 | tf_op jit(solution)/shard_map/finish/pallas_call | solution.py:329
  (38 shorter events, 7.9 us)
Async XLA Ops:
  0.6 0.9 %copy-start = (bf16[128,512]{1,0:T(8,128)(2,1)S(1)}, bf16[128,512]{1,0:T(8,128)(2,1)}, u32[]{:S(2)}) copy-start(bf16[128,512]{1,0:T(8,128)(2,1)} %refs_6_.3) | copy-start | bytes 393220
  1.5 0.9 %copy-start.2 = (bf16[15,30,128]{2,1,0:T(8,128)(2,1)S(1)}, bf16[15,30,128]{2,1,0:T(8,128)(2,1)}, u32[]{:S(2)}) copy-start(bf16[15,30,128]{2,1,0:T(8,128)(2,1)} %x_ref.3) | copy-start | bytes 345604
  3.1 6.6 %copy-start.5 = (bf16[15,30,128]{2,1,0:T(8,128)(2,1)S(1)}, bf16[15,30,128]{2,1,0:T(8,128)(2,1)}, u32[]{:S(2)}) copy-start(bf16[15,30,128]{2,1,0:T(8,128)(2,1)} %cot_ref) | copy-start | bytes 345604
  3.1 8.2 %copy-start.1 = (bf16[128,512]{1,0:T(8,128)(2,1)S(1)}, bf16[128,512]{1,0:T(8,128)(2,1)}, u32[]{:S(2)}) copy-start(bf16[128,512]{1,0:T(8,128)(2,1)} %refs_6_.3) | copy-start | bytes 393220
  3.1 8.2 %copy-start.4 = (bf16[128,128]{1,0:T(8,128)(2,1)S(1)}, bf16[128,128]{1,0:T(8,128)(2,1)}, u32[]{:S(2)}) copy-start(bf16[128,128]{1,0:T(8,128)(2,1)} %wg_ref.3) | copy-start | bytes 98308
  4.0 8.8 %collective-permute-start.2 = (bf16[480,128]{1,0:T(8,128)(2,1)S(1)}, bf16[480,128]{1,0:T(8,128)(2,1)S(1)}, u32[]{:S(2)}, u32[]{:S(2)}) collective-permute-start(bf16[480,128]{1,0:T(8,128)(2,1)S(1)} %right.1.refs_1_.refs_5_), channel_id=1, source_target_pairs={{0,8},{4,12},{8,0},{12,4},{16,24},{20,28},{24,16},{28,20},{1,9},{5... | collective-permute-start | bytes 368648 | tf_op jit(solution)/shard_map/ppermute | solution.py:350
  7.1 9.4 %collective-permute-start.4 = (bf16[480,128]{1,0:T(8,128)(2,1)S(1)}, bf16[480,128]{1,0:T(8,128)(2,1)S(1)}, u32[]{:S(2)}, u32[]{:S(2)}) collective-permute-start(bf16[480,128]{1,0:T(8,128)(2,1)S(1)} %right.1.refs_1_.refs_5_), channel_id=1, source_target_pairs={{0,24},{4,28},{8,16},{12,20},{16,8},{20,12},{24,0},{28,4},{1,25},{... | collective-permute-start | bytes 368648 | tf_op jit(solution)/shard_map/ppermute | solution.py:350
  9.6 11.1 %collective-permute-start.3 = (bf16[480,128]{1,0:T(8,128)(2,1)S(1)}, bf16[480,128]{1,0:T(8,128)(2,1)S(1)}, u32[]{:S(2)}, u32[]{:S(2)}) collective-permute-start(bf16[480,128]{1,0:T(8,128)(2,1)S(1)} %right.1.refs_1_.refs_5_), channel_id=1, source_target_pairs={{0,16},{4,20},{8,24},{12,28},{16,0},{20,4},{24,8},{28,12},{1,17},{... | collective-permute-start | bytes 368648 | tf_op jit(solution)/shard_map/ppermute | solution.py:350
  9.7 1.3 %collective-permute-start.1 = (bf16[15,30,128]{2,1,0:T(8,128)(2,1)S(1)}, bf16[15,30,128]{2,1,0:T(8,128)(2,1)S(1)}, u32[]{:S(2)}, u32[]{:S(2)}) collective-permute-start(bf16[15,30,128]{2,1,0:T(8,128)(2,1)S(1)} %copy-done.5), channel_id=1, source_target_pairs={{0,4},{4,0},{8,12},{12,8},{16,20},{20,16},{24,28},{28,24},{1,5},{5... | collective-permute-start | bytes 345608 | tf_op jit(solution)/shard_map/ppermute | solution.py:356
  9.7 1.5 %collective-permute-start = (bf16[15,30,128]{2,1,0:T(8,128)(2,1)S(1)}, bf16[15,30,128]{2,1,0:T(8,128)(2,1)S(1)}, u32[]{:S(2)}, u32[]{:S(2)}) collective-permute-start(bf16[15,30,128]{2,1,0:T(8,128)(2,1)S(1)} %copy-done.2), channel_id=1, source_target_pairs={{0,4},{4,0},{8,12},{12,8},{16,20},{20,16},{24,28},{28,24},{1,5},{5... | collective-permute-start | bytes 345608 | tf_op jit(solution)/shard_map/ppermute | solution.py:356
  20.7 10.5 %copy-start.6 = (bf16[128,128]{1,0:T(8,128)(2,1)S(1)}, bf16[128,128]{1,0:T(8,128)(2,1)}, u32[]{:S(2)}) copy-start(bf16[128,128]{1,0:T(8,128)(2,1)} %refs_6_.2) | copy-start | bytes 98308
  22.1 5.5 %collective-permute-start.5 = (bf16[480,128]{1,0:T(8,128)(2,1)S(1)}, bf16[480,128]{1,0:T(8,128)(2,1)S(1)}, u32[]{:S(2)}, u32[]{:S(2)}) collective-permute-start(bf16[480,128]{1,0:T(8,128)(2,1)S(1)} %get-tuple-element.33), channel_id=1, source_target_pairs={{0,1},{1,0},{2,3},{3,2},{4,5},{5,4},{6,7},{7,6},{8,9},{9,8},{10,11... | collective-permute-start | bytes 368648 | tf_op jit(solution)/shard_map/ppermute | solution.py:353
  23.7 7.5 %collective-permute-start.6 = (bf16[480,128]{1,0:T(8,128)(2,1)S(1)}, bf16[480,128]{1,0:T(8,128)(2,1)S(1)}, u32[]{:S(2)}, u32[]{:S(2)}) collective-permute-start(bf16[480,128]{1,0:T(8,128)(2,1)S(1)} %get-tuple-element.34), channel_id=1, source_target_pairs={{0,2},{1,3},{2,0},{3,1},{4,6},{5,7},{6,4},{7,5},{8,10},{9,11},{10,... | collective-permute-start | bytes 368648 | tf_op jit(solution)/shard_map/ppermute | solution.py:353
  25.2 6.0 %collective-permute-start.7 = (bf16[480,128]{1,0:T(8,128)(2,1)S(1)}, bf16[480,128]{1,0:T(8,128)(2,1)S(1)}, u32[]{:S(2)}, u32[]{:S(2)}) collective-permute-start(bf16[480,128]{1,0:T(8,128)(2,1)S(1)} %get-tuple-element.35), channel_id=1, source_target_pairs={{0,3},{1,2},{2,1},{3,0},{4,7},{5,6},{6,5},{7,4},{8,11},{9,10},{10,... | collective-permute-start | bytes 368648 | tf_op jit(solution)/shard_map/ppermute | solution.py:353
  31.7 5.9 %collective-permute-start.10 = (bf16[480,128]{1,0:T(8,128)(2,1)S(1)}, bf16[480,128]{1,0:T(8,128)(2,1)S(1)}, u32[]{:S(2)}, u32[]{:S(2)}) collective-permute-start(bf16[480,128]{1,0:T(8,128)(2,1)S(1)} %get-tuple-element.38.refs_1_), channel_id=1, source_target_pairs={{0,3},{1,2},{2,1},{3,0},{4,7},{5,6},{6,5},{7,4},{8,11},{9,10},{10,... | collective-permute-start | bytes 368648 | tf_op jit(solution)/shard_map/ppermute | solution.py:353
  32.7 6.1 %collective-permute-start.9 = (bf16[480,128]{1,0:T(8,128)(2,1)S(1)}, bf16[480,128]{1,0:T(8,128)(2,1)S(1)}, u32[]{:S(2)}, u32[]{:S(2)}) collective-permute-start(bf16[480,128]{1,0:T(8,128)(2,1)S(1)} %get-tuple-element.38.refs_1_), channel_id=1, source_target_pairs={{0,2},{1,3},{2,0},{3,1},{4,6},{5,7},{6,4},{7,5},{8,10},{9,11},{10,... | collective-permute-start | bytes 368648 | tf_op jit(solution)/shard_map/ppermute | solution.py:353
  33.9 4.9 %collective-permute-start.8 = (bf16[480,128]{1,0:T(8,128)(2,1)S(1)}, bf16[480,128]{1,0:T(8,128)(2,1)S(1)}, u32[]{:S(2)}, u32[]{:S(2)}) collective-permute-start(bf16[480,128]{1,0:T(8,128)(2,1)S(1)} %get-tuple-element.38.refs_1_), channel_id=1, source_target_pairs={{0,1},{1,0},{2,3},{3,2},{4,5},{5,4},{6,7},{7,6},{8,9},{9,8},{10,11... | collective-permute-start | bytes 368648 | tf_op jit(solution)/shard_map/ppermute | solution.py:353
  35.2 13.2 %collective-permute-start.12 = (bf16[480,128]{1,0:T(8,128)(2,1)S(1)}, bf16[480,128]{1,0:T(8,128)(2,1)S(1)}, u32[]{:S(2)}, u32[]{:S(2)}) collective-permute-start(bf16[480,128]{1,0:T(8,128)(2,1)S(1)} %get-tuple-element.46), channel_id=1, source_target_pairs={{0,4},{4,0},{8,12},{12,8},{16,20},{20,16},{24,28},{28,24},{1,5},{5... | collective-permute-start | bytes 368648 | tf_op jit(solution)/shard_map/ppermute | solution.py:356
  42.4 6.1 %collective-permute-start.11 = (bf16[480,128]{1,0:T(8,128)(2,1)S(1)}, bf16[480,128]{1,0:T(8,128)(2,1)S(1)}, u32[]{:S(2)}, u32[]{:S(2)}) collective-permute-start(bf16[480,128]{1,0:T(8,128)(2,1)S(1)} %get-tuple-element.41), channel_id=1, source_target_pairs={{0,4},{4,0},{8,12},{12,8},{16,20},{20,16},{24,28},{28,24},{1,5},{5... | collective-permute-start | bytes 368648 | tf_op jit(solution)/shard_map/ppermute | solution.py:356
  43.1 4.2 %copy-start.3 = (bf16[15,30,128]{2,1,0:T(8,128)(2,1)S(1)}, bf16[15,30,128]{2,1,0:T(8,128)(2,1)}, u32[]{:S(2)}) copy-start(bf16[15,30,128]{2,1,0:T(8,128)(2,1)} %x_ref.3) | copy-start | bytes 345604
  43.1 4.2 %copy-start.8 = (s32[120]{0:T(128)S(1)}, s32[120]{0:T(128)}, u32[]{:S(2)}) copy-start(s32[120]{0:T(128)} %mask_ref.5) | copy-start | bytes 1444
  43.1 11.8 %collective-permute-start.14 = (bf16[480,128]{1,0:T(8,128)(2,1)S(1)}, bf16[480,128]{1,0:T(8,128)(2,1)S(1)}, u32[]{:S(2)}, u32[]{:S(2)}) collective-permute-start(bf16[480,128]{1,0:T(8,128)(2,1)S(1)} %send_right.4), channel_id=1, source_target_pairs={{0,16},{4,20},{8,24},{12,28},{16,0},{20,4},{24,8},{28,12},{1,17},{... | collective-permute-start | bytes 368648 | tf_op jit(solution)/shard_map/ppermute | solution.py:350
  43.8 11.1 %collective-permute-start.15 = (bf16[480,128]{1,0:T(8,128)(2,1)S(1)}, bf16[480,128]{1,0:T(8,128)(2,1)S(1)}, u32[]{:S(2)}, u32[]{:S(2)}) collective-permute-start(bf16[480,128]{1,0:T(8,128)(2,1)S(1)} %send_right.5), channel_id=1, source_target_pairs={{0,24},{4,28},{8,16},{12,20},{16,8},{20,12},{24,0},{28,4},{1,25},{... | collective-permute-start | bytes 368648 | tf_op jit(solution)/shard_map/ppermute | solution.py:350
  46.3 10.6 %collective-permute-start.13 = (bf16[480,128]{1,0:T(8,128)(2,1)S(1)}, bf16[480,128]{1,0:T(8,128)(2,1)S(1)}, u32[]{:S(2)}, u32[]{:S(2)}) collective-permute-start(bf16[480,128]{1,0:T(8,128)(2,1)S(1)} %send_right.3), channel_id=1, source_target_pairs={{0,8},{4,12},{8,0},{12,4},{16,24},{20,28},{24,16},{28,20},{1,9},{5... | collective-permute-start | bytes 368648 | tf_op jit(solution)/shard_map/ppermute | solution.py:350
  (1 other events, 0.7 us)

commit v3 on v2

--- a/solution.py
+++ b/solution.py
@@ -7,10 +7,10 @@
 from jax.experimental.pallas import tpu as pltpu
 from jax.sharding import PartitionSpec as P
 
+
 EPSILON = 1e-05
 F32 = jnp.float32
 BF16 = jnp.bfloat16
-EARLY = 2
 JB = 5
 
 
@@ -39,12 +39,27 @@
     return lax.dot_general(a, b, (((1,), (1,)), ((), ())), preferred_element_type=F32)
 
 
-def col_mask(mask_ref, start, count, pitch, channels):
-    row = lax.broadcasted_iota(jnp.int32, (pitch, channels), 0)
-    flags = jnp.zeros((pitch, channels), F32)
-    for k in range(count):
-        flags = jnp.where(row == k, mask_ref[start + k].astype(F32), flags)
-    return flags
+def load_kernel(*refs):
+    count = len(refs) // 2 - 1
+    sources, outs, (sems, flags) = refs[:count], refs[count : 2 * count], refs[2 * count :]
+    live_ref = outs[-1]
+    copies = [pltpu.make_async_copy(sources[0], flags, sems.at[0])]
+    copies += [pltpu.make_async_copy(a, b, sems.at[n + 1]) for n, (a, b) in enumerate(zip(sources[1:], outs[:-1]))]
+    for copy in copies:
+        copy.start()
+    copies[0].wait()
+    residues, total = flags.shape[0], live_ref.shape[0]
+    for r in range(residues):
+        live_ref[r : r + 1, :] = jnp.full((1, live_ref.shape[1]), flags[r].astype(F32))
+    live_ref[residues:, :] = jnp.zeros((total - residues, live_ref.shape[1]), F32)
+    for copy in copies[1:]:
+        copy.wait()
+
+
+def live_rows(live_ref, start, first, rows, pitch):
+    columns = tiles(live_ref[pl.ds(first, pitch), :])
+    for i in range(rows):
+        yield i, (columns * row_of(live_ref, start + i)[None]).reshape(pitch, columns.shape[2])
 
 
 def load_cells(cells_ref, scratch, first):
@@ -65,23 +80,7 @@
     return value.reshape(value.shape[0] // 8, 8, value.shape[1])
 
 
-def right_kernel(mask_ref, x_ref, w_ref, out_ref, xs):
-    rows, cols, channels = x_ref.shape
-    pitch = pad_to(cols, 16)
-    hidden = w_ref.shape[1] // 4
-    load_cells(x_ref, xs, 0)
-    normed, _ = normalize(xs[...])
-    projected = matmul(normed.astype(BF16), w_ref[:, 2 * hidden :])
-    right = jax.nn.sigmoid(projected[:, :hidden]) * projected[:, hidden:]
-    flags = col_mask(mask_ref, lax.axis_index("ch") * cols, cols, pitch, hidden)
-    start = lax.axis_index("dap") * rows
-    for i in range(rows):
-        block = slice(i * pitch, (i + 1) * pitch)
-        live = flags * mask_ref[start + i].astype(F32)
-        out_ref[block, :] = (right[block] * live).astype(BF16)
-
-
-def left_kernel(mask_ref, x_ref, xp_ref, cot_ref, cotp_ref, w_ref, wg_ref,
+def left_kernel(live_ref, x_ref, xp_ref, cot_ref, cotp_ref, w_ref, wg_ref,
                 l_ref, lt_ref, gate_ref, cotm_ref, xs, ls, gs):
     rows, cols, channels = x_ref.shape
     pitch = pad_to(cols, 16)
@@ -95,14 +94,12 @@
     normed_half = normed.astype(BF16)
     projected = matmul(normed_half, w_ref[:, : 2 * hidden])
     left = jax.nn.sigmoid(projected[:, :hidden]) * projected[:, hidden:]
-    flags = col_mask(mask_ref, lax.axis_index("ch") * cols, cols, pitch, hidden)
-    for i in range(2 * rows):
-        owner = dap if i < rows else dap + 1 - 2 * core
-        block = slice(i * pitch, (i + 1) * pitch)
-        live = flags * mask_ref[owner * rows + i % rows].astype(F32)
-        value = (left[block] * live).astype(BF16).astype(F32)
-        l_ref[block, :] = value
-        ls[block, :] = value
+    for part, owner in enumerate((dap, dap + 1 - 2 * core)):
+        for i, live in live_rows(live_ref, owner * rows, lax.axis_index("ch") * cols, rows, pitch):
+            block = slice((part * rows + i) * pitch, (part * rows + i + 1) * pitch)
+            value = (left[block] * live).astype(BF16).astype(F32)
+            l_ref[block, :] = value
+            ls[block, :] = value
     tall = pad_to(2 * rows, 16)
     ls[2 * rows * pitch :, :] = jnp.zeros(((tall - 2 * rows) * pitch, hidden), F32)
     for k in range(cols):
@@ -123,8 +120,8 @@
     pick(cotm_ref)
 
 
-def factor_kernel(mask_ref, x_ref, w_ref, normed_ref, scale_ref, l1_ref, l2_ref, r1_ref, r2_ref, xs):
-    rows, cols, channels = x_ref.shape
+def factor_kernel(live_ref, x_ref, w_ref, normed_ref, scale_ref, l1_ref, l2_ref, r1_ref, r2_ref, xs):
+    rows, cols, _ = x_ref.shape
     pitch = pad_to(cols, 16)
     hidden = w_ref.shape[1] // 4
     load_cells(x_ref, xs, 0)
@@ -136,20 +133,17 @@
     right_sig = jax.nn.sigmoid(projected[:, 2 * hidden : 3 * hidden])
     left_in = projected[:, hidden : 2 * hidden] * left_sig * (1.0 - left_sig)
     right_in = projected[:, 3 * hidden :] * right_sig * (1.0 - right_sig)
-    flags = col_mask(mask_ref, lax.axis_index("ch") * cols, cols, pitch, hidden)
     start = lax.axis_index("dap") * rows
-    for i in range(rows):
+    for i, live in live_rows(live_ref, start, lax.axis_index("ch") * cols, rows, pitch):
         block = slice(i * pitch, (i + 1) * pitch)
-        live = flags * mask_ref[start + i].astype(F32)
         l1_ref[block, :] = left_in[block] * live
         l2_ref[block, :] = left_sig[block] * live
         r1_ref[block, :] = right_in[block] * live
         r2_ref[block, :] = right_sig[block] * live
 
 
-def product_part(lt_ref, r_ref, rs, out, rows, cols):
+def product_part(lt_ref, rs, out, rows, cols):
     pitch, half, tall = pad_to(cols, 16), pad_to(rows, 16), pad_to(2 * rows, 16)
-    rs[...] = r_ref[...].astype(F32)
 
     def step(b, _):
         sums = [jnp.zeros((tall // 8, 8, rs.shape[1]), F32) for _ in range(JB)]
@@ -164,27 +158,44 @@
     lax.fori_loop(0, rows // JB, step, 0)
 
 
-def early_kernel(rows, cols, count, *refs):
-    lt_ref, shards = refs[0], refs[1 : 1 + count]
-    out_ref, rs, ps = refs[1 + count :]
-    for s in range(count):
-        product_part(lt_ref, shards[s], rs, ps, rows, cols)
-        out_ref[s] = ps[: out_ref.shape[1], :].astype(BF16)
-
-
-def late_kernel(rows, cols, blocks, early, *refs):
-    lt_ref, early_ref = refs[:2]
-    shards = refs[2 : 2 + blocks - early]
-    outs = refs[2 + blocks - early : 2 + 2 * blocks - early]
-    rs, ps, held = refs[2 + 2 * blocks - early :]
-    chip, column = lax.axis_index("dap") // 2, lax.axis_index("ch")
-    for s in range(early):
-        held[s] = early_ref[s]
-    for s in range(early, blocks):
-        product_part(lt_ref, shards[s - early], rs, ps, rows, cols)
-        held[s] = ps[: held.shape[1], :].astype(BF16)
+def right_of(live_ref, x_ref, w_ref, xs, rs, r_ref, s):
+    rows, cols, _ = x_ref.shape
+    pitch = pad_to(cols, 16)
+    hidden = w_ref.shape[1] // 4
+    load_cells(x_ref, xs, 0)
+    normed, _ = normalize(xs[...])
+    projected = matmul(normed.astype(BF16), w_ref[:, 2 * hidden :])
+    right = jax.nn.sigmoid(projected[:, :hidden]) * projected[:, hidden:]
+    start = (lax.axis_index("dap") ^ (2 * s)) * rows
+    for i, live in live_rows(live_ref, start, lax.axis_index("ch") * cols, rows, pitch):
+        block = slice(i * pitch, (i + 1) * pitch)
+        value = (right[block] * live).astype(BF16)
+        r_ref[block, :] = value
+        rs[block, :] = value.astype(F32)
+
+
+def part_kernel(step, live_ref, lt_ref, w_ref, shard, right_ref, part_ref, xs, rs, ps):
+    rows, cols, _ = shard.shape
+    right_of(live_ref, shard, w_ref, xs, rs, right_ref, step)
+    product_part(lt_ref, rs, ps, rows, cols)
+    part_ref[...] = ps[: part_ref.shape[0], :].astype(BF16)
+
+
+def late_kernel(blocks, step, *refs):
+    live_ref, lt_ref, w_ref, shard = refs[:4]
+    done = refs[4 : 3 + blocks]
+    right_ref, outs = refs[3 + blocks], refs[4 + blocks : 4 + 2 * blocks]
+    xs, rs, ps, held = refs[4 + 2 * blocks :]
+    rows, cols, _ = shard.shape
+    for s in range(blocks):
+        if s != step:
+            held[s] = done[s - (s > step)][...]
+    right_of(live_ref, shard, w_ref, xs, rs, right_ref, step)
+    product_part(lt_ref, rs, ps, rows, cols)
+    held[step] = ps[: held.shape[1], :].astype(BF16)
+    turn = (lax.axis_index("dap") // 2) ^ lax.axis_index("ch")
     for t in range(blocks):
-        outs[t][...] = held[chip ^ column ^ t]
+        outs[t][...] = held[turn ^ t]
 
 
 def middle_kernel(blocks, *refs):
@@ -320,20 +331,20 @@
 
 
 VMEM = pl.BlockSpec(memory_space=pltpu.VMEM)
-SMEM = pl.BlockSpec(memory_space=pltpu.SMEM)
-
-
-def call(body, name, outs, args, scratch=(), smem=0, flops=10**7, limit=20):
+HBM = pl.BlockSpec(memory_space=pltpu.HBM)
+
+
+def call(body, outs, args, scratch=(), specs=VMEM, flops=10**7):
     outs = [jax.ShapeDtypeStruct(shape, dtype) for shape, dtype in outs]
-    moved = sum(a.size * a.dtype.itemsize for a in list(args) + outs)
+    moved = sum(a.size * a.dtype.itemsize for a in [*args, *outs])
+    scratch = [pltpu.VMEM(shape, F32) if isinstance(shape, tuple) else shape for shape in scratch]
     return pl.pallas_call(
         body,
-        name=name,
         out_shape=outs,
-        in_specs=[SMEM] * smem + [VMEM] * (len(args) - smem),
+        in_specs=[specs] * len(args),
         out_specs=[VMEM] * len(outs),
-        scratch_shapes=[pltpu.VMEM(shape[:-1], BF16) if shape[-1] is None else pltpu.VMEM(shape, F32) for shape in scratch],
-        compiler_params=pltpu.CompilerParams(vmem_limit_bytes=limit << 20),
+        scratch_shapes=scratch,
+        compiler_params=pltpu.CompilerParams(vmem_limit_bytes=20 << 20),
         cost_estimate=pl.CostEstimate(flops=flops, bytes_accessed=moved, transcendentals=0),
     )(*args)
 
@@ -355,56 +366,76 @@
     def to_partner(value):
         return lax.ppermute(value, "dap", [(d, d ^ 1) for d in range(devices)])
 
-    (right,) = call(right_kernel, "right", [((cells, hidden), BF16)], (mask, x, w_proj),
-                    [(cells, channels)], smem=1)
-    shards = [right] + [along_dap(right, s) for s in range(1, blocks)]
-    x_late, cot_late, _ = lax.optimization_barrier((x, cot, right))
-    x_pair, cot_pair = to_partner(x_late), to_partner(cot_late)
+    last = blocks - 1
+    shards = [x] + [None] * last
+    for s in dap_order(blocks):
+        direct = s == 1 or s % 2 == 0
+        shards[s] = along_dap(x if direct else shards[s ^ 1], s if direct else 1)
+    x_pair, cot_pair = to_partner(x), to_partner(cot)
+    sources = (x, cot, w_proj, w_gate, w_out)
+    residues = mask.shape[0]
+    xv, cotv, w_proj, w_gate, w_out, live = call(
+        load_kernel,
+        [(a.shape, a.dtype) for a in sources] + [((pad_to(residues + pitch - cols, 8), channels), F32)],
+        [pltpu.with_memory_space_constraint(a, pltpu.HBM) for a in (mask, *sources)], [pltpu.SemaphoreType.DMA((6,)), pltpu.SMEM((residues,), jnp.int32)], specs=HBM)
     left, left_t, gate, upstream = call(
-        left_kernel, "left",
+        left_kernel,
         [((wide, hidden), F32), ((cols * tall, hidden), F32), ((mids, channels), F32), ((mids, channels), F32)],
-        (mask, x_late, x_pair, cot_late, cot_pair, w_proj, w_gate),
-        [(wide, channels), (tall * pitch, hidden), (wide, channels)], smem=1)
-    normed, scale, l1, l2, r1, r2 = call(
-        factor_kernel, "factor", [((cells, hidden), F32)] * 6, (mask, x_late, w_proj),
-        [(cells, channels)], smem=1)
-    early = min(EARLY, blocks)
-    (started,) = call(functools.partial(early_kernel, rows, cols, early), "early",
-                      [((early, mids, hidden), BF16)], (left_t, *shards[:early]), [(cells, hidden), (tall * half, hidden)])
-    parts = call(functools.partial(late_kernel, rows, cols, blocks, early), "late",
-                 [((mids, hidden), BF16)] * blocks,
-                 (left_t, started, *shards[early:]),
-                 [(cells, hidden), (tall * half, hidden), (blocks, mids, hidden, None)])
-    parts = [parts[0]] + [along_ch(parts[t], t) for t in range(1, blocks)]
+        (live, xv, x_pair, cotv, cot_pair, w_proj, w_gate),
+        [(wide, channels), (tall * pitch, hidden), (wide, channels)])
+    scratch = [(cells, channels), (cells, hidden), (tall * half, hidden)]
+    rights, done = [None] * blocks, []
+    for s in range(last):
+        rights[s], part = call(
+            functools.partial(part_kernel, s), [((cells, hidden), BF16), ((mids, hidden), BF16)],
+            (live, left_t, w_proj, shards[s] if s else xv), scratch)
+        done.append(part)
+    rights[last], *parts = call(
+        functools.partial(late_kernel, blocks, last),
+        [((cells, hidden), BF16)] + [((mids, hidden), BF16)] * blocks,
+        (live, left_t, w_proj, shards[last], *done), scratch + [pltpu.VMEM((blocks, mids, hidden), BF16)])
+    for t in range(1, blocks):
+        parts[t] = along_ch(parts[t], t)
     update, back, logit, grad_product = call(
-        functools.partial(middle_kernel, blocks), "middle",
+        functools.partial(middle_kernel, blocks),
         [((mids // 2, channels), BF16), ((mids, channels), BF16), ((mids // 2, channels), BF16), ((mids, hidden), BF16)],
         (*parts, gate, upstream, w_out))
     pieces = [grad_product] + [along_ch(grad_product, t) for t in range(1, blocks)]
     back = to_partner(back)
     gots = [None] * blocks
-    for s in [*range(2, blocks), 1]:
-        (send,) = call(functools.partial(send_right_kernel, rows, cols, blocks, s), "send_right",
+    for s in range(1, blocks):
+        (send,) = call(functools.partial(send_right_kernel, rows, cols, blocks, s),
                        [((cells, hidden), BF16)], (left, *pieces), [(mids, hidden)])
         gots[s] = along_dap(send, s)
-    left_late, _ = lax.optimization_barrier((left, send))
     left_own, left_send, right_own = call(
-        functools.partial(grad_left_kernel, rows, cols, blocks), "grad_left",
+        functools.partial(grad_left_kernel, rows, cols, blocks),
         [((cells, hidden), F32), ((cells, hidden), BF16), ((cells, hidden), F32)],
-        (left_late, *pieces, *shards), [(blocks, mids, hidden), (blocks, cells, hidden)])
+        (left, *pieces, *rights), [(blocks, mids, hidden), (blocks, cells, hidden)])
     left_got = to_partner(left_send)
+    normed, scale, l1, l2, r1, r2 = call(
+        factor_kernel, [((cells, hidden), F32)] * 6, (live, xv, w_proj),
+        [(cells, channels)])
     pair_update, acc = call(
-        finish_left_kernel, "finish_left", [((rows, cols, channels), BF16), ((cells, channels), F32)],
+        finish_left_kernel, [((rows, cols, channels), BF16), ((cells, channels), F32)],
         (left_own, left_got, l1, l2, w_proj, w_gate, update, logit, back),
         [(cells, channels), (cells, channels)])
-    (grad_pair,) = call(functools.partial(finish_kernel, blocks), "finish", [((rows, cols, channels), BF16)],
+    (grad_pair,) = call(functools.partial(finish_kernel, blocks), [((rows, cols, channels), BF16)],
                         (right_own, *gots[1:], r1, r2, w_proj, acc, normed, scale))
     return pair_update, grad_pair
 
 
+def dap_order(blocks):
+    return [*range(2, blocks, 2), 1, *range(3, blocks, 2)]
+
+
 def solution(mesh):
+    blocks = mesh.shape["ch"]
+
+    def body(*args):
+        return on_device(mesh.shape["dap"], blocks, *args)
+
     return jax.shard_map(
-        functools.partial(on_device, mesh.shape["dap"], mesh.shape["ch"]),
+        body,
         mesh=mesh,
         in_specs=(P("dap", "ch", None), P(), P(), P(), P(), P("dap", "ch", None)),
         out_specs=(P("dap", "ch", None), P("dap", "ch", None)),

time: 58.1 us -> 54.4 us (0.936); the launches traced: 57.9 us -> 53.4 us
  waiting for transfers between devices: 24.1 us -> 19.9 us
  local copies, waits for them, and re-layouts: 2.48 us -> 0 us
  starting transfers between devices: 17 us -> 19.2 us
    ppermute x6, waiting for transfers between devices: 14 us -> 10.4 us  [along_dap(): return lax.ppermute(value, 'dap', [(d, d ^ 2 * s) for d in range(devices)])]
    unnamed x18 -> x0, local copies, waits for them, and re-layouts: 2.48 us -> none
    ppermute x6, starting transfers between devices: 9.29 us -> 11.5 us  [along_dap(): return lax.ppermute(value, 'dap', [(d, d ^ 2 * s) for d in range(devices)])]
    ppermute x4, waiting for transfers between devices: 1.01 us -> 0.01 us  [to_partner(): return lax.ppermute(value, 'dap', [(d, d ^ 1) for d in range(devices)])]
    pallas_call x12 -> x14, Pallas kernels: 13.5 us -> 13.6 us  [call(): pl.pallas_call(body, out_shape=outs, in_specs=[specs] * len(args), out_sp...]
  transfers between devices with their start and end apart: 16 -> 16, of which waited for: 10 -> 8; matrix products, arithmetic and copies ran while one was open for 0% -> 0% of each run, Pallas kernels for 17% -> 21%
where the time goes in v3:
time: 54.4 us; the launch traced here: 53.4 us
  waiting for transfers between devices  19.9 us (37%)
  starting transfers between devices  19.2 us (35%)
  Pallas kernels  13.6 us (25%)
  between operations  0.77 us (1%)
    pallas_call x14, Pallas kernels, call(): pl.pallas_call(body, out_shape=outs, in_specs=[specs] * len(args), out_sp...  13.6 us
    ppermute x6, starting transfers between devices, along_dap(): return lax.ppermute(value, 'dap', [(d, d ^ 2 * s) for d in range(devices)])  11.5 us
    ppermute x6, waiting for transfers between devices, along_dap(): return lax.ppermute(value, 'dap', [(d, d ^ 2 * s) for d in range(devices)])  10.4 us
    ppermute x6, waiting for transfers between devices, along_ch(): return lax.ppermute(value, 'ch', [(h, h ^ t) for h in range(blocks)])  9.42 us
    ppermute x6, starting transfers between devices, along_ch(): return lax.ppermute(value, 'ch', [(h, h ^ t) for h in range(blocks)])  7.11 us
  transfers between devices with their start and end apart: 16, of which 8 were waited for; matrix products, arithmetic and copies ran while one was open for 0% of the time, Pallas kernels for 21%

profile of v3, /device:TPU:0, one launch (start us, length us, event | category | flops | bytes accessed | tf_op | source)
XLA Modules:
  0.0 53.4 jit_solution(10224335139720579997)
XLA Ops:
  0.6 4.1 %collective-permute-start.2 = (bf16[15,30,128]{2,1,0:T(8,128)(2,1)}, bf16[15,30,128]{2,1,0:T(8,128)(2,1)S(1)}, u32[]{:S(2)}, u32[]{:S(2)}) collective-permute-start(bf16[15,30,128]{2,1,0:T(8,128)(2,1)} %refs_1_.1), channel_id=1, source_target_pairs={{0,16},{4,20},{8,24},{12,28},{16,0},{20,4},{24,8},{28,12},{1,17},{... | collective-permute-start | bytes 345608 | tf_op jit(solution)/shard_map/ppermute | solution.py:361
  5.3 1.6 %collective-permute-start.4 = (bf16[15,30,128]{2,1,0:T(8,128)(2,1)}, bf16[15,30,128]{2,1,0:T(8,128)(2,1)S(1)}, u32[]{:S(2)}, u32[]{:S(2)}) collective-permute-start(bf16[15,30,128]{2,1,0:T(8,128)(2,1)} %refs_1_.1), channel_id=1, source_target_pairs={{0,8},{4,12},{8,0},{12,4},{16,24},{20,28},{24,16},{28,20},{1,9},{5... | collective-permute-start | bytes 345608 | tf_op jit(solution)/shard_map/ppermute | solution.py:361
  6.8 4.2 %collective-permute-done.2.shard = bf16[15,30,128]{2,1,0:T(8,128)(2,1)S(1)} collective-permute-done((bf16[15,30,128]{2,1,0:T(8,128)(2,1)}, bf16[15,30,128]{2,1,0:T(8,128)(2,1)S(1)}, u32[]{:S(2)}, u32[]{:S(2)}) %collective-permute-start.2) | collective-permute-done | bytes 115232 | tf_op jit(solution)/shard_map/ppermute | solution.py:361
  11.8 1.1 %shard_map.77 = (bf16[15,30,128]{2,1,0:T(8,128)(2,1)S(1)}, bf16[15,30,128]{2,1,0:T(8,128)(2,1)S(1)}, bf16[128,512]{1,0:T(8,128)(2,1)S(1)}, bf16[128,128]{1,0:T(8...) custom-call(s32[120]{0:T(128)} %refs_0_.1, bf16[15,30,128]{2,1,0:T(8,128)(2,1)} %refs_1_.1, ...), custom_call_target="tpu_custom_call" | custom-call | flops 10000000 | bytes 920032 | tf_op jit(solution)/shard_map/pallas_call | solution.py:341
  12.9 1.0 %shard_map.78 = (f32[960,128]{1,0:T(8,128)S(1)}, f32[960,128]{1,0:T(8,128)S(1)}, f32[480,128]{1,0:T(8,128)S(1)}, f32[480,128]{1,0:T(8,128)S(1)}) custom-call(f32[128,128]{1,0:T(8,128)S(1)} %get-tuple-element.38.live_ref.refs_0_, bf16[15,30,128]{2,1,0:T(8,128)(2,1)S(1)} %get-tuple-element.39.x_ref.shard, ...), custom_call_target="tpu_custom_call" | custom-call | flops 10000000 | bytes 2164736 | tf_op jit(solution)/shard_map/pallas_call | solution.py:341
  13.9 1.0 %shard_map.79 = (bf16[480,128]{1,0:T(8,128)(2,1)S(1)}, bf16[480,128]{1,0:T(8,128)(2,1)S(1)}) custom-call(f32[128,128]{1,0:T(8,128)S(1)} %get-tuple-element.38.live_ref.refs_0_, f32[960,128]{1,0:T(8,128)S(1)} %get-tuple-element.44.lt_ref.refs_1_, bf16[128,512]{1,0:T(8,128)(2,1)S(1)} %get-tuple-element.41.w_ref.refs_2_.refs_6_, ...), custom_call_target="tpu_custom_call" | custom-call | flops 10000000 | bytes 1049088 | tf_op jit(solution)/shard_map/pallas_call | solution.py:341
  14.9 1.0 %shard_map.81 = (bf16[480,128]{1,0:T(8,128)(2,1)S(1)}, bf16[480,128]{1,0:T(8,128)(2,1)S(1)}) custom-call(f32[128,128]{1,0:T(8,128)S(1)} %get-tuple-element.38.live_ref.refs_0_, f32[960,128]{1,0:T(8,128)S(1)} %get-tuple-element.44.lt_ref.refs_1_, bf16[128,512]{1,0:T(8,128)(2,1)S(1)} %get-tuple-element.41.w_ref.refs_2_.refs_6_, ...), custom_call_target="tpu_custom_call" | custom-call | flops 10000000 | bytes 1049088 | tf_op jit(solution)/shard_map/pallas_call | solution.py:341
  15.9 1.0 %shard_map.80 = (bf16[480,128]{1,0:T(8,128)(2,1)S(1)}, bf16[480,128]{1,0:T(8,128)(2,1)S(1)}) custom-call(f32[128,128]{1,0:T(8,128)S(1)} %get-tuple-element.38.live_ref.refs_0_, f32[960,128]{1,0:T(8,128)S(1)} %get-tuple-element.44.lt_ref.refs_1_, bf16[128,512]{1,0:T(8,128)(2,1)S(1)} %get-tuple-element.41.w_ref.refs_2_.refs_6_, ...), custom_call_target="tpu_custom_call" | custom-call | flops 10000000 | bytes 1049088 | tf_op jit(solution)/shard_map/pallas_call | solution.py:341
  16.9 1.0 %shard_map.82 = (bf16[480,128]{1,0:T(8,128)(2,1)S(1)}, bf16[480,128]{1,0:T(8,128)(2,1)S(1)}, bf16[480,128]{1,0:T(8,128)(2,1)S(1)}, bf16[480,128]{1,0:T(8,128)(2,1)S(1)}, bf16[480,128]{1,0:T(8,128)(2,1)S(1)}) custom-call(f32[128,128]{1,0:T(8,128)S(1)} %get-tuple-element.38.live_ref.refs_0_, f32[960,128]{1,0:T(8,128)S(1)} %get-tuple-element.44.lt_ref.refs_1_, ...), custom_call_target="tpu_custom_call" | custom-call | flops 10000000 | bytes 1786368 | tf_op jit(solution)/shard_map/pallas_call | solution.py:341
  17.9 1.6 %collective-permute-start.5 = (bf16[480,128]{1,0:T(8,128)(2,1)S(1)}, bf16[480,128]{1,0:T(8,128)(2,1)S(1)}, u32[]{:S(2)}, u32[]{:S(2)}) collective-permute-start(bf16[480,128]{1,0:T(8,128)(2,1)S(1)} %get-tuple-element.49), channel_id=1, source_target_pairs={{0,1},{1,0},{2,3},{3,2},{4,5},{5,4},{6,7},{7,6},{8,9},{9,8},{10,11... | collective-permute-start | bytes 368648 | tf_op jit(solution)/shard_map/ppermute | solution.py:364
  19.5 1.5 %collective-permute-start.6 = (bf16[480,128]{1,0:T(8,128)(2,1)S(1)}, bf16[480,128]{1,0:T(8,128)(2,1)S(1)}, u32[]{:S(2)}, u32[]{:S(2)}) collective-permute-start(bf16[480,128]{1,0:T(8,128)(2,1)S(1)} %get-tuple-element.50), channel_id=1, source_target_pairs={{0,2},{1,3},{2,0},{3,1},{4,6},{5,7},{6,4},{7,5},{8,10},{9,11},{10,... | collective-permute-start | bytes 368648 | tf_op jit(solution)/shard_map/ppermute | solution.py:364
  21.5 1.7 %collective-permute-done.5.refs_1_ = bf16[480,128]{1,0:T(8,128)(2,1)S(1)} collective-permute-done((bf16[480,128]{1,0:T(8,128)(2,1)S(1)}, bf16[480,128]{1,0:T(8,128)(2,1)S(1)}, u32[]{:S(2)}, u32[]{:S(2)}) %collective-permute-start.5) | collective-permute-done | bytes 122912 | tf_op jit(solution)/shard_map/ppermute | solution.py:364
  23.2 3.8 %collective-permute-done.6.refs_2_ = bf16[480,128]{1,0:T(8,128)(2,1)S(1)} collective-permute-done((bf16[480,128]{1,0:T(8,128)(2,1)S(1)}, bf16[480,128]{1,0:T(8,128)(2,1)S(1)}, u32[]{:S(2)}, u32[]{:S(2)}) %collective-permute-start.6) | collective-permute-done | bytes 122912 | tf_op jit(solution)/shard_map/ppermute | solution.py:364
  27.5 1.4 %collective-permute-start.10 = (bf16[480,128]{1,0:T(8,128)(2,1)S(1)}, bf16[480,128]{1,0:T(8,128)(2,1)S(1)}, u32[]{:S(2)}, u32[]{:S(2)}) collective-permute-start(bf16[480,128]{1,0:T(8,128)(2,1)S(1)} %get-tuple-element.55.refs_1_), channel_id=1, source_target_pairs={{0,3},{1,2},{2,1},{3,0},{4,7},{5,6},{6,5},{7,4},{8,11},{9,10},{10,... | collective-permute-start | bytes 368648 | tf_op jit(solution)/shard_map/ppermute | solution.py:364
  28.8 1.2 %collective-permute-start.9 = (bf16[480,128]{1,0:T(8,128)(2,1)S(1)}, bf16[480,128]{1,0:T(8,128)(2,1)S(1)}, u32[]{:S(2)}, u32[]{:S(2)}) collective-permute-start(bf16[480,128]{1,0:T(8,128)(2,1)S(1)} %get-tuple-element.55.refs_1_), channel_id=1, source_target_pairs={{0,2},{1,3},{2,0},{3,1},{4,6},{5,7},{6,4},{7,5},{8,10},{9,11},{10,... | collective-permute-start | bytes 368648 | tf_op jit(solution)/shard_map/ppermute | solution.py:364
  30.0 1.0 %collective-permute-start.8 = (bf16[480,128]{1,0:T(8,128)(2,1)S(1)}, bf16[480,128]{1,0:T(8,128)(2,1)S(1)}, u32[]{:S(2)}, u32[]{:S(2)}) collective-permute-start(bf16[480,128]{1,0:T(8,128)(2,1)S(1)} %get-tuple-element.55.refs_1_), channel_id=1, source_target_pairs={{0,1},{1,0},{2,3},{3,2},{4,5},{5,4},{6,7},{7,6},{8,9},{9,8},{10,11... | collective-permute-start | bytes 368648 | tf_op jit(solution)/shard_map/ppermute | solution.py:364
  31.0 2.6 %collective-permute-done.10.refs_4_ = bf16[480,128]{1,0:T(8,128)(2,1)S(1)} collective-permute-done((bf16[480,128]{1,0:T(8,128)(2,1)S(1)}, bf16[480,128]{1,0:T(8,128)(2,1)S(1)}, u32[]{:S(2)}, u32[]{:S(2)}) %collective-permute-start.10) | collective-permute-done | bytes 122912 | tf_op jit(solution)/shard_map/ppermute | solution.py:364
  33.7 1.2 %collective-permute-done.9.refs_3_ = bf16[480,128]{1,0:T(8,128)(2,1)S(1)} collective-permute-done((bf16[480,128]{1,0:T(8,128)(2,1)S(1)}, bf16[480,128]{1,0:T(8,128)(2,1)S(1)}, u32[]{:S(2)}, u32[]{:S(2)}) %collective-permute-start.9) | collective-permute-done | bytes 122912 | tf_op jit(solution)/shard_map/ppermute | solution.py:364
  34.9 2.9 %shard_map.84 = (f32[480,128]{1,0:T(8,128)S(1)}, bf16[480,128]{1,0:T(8,128)(2,1)S(1)}, f32[480,128]{1,0:T(8,128)S(1)}) custom-call(f32[960,128]{1,0:T(8,128)S(1)} %get-tuple-element.43.refs_0_, bf16[480,128]{1,0:T(8,128)(2,1)S(1)} %get-tuple-element.55.refs_1_, bf16[480,128]{1,0:T(8,128)(2,1)S(1)} %collective-permute-done.8.refs_2_, ...), custom_call_target="tpu_custom_call" | custom-call | flops 10000000 | bytes 2088960 | tf_op jit(solution)/shard_map/pallas_call | solution.py:341
  39.7 3.2 %collective-permute-start.14 = (bf16[480,128]{1,0:T(8,128)(2,1)S(1)}, bf16[480,128]{1,0:T(8,128)(2,1)S(1)}, u32[]{:S(2)}, u32[]{:S(2)}) collective-permute-start(bf16[480,128]{1,0:T(8,128)(2,1)S(1)} %shard_map.88), channel_id=1, source_target_pairs={{0,16},{4,20},{8,24},{12,28},{16,0},{20,4},{24,8},{28,12},{1,17},{... | collective-permute-start | bytes 368648 | tf_op jit(solution)/shard_map/ppermute | solution.py:361
  43.4 1.2 %collective-permute-start.15 = (bf16[480,128]{1,0:T(8,128)(2,1)S(1)}, bf16[480,128]{1,0:T(8,128)(2,1)S(1)}, u32[]{:S(2)}, u32[]{:S(2)}) collective-permute-start(bf16[480,128]{1,0:T(8,128)(2,1)S(1)} %shard_map.89), channel_id=1, source_target_pairs={{0,24},{4,28},{8,16},{12,20},{16,8},{20,12},{24,0},{28,4},{1,25},{... | collective-permute-start | bytes 368648 | tf_op jit(solution)/shard_map/ppermute | solution.py:361
  45.2 0.9 %shard_map.86 = (bf16[15,30,128]{2,1,0:T(8,128)(2,1)}, f32[480,128]{1,0:T(8,128)S(1)}) custom-call(f32[480,128]{1,0:T(8,128)S(1)} %get-tuple-element.60.own_ref, bf16[480,128]{1,0:T(8,128)(2,1)S(1)} %collective-permute-done.11.got_ref, f32[480,128]{1,0:T(8,128)S(1)} %get-tuple-element.62.l1_ref, f32[480,128]{1,0:T(8,128)S(1)} %get-tuple-element.63.l2_ref, ...), custom_call_target="tpu_custom_call" | custom-call | flops 10000000 | bytes 1630720 | tf_op jit(solution)/shard_map/pallas_call | solution.py:341
  46.9 5.4 %collective-permute-done.15.refs_3_ = bf16[480,128]{1,0:T(8,128)(2,1)S(1)} collective-permute-done((bf16[480,128]{1,0:T(8,128)(2,1)S(1)}, bf16[480,128]{1,0:T(8,128)(2,1)S(1)}, u32[]{:S(2)}, u32[]{:S(2)}) %collective-permute-start.15) | collective-permute-done | bytes 122912 | tf_op jit(solution)/shard_map/ppermute | solution.py:361
  52.3 1.0 %shard_map.90 = bf16[15,30,128]{2,1,0:T(8,128)(2,1)} custom-call(f32[480,128]{1,0:T(8,128)S(1)} %get-tuple-element.68.refs_0_, bf16[480,128]{1,0:T(8,128)(2,1)S(1)} %collective-permute-done.13.refs_1_, bf16[480,128]{1,0:T(8,128)(2,1)S(1)} %collective-permute-done.14.refs_2_, bf16[480,128]{1,0:T(8,128)(2,1)S(1)} %collective-permute-done.15.refs_3_, ...), custom_call_target="tpu_custom_call" | custom-call | flops 10000000 | bytes 2089472 | tf_op jit(solution)/shard_map/pallas_call | solution.py:341
  (22 shorter events, 6.1 us)
Async XLA Ops:
  0.6 10.4 %collective-permute-start.2 = (bf16[15,30,128]{2,1,0:T(8,128)(2,1)}, bf16[15,30,128]{2,1,0:T(8,128)(2,1)S(1)}, u32[]{:S(2)}, u32[]{:S(2)}) collective-permute-start(bf16[15,30,128]{2,1,0:T(8,128)(2,1)} %refs_1_.1), channel_id=1, source_target_pairs={{0,16},{4,20},{8,24},{12,28},{16,0},{20,4},{24,8},{28,12},{1,17},{... | collective-permute-start | bytes 345608 | tf_op jit(solution)/shard_map/ppermute | solution.py:361
  4.8 8.1 %collective-permute-start.1 = (bf16[15,30,128]{2,1,0:T(8,128)(2,1)}, bf16[15,30,128]{2,1,0:T(8,128)(2,1)S(1)}, u32[]{:S(2)}, u32[]{:S(2)}) collective-permute-start(bf16[15,30,128]{2,1,0:T(8,128)(2,1)} %refs_2_.1), channel_id=1, source_target_pairs={{0,4},{4,0},{8,12},{12,8},{16,20},{20,16},{24,28},{28,24},{1,5},{5... | collective-permute-start | bytes 345608 | tf_op jit(solution)/shard_map/ppermute | solution.py:367
  4.8 8.1 %collective-permute-start = (bf16[15,30,128]{2,1,0:T(8,128)(2,1)}, bf16[15,30,128]{2,1,0:T(8,128)(2,1)S(1)}, u32[]{:S(2)}, u32[]{:S(2)}) collective-permute-start(bf16[15,30,128]{2,1,0:T(8,128)(2,1)} %refs_1_.1), channel_id=1, source_target_pairs={{0,4},{4,0},{8,12},{12,8},{16,20},{20,16},{24,28},{28,24},{1,5},{5... | collective-permute-start | bytes 345608 | tf_op jit(solution)/shard_map/ppermute | solution.py:367
  5.3 10.6 %collective-permute-start.4 = (bf16[15,30,128]{2,1,0:T(8,128)(2,1)}, bf16[15,30,128]{2,1,0:T(8,128)(2,1)S(1)}, u32[]{:S(2)}, u32[]{:S(2)}) collective-permute-start(bf16[15,30,128]{2,1,0:T(8,128)(2,1)} %refs_1_.1), channel_id=1, source_target_pairs={{0,8},{4,12},{8,0},{12,4},{16,24},{20,28},{24,16},{28,20},{1,9},{5... | collective-permute-start | bytes 345608 | tf_op jit(solution)/shard_map/ppermute | solution.py:361
  11.0 5.9 %collective-permute-start.3 = (bf16[15,30,128]{2,1,0:T(8,128)(2,1)S(1)}, bf16[15,30,128]{2,1,0:T(8,128)(2,1)S(1)}, u32[]{:S(2)}, u32[]{:S(2)}) collective-permute-start(bf16[15,30,128]{2,1,0:T(8,128)(2,1)S(1)} %collective-permute-done.2.shard), channel_id=1, source_target_pairs={{0,8},{4,12},{8,0},{12,4},{16,24},{20,28},{24,16},{28,20},{1,9},{5... | collective-permute-start | bytes 345608 | tf_op jit(solution)/shard_map/ppermute | solution.py:361
  17.9 5.3 %collective-permute-start.5 = (bf16[480,128]{1,0:T(8,128)(2,1)S(1)}, bf16[480,128]{1,0:T(8,128)(2,1)S(1)}, u32[]{:S(2)}, u32[]{:S(2)}) collective-permute-start(bf16[480,128]{1,0:T(8,128)(2,1)S(1)} %get-tuple-element.49), channel_id=1, source_target_pairs={{0,1},{1,0},{2,3},{3,2},{4,5},{5,4},{6,7},{7,6},{8,9},{9,8},{10,11... | collective-permute-start | bytes 368648 | tf_op jit(solution)/shard_map/ppermute | solution.py:364
  19.5 7.5 %collective-permute-start.6 = (bf16[480,128]{1,0:T(8,128)(2,1)S(1)}, bf16[480,128]{1,0:T(8,128)(2,1)S(1)}, u32[]{:S(2)}, u32[]{:S(2)}) collective-permute-start(bf16[480,128]{1,0:T(8,128)(2,1)S(1)} %get-tuple-element.50), channel_id=1, source_target_pairs={{0,2},{1,3},{2,0},{3,1},{4,6},{5,7},{6,4},{7,5},{8,10},{9,11},{10,... | collective-permute-start | bytes 368648 | tf_op jit(solution)/shard_map/ppermute | solution.py:364
  21.0 6.0 %collective-permute-start.7 = (bf16[480,128]{1,0:T(8,128)(2,1)S(1)}, bf16[480,128]{1,0:T(8,128)(2,1)S(1)}, u32[]{:S(2)}, u32[]{:S(2)}) collective-permute-start(bf16[480,128]{1,0:T(8,128)(2,1)S(1)} %get-tuple-element.51), channel_id=1, source_target_pairs={{0,3},{1,2},{2,1},{3,0},{4,7},{5,6},{6,5},{7,4},{8,11},{9,10},{10,... | collective-permute-start | bytes 368648 | tf_op jit(solution)/shard_map/ppermute | solution.py:364
  27.5 6.2 %collective-permute-start.10 = (bf16[480,128]{1,0:T(8,128)(2,1)S(1)}, bf16[480,128]{1,0:T(8,128)(2,1)S(1)}, u32[]{:S(2)}, u32[]{:S(2)}) collective-permute-start(bf16[480,128]{1,0:T(8,128)(2,1)S(1)} %get-tuple-element.55.refs_1_), channel_id=1, source_target_pairs={{0,3},{1,2},{2,1},{3,0},{4,7},{5,6},{6,5},{7,4},{8,11},{9,10},{10,... | collective-permute-start | bytes 368648 | tf_op jit(solution)/shard_map/ppermute | solution.py:364
  28.8 6.0 %collective-permute-start.9 = (bf16[480,128]{1,0:T(8,128)(2,1)S(1)}, bf16[480,128]{1,0:T(8,128)(2,1)S(1)}, u32[]{:S(2)}, u32[]{:S(2)}) collective-permute-start(bf16[480,128]{1,0:T(8,128)(2,1)S(1)} %get-tuple-element.55.refs_1_), channel_id=1, source_target_pairs={{0,2},{1,3},{2,0},{3,1},{4,6},{5,7},{6,4},{7,5},{8,10},{9,11},{10,... | collective-permute-start | bytes 368648 | tf_op jit(solution)/shard_map/ppermute | solution.py:364
  30.0 4.9 %collective-permute-start.8 = (bf16[480,128]{1,0:T(8,128)(2,1)S(1)}, bf16[480,128]{1,0:T(8,128)(2,1)S(1)}, u32[]{:S(2)}, u32[]{:S(2)}) collective-permute-start(bf16[480,128]{1,0:T(8,128)(2,1)S(1)} %get-tuple-element.55.refs_1_), channel_id=1, source_target_pairs={{0,1},{1,0},{2,3},{3,2},{4,5},{5,4},{6,7},{7,6},{8,9},{9,8},{10,11... | collective-permute-start | bytes 368648 | tf_op jit(solution)/shard_map/ppermute | solution.py:364
  31.0 14.1 %collective-permute-start.12 = (bf16[480,128]{1,0:T(8,128)(2,1)S(1)}, bf16[480,128]{1,0:T(8,128)(2,1)S(1)}, u32[]{:S(2)}, u32[]{:S(2)}) collective-permute-start(bf16[480,128]{1,0:T(8,128)(2,1)S(1)} %get-tuple-element.66), channel_id=1, source_target_pairs={{0,4},{4,0},{8,12},{12,8},{16,20},{20,16},{24,28},{28,24},{1,5},{5... | collective-permute-start | bytes 368648 | tf_op jit(solution)/shard_map/ppermute | solution.py:367
  37.8 7.4 %collective-permute-start.11 = (bf16[480,128]{1,0:T(8,128)(2,1)S(1)}, bf16[480,128]{1,0:T(8,128)(2,1)S(1)}, u32[]{:S(2)}, u32[]{:S(2)}) collective-permute-start(bf16[480,128]{1,0:T(8,128)(2,1)S(1)} %get-tuple-element.61), channel_id=1, source_target_pairs={{0,4},{4,0},{8,12},{12,8},{16,20},{20,16},{24,28},{28,24},{1,5},{5... | collective-permute-start | bytes 368648 | tf_op jit(solution)/shard_map/ppermute | solution.py:367
  38.5 8.4 %collective-permute-start.13 = (bf16[480,128]{1,0:T(8,128)(2,1)S(1)}, bf16[480,128]{1,0:T(8,128)(2,1)S(1)}, u32[]{:S(2)}, u32[]{:S(2)}) collective-permute-start(bf16[480,128]{1,0:T(8,128)(2,1)S(1)} %shard_map.87), channel_id=1, source_target_pairs={{0,8},{4,12},{8,0},{12,4},{16,24},{20,28},{24,16},{28,20},{1,9},{5... | collective-permute-start | bytes 368648 | tf_op jit(solution)/shard_map/ppermute | solution.py:361
  39.7 7.2 %collective-permute-start.14 = (bf16[480,128]{1,0:T(8,128)(2,1)S(1)}, bf16[480,128]{1,0:T(8,128)(2,1)S(1)}, u32[]{:S(2)}, u32[]{:S(2)}) collective-permute-start(bf16[480,128]{1,0:T(8,128)(2,1)S(1)} %shard_map.88), channel_id=1, source_target_pairs={{0,16},{4,20},{8,24},{12,28},{16,0},{20,4},{24,8},{28,12},{1,17},{... | collective-permute-start | bytes 368648 | tf_op jit(solution)/shard_map/ppermute | solution.py:361
  43.4 8.9 %collective-permute-start.15 = (bf16[480,128]{1,0:T(8,128)(2,1)S(1)}, bf16[480,128]{1,0:T(8,128)(2,1)S(1)}, u32[]{:S(2)}, u32[]{:S(2)}) collective-permute-start(bf16[480,128]{1,0:T(8,128)(2,1)S(1)} %shard_map.89), channel_id=1, source_target_pairs={{0,24},{4,28},{8,16},{12,20},{16,8},{20,12},{24,0},{28,4},{1,25},{... | collective-permute-start | bytes 368648 | tf_op jit(solution)/shard_map/ppermute | solution.py:361

commit v4 on v3

--- a/solution.py
+++ b/solution.py
@@ -62,12 +62,12 @@
         yield i, (columns * row_of(live_ref, start + i)[None]).reshape(pitch, columns.shape[2])
 
 
-def load_cells(cells_ref, scratch, first):
-    rows, cols, channels = cells_ref.shape
+def load_cells(cells_refs, scratch, first):
+    rows, cols, channels = cells_refs[0].shape
     pitch = pad_to(cols, 16)
     for i in range(rows):
         at = (first + i) * pitch
-        scratch[at : at + cols, :] = cells_ref[i].astype(F32)
+        scratch[at : at + cols, :] = sum(ref[i].astype(F32) for ref in cells_refs)
         if pitch > cols:
             scratch[at + cols : at + pitch, :] = jnp.zeros((pitch - cols, channels), F32)
 
@@ -88,8 +88,8 @@
     hidden = w_ref.shape[1] // 4
     dap = lax.axis_index("dap")
     core = lax.rem(dap, 2)
-    load_cells(x_ref, xs, 0)
-    load_cells(xp_ref, xs, rows)
+    load_cells([x_ref], xs, 0)
+    load_cells([xp_ref], xs, rows)
     normed, _ = normalize(xs[...])
     normed_half = normed.astype(BF16)
     projected = matmul(normed_half, w_ref[:, : 2 * hidden])
@@ -115,8 +115,8 @@
                 out_ref[i * half + rows : (i + 1) * half, :] = jnp.zeros((half - rows, channels), F32)
 
     pick(gate_ref)
-    load_cells(cot_ref, gs, 0)
-    load_cells(cotp_ref, gs, rows)
+    load_cells([cot_ref], gs, 0)
+    load_cells([cotp_ref], gs, rows)
     pick(cotm_ref)
 
 
@@ -124,7 +124,7 @@
     rows, cols, _ = x_ref.shape
     pitch = pad_to(cols, 16)
     hidden = w_ref.shape[1] // 4
-    load_cells(x_ref, xs, 0)
+    load_cells([x_ref], xs, 0)
     normed, scale = normalize(xs[...])
     normed_ref[...] = normed
     scale_ref[...] = jnp.broadcast_to(scale, normed.shape)
@@ -158,11 +158,23 @@
     lax.fori_loop(0, rows // JB, step, 0)
 
 
-def right_of(live_ref, x_ref, w_ref, xs, rs, r_ref, s):
-    rows, cols, _ = x_ref.shape
+def lookup(table, chip):
+    value = table[0]
+    for z in range(1, len(table)):
+        if table[z] != table[0]:
+            value = jnp.where(chip == z, table[z], value)
+    return value
+
+
+def this_chip():
+    return lax.axis_index("dap") // 2
+
+
+def right_of(live_ref, x_refs, w_ref, xs, rs, r_ref, s):
+    rows, cols, _ = x_refs[0].shape
     pitch = pad_to(cols, 16)
     hidden = w_ref.shape[1] // 4
-    load_cells(x_ref, xs, 0)
+    load_cells(x_refs, xs, 0)
     normed, _ = normalize(xs[...])
     projected = matmul(normed.astype(BF16), w_ref[:, 2 * hidden :])
     right = jax.nn.sigmoid(projected[:, :hidden]) * projected[:, hidden:]
@@ -174,26 +186,28 @@
         rs[block, :] = value.astype(F32)
 
 
-def part_kernel(step, live_ref, lt_ref, w_ref, shard, right_ref, part_ref, xs, rs, ps):
-    rows, cols, _ = shard.shape
-    right_of(live_ref, shard, w_ref, xs, rs, right_ref, step)
+def part_kernel(steps, live_ref, lt_ref, w_ref, *refs):
+    shards, (right_ref, part_ref, xs, rs, ps) = refs[:-5], refs[-5:]
+    rows, cols, _ = shards[0].shape
+    right_of(live_ref, shards, w_ref, xs, rs, right_ref, lookup(steps, this_chip()))
     product_part(lt_ref, rs, ps, rows, cols)
     part_ref[...] = ps[: part_ref.shape[0], :].astype(BF16)
 
 
-def late_kernel(blocks, step, *refs):
-    live_ref, lt_ref, w_ref, shard = refs[:4]
-    done = refs[4 : 3 + blocks]
-    right_ref, outs = refs[3 + blocks], refs[4 + blocks : 4 + 2 * blocks]
-    xs, rs, ps, held = refs[4 + 2 * blocks :]
-    rows, cols, _ = shard.shape
-    for s in range(blocks):
-        if s != step:
-            held[s] = done[s - (s > step)][...]
-    right_of(live_ref, shard, w_ref, xs, rs, right_ref, step)
+def late_kernel(steps, live_ref, lt_ref, w_ref, *refs):
+    blocks = len(steps)
+    done, refs = refs[: blocks - 1], refs[blocks - 1 :]
+    split = len(refs) - blocks - 5
+    shards, right_ref, outs, (xs, rs, ps, held) = refs[:split], refs[split], refs[split + 1 : -4], refs[-4:]
+    rows, cols, _ = shards[0].shape
+    chip = this_chip()
+    for part, table in zip(done, steps):
+        held[lookup(table, chip)] = part[...]
+    last = lookup(steps[-1], chip)
+    right_of(live_ref, shards, w_ref, xs, rs, right_ref, last)
     product_part(lt_ref, rs, ps, rows, cols)
-    held[step] = ps[: held.shape[1], :].astype(BF16)
-    turn = (lax.axis_index("dap") // 2) ^ lax.axis_index("ch")
+    held[last] = ps[: held.shape[1], :].astype(BF16)
+    turn = chip ^ lax.axis_index("ch")
     for t in range(blocks):
         outs[t][...] = held[turn ^ t]
 
@@ -237,21 +251,26 @@
     lax.fori_loop(0, rows // JB, step, 0)
 
 
-def send_right_kernel(rows, cols, blocks, s, *refs):
-    l_ref, pieces, (out_ref, gs) = refs[0], refs[1 : 1 + blocks], refs[1 + blocks :]
-    chip, column = lax.axis_index("dap") // 2, lax.axis_index("ch")
+def send_right_kernel(rows, cols, blocks, steps, *refs):
+    l_ref, pieces = refs[0], refs[1 : 1 + blocks]
+    more, (out_ref, gs) = refs[1 + blocks : -2], refs[-2:]
+    chip, column = this_chip(), lax.axis_index("ch")
+    step = lookup(steps, chip)
     for t in range(blocks):
-        @pl.when(chip ^ column ^ s == t)
+        @pl.when(chip ^ column ^ step == t)
         def _(t=t):
             gs[...] = pieces[t][...].astype(F32)
 
     def store(where, value):
+        for ref in more:
+            value = value + ref[where, :].astype(F32)
         out_ref[where, :] = value.astype(BF16)
 
     grad_right_part(l_ref, gs, store, rows, cols)
 
 
-def grad_left_kernel(rows, cols, blocks, *refs):
+def grad_left_kernel(rows, cols, steps, *refs):
+    blocks = len(steps)
     l_ref, pieces, shards = refs[0], refs[1 : 1 + blocks], refs[1 + blocks : 1 + 2 * blocks]
     own_ref, send_ref, right_ref, gs, rs = refs[1 + 2 * blocks :]
     pitch, half = pad_to(cols, 16), pad_to(rows, 16)
@@ -259,8 +278,8 @@
     column = lax.axis_index("ch")
     for t in range(blocks):
         gs[column ^ t] = pieces[t][...].astype(F32)
-    for s in range(blocks):
-        rs[chip ^ s] = shards[s][...].astype(F32)
+    for table, shard in zip(steps, shards):
+        rs[chip ^ lookup(table, chip)] = shard[...].astype(F32)
 
     def left_rows(first, ref):
         def step(b, _):
@@ -313,13 +332,13 @@
     acc_ref[...] = acc + matmul_t(gs[...].astype(BF16), wg_ref[...])
 
 
-def finish_kernel(blocks, *refs):
-    parts = refs[:blocks]
-    r1_ref, r2_ref, w_ref, acc_ref, normed_ref, scale_ref, out_ref = refs[blocks:]
+def finish_kernel(count, *refs):
+    parts = refs[:count]
+    r1_ref, r2_ref, w_ref, acc_ref, normed_ref, scale_ref, out_ref = refs[count:]
     rows, cols, _ = out_ref.shape
     pitch = pad_to(cols, 16)
     total = parts[0][...]
-    for s in range(1, blocks):
+    for s in range(1, count):
         total = total + parts[s][...].astype(F32)
     grad_right = total.astype(BF16).astype(F32)
     hidden = total.shape[1]
@@ -357,8 +376,8 @@
     if devices != 2 * blocks or cols != 2 * rows or blocks & (blocks - 1) or rows % JB:
         raise ValueError("unsupported split")
 
-    def along_dap(value, s):
-        return lax.ppermute(value, "dap", [(d, d ^ (2 * s)) for d in range(devices)])
+    def along_dap(value, pairs):
+        return lax.ppermute(value, "dap", [(2 * a + c, 2 * b + c) for a, b in pairs for c in range(2)])
 
     def along_ch(value, t):
         return lax.ppermute(value, "ch", [(h, h ^ t) for h in range(blocks)])
@@ -366,11 +385,10 @@
     def to_partner(value):
         return lax.ppermute(value, "dap", [(d, d ^ 1) for d in range(devices)])
 
-    last = blocks - 1
-    shards = [x] + [None] * last
-    for s in dap_order(blocks):
-        direct = s == 1 or s % 2 == 0
-        shards[s] = along_dap(x if direct else shards[s ^ 1], s if direct else 1)
+    moves, shards = gather_plan(blocks)
+    moved = []
+    for pairs, source in moves:
+        moved.append(along_dap(x if source is None else moved[source], pairs))
     x_pair, cot_pair = to_partner(x), to_partner(cot)
     sources = (x, cot, w_proj, w_gate, w_out)
     residues = mask.shape[0]
@@ -384,16 +402,19 @@
         (live, xv, x_pair, cotv, cot_pair, w_proj, w_gate),
         [(wide, channels), (tall * pitch, hidden), (wide, channels)])
     scratch = [(cells, channels), (cells, hidden), (tall * half, hidden)]
-    rights, done = [None] * blocks, []
-    for s in range(last):
-        rights[s], part = call(
-            functools.partial(part_kernel, s), [((cells, hidden), BF16), ((mids, hidden), BF16)],
-            (live, left_t, w_proj, shards[s] if s else xv), scratch)
+    steps = [[0] * blocks] + [table for _, table in shards]
+    held = [[xv]] + [[moved[n] for n in group] for group, _ in shards]
+    rights, done = [], []
+    for s in range(blocks - 1):
+        right, part = call(
+            functools.partial(part_kernel, steps[s]), [((cells, hidden), BF16), ((mids, hidden), BF16)],
+            (live, left_t, w_proj, *held[s]), scratch)
+        rights.append(right)
         done.append(part)
-    rights[last], *parts = call(
-        functools.partial(late_kernel, blocks, last),
-        [((cells, hidden), BF16)] + [((mids, hidden), BF16)] * blocks,
-        (live, left_t, w_proj, shards[last], *done), scratch + [pltpu.VMEM((blocks, mids, hidden), BF16)])
+    right, *parts = call(
+        functools.partial(late_kernel, steps), [((cells, hidden), BF16)] + [((mids, hidden), BF16)] * blocks,
+        (live, left_t, w_proj, *done, *held[-1]), scratch + [pltpu.VMEM((blocks, mids, hidden), BF16)])
+    rights.append(right)
     for t in range(1, blocks):
         parts[t] = along_ch(parts[t], t)
     update, back, logit, grad_product = call(
@@ -402,13 +423,15 @@
         (*parts, gate, upstream, w_out))
     pieces = [grad_product] + [along_ch(grad_product, t) for t in range(1, blocks)]
     back = to_partner(back)
-    gots = [None] * blocks
-    for s in range(1, blocks):
-        (send,) = call(functools.partial(send_right_kernel, rows, cols, blocks, s),
-                       [((cells, hidden), BF16)], (left, *pieces), [(mids, hidden)])
-        gots[s] = along_dap(send, s)
+    sends, returns, arrivals = reduce_plan(blocks)
+    got = []
+    for n, (table, extra) in enumerate(sends):
+        more = () if extra is None else (got[extra],)
+        (send,) = call(functools.partial(send_right_kernel, rows, cols, blocks, table),
+                       [((cells, hidden), BF16)], (left, *pieces, *more), [(mids, hidden)])
+        got += [along_dap(send, pairs) for pairs in returns[n]]
     left_own, left_send, right_own = call(
-        functools.partial(grad_left_kernel, rows, cols, blocks),
+        functools.partial(grad_left_kernel, rows, cols, steps),
         [((cells, hidden), F32), ((cells, hidden), BF16), ((cells, hidden), F32)],
         (left, *pieces, *rights), [(blocks, mids, hidden), (blocks, cells, hidden)])
     left_got = to_partner(left_send)
@@ -419,13 +442,40 @@
         finish_left_kernel, [((rows, cols, channels), BF16), ((cells, channels), F32)],
         (left_own, left_got, l1, l2, w_proj, w_gate, update, logit, back),
         [(cells, channels), (cells, channels)])
-    (grad_pair,) = call(functools.partial(finish_kernel, blocks), [((rows, cols, channels), BF16)],
-                        (right_own, *gots[1:], r1, r2, w_proj, acc, normed, scale))
+    (grad_pair,) = call(functools.partial(finish_kernel, 1 + len(arrivals)), [((rows, cols, channels), BF16)],
+                        (right_own, *[got[n] for n in arrivals], r1, r2, w_proj, acc, normed, scale))
     return pair_update, grad_pair
 
 
-def dap_order(blocks):
-    return [*range(2, blocks, 2), 1, *range(3, blocks, 2)]
+def gather_plan(blocks):
+    if blocks == 4:
+        moves = [
+            ([(0, 2), (3, 1), (1, 0), (2, 3)], None),
+            ([(0, 1), (1, 3), (3, 2), (2, 0)], None),
+            ([(1, 2), (2, 1)], None),
+            ([(2, 3), (1, 0)], 0),
+        ]
+        return moves, [([0], [1, 2, 2, 1]), ([1], [2, 1, 1, 2]), ([2, 3], [3] * 4)]
+    order = [*range(2, blocks, 2), 1, *range(3, blocks, 2)]
+    moves = []
+    for s in order:
+        relay = s % 2 and s > 1
+        moves.append(([(z, z ^ (1 if relay else s)) for z in range(blocks)], order.index(s ^ 1) if relay else None))
+    return moves, [([n], [s] * blocks) for n, s in enumerate(order)]
+
+
+def reduce_plan(blocks):
+    if blocks == 4:
+        sends = [([3] * 4, None), ([2, 1, 1, 2], None), ([1, 2, 2, 1], 0)]
+        returns = [
+            [[(3, 2), (0, 1)], [(1, 2), (2, 1)]],
+            [[(1, 0), (3, 1), (2, 3), (0, 2)]],
+            [[(2, 0), (1, 3), (0, 1), (3, 2)]],
+        ]
+        return sends, returns, [1, 2, 3]
+    far = [*range(2, blocks), 1]
+    sends = [([s] * blocks, None) for s in far]
+    return sends, [[[(z, z ^ s) for z in range(blocks)]] for s in far], [*range(blocks - 1)]
 
 
 def solution(mesh):

time: 54.4 us -> 54.2 us (level); the launches traced: 53.4 us -> 54 us
  starting transfers between devices: 19.2 us -> 21.4 us
  waiting for transfers between devices: 19.9 us -> 18.2 us
    ppermute x6 -> x8, starting transfers between devices: 11.5 us -> 13.1 us  [along_dap(): lax.ppermute(value, 'dap', [(2 * a + c, 2 * b + c) for a, b in pairs for...]
    ppermute x6 -> x8, waiting for transfers between devices: 10.4 us -> 9.55 us  [along_dap(): lax.ppermute(value, 'dap', [(2 * a + c, 2 * b + c) for a, b in pairs for...]
    ppermute x6, waiting for transfers between devices: 9.42 us -> 8.69 us  [along_ch(): return lax.ppermute(value, 'ch', [(h, h ^ t) for h in range(blocks)])]
    ppermute x4, starting transfers between devices: 0.58 us -> 1.13 us  [to_partner(): return lax.ppermute(value, 'dap', [(d, d ^ 1) for d in range(devices)])]
  transfers between devices with their start and end apart: 16 -> 18, of which waited for: 8 -> 10; matrix products, arithmetic and copies ran while one was open for 0% -> 0% of each run, Pallas kernels for 21% -> 19%
where the time goes in v4:
time: 54.2 us; the launch traced here: 54 us
  starting transfers between devices  21.4 us (39%)
  waiting for transfers between devices  18.2 us (34%)
  Pallas kernels  13.6 us (25%)
  between operations  0.81 us (1%)
    pallas_call x14, Pallas kernels, call(): pl.pallas_call(body, out_shape=outs, in_specs=[specs] * len(args), out_sp...  13.6 us
    ppermute x8, starting transfers between devices, along_dap(): lax.ppermute(value, 'dap', [(2 * a + c, 2 * b + c) for a, b in pairs for...  13.1 us
    ppermute x8, waiting for transfers between devices, along_dap(): lax.ppermute(value, 'dap', [(2 * a + c, 2 * b + c) for a, b in pairs for...  9.55 us
    ppermute x6, waiting for transfers between devices, along_ch(): return lax.ppermute(value, 'ch', [(h, h ^ t) for h in range(blocks)])  8.69 us
    ppermute x6, starting transfers between devices, along_ch(): return lax.ppermute(value, 'ch', [(h, h ^ t) for h in range(blocks)])  7.11 us
    ppermute x4, starting transfers between devices, to_partner(): return lax.ppermute(value, 'dap', [(d, d ^ 1) for d in range(devices)])  1.13 us
  transfers between devices with their start and end apart: 18, of which 10 were waited for; matrix products, arithmetic and copies ran while one was open for 0% of the time, Pallas kernels for 19%

profile of v4, /device:TPU:0, one launch (start us, length us, event | category | flops | bytes accessed | tf_op | source)
XLA Modules:
  0.0 54.0 jit_solution(8354126915539082121)
XLA Ops:
  0.6 4.1 %collective-permute-start.2 = (bf16[15,30,128]{2,1,0:T(8,128)(2,1)}, bf16[15,30,128]{2,1,0:T(8,128)(2,1)S(1)}, u32[]{:S(2)}, u32[]{:S(2)}) collective-permute-start(bf16[15,30,128]{2,1,0:T(8,128)(2,1)} %refs_1_.1), channel_id=1, source_target_pairs={{0,16},{4,20},{24,8},{28,12},{8,0},{12,4},{16,24},{20,28},{1,17},{... | collective-permute-start | bytes 345608 | tf_op jit(solution)/shard_map/ppermute | solution.py:380
  5.9 2.8 %collective-permute-done.2.refs_0_ = bf16[15,30,128]{2,1,0:T(8,128)(2,1)S(1)} collective-permute-done((bf16[15,30,128]{2,1,0:T(8,128)(2,1)}, bf16[15,30,128]{2,1,0:T(8,128)(2,1)S(1)}, u32[]{:S(2)}, u32[]{:S(2)}) %collective-permute-start.2) | collective-permute-done | bytes 115232 | tf_op jit(solution)/shard_map/ppermute | solution.py:380
  8.8 1.3 %collective-permute-start.5 = (bf16[15,30,128]{2,1,0:T(8,128)(2,1)S(1)}, bf16[15,30,128]{2,1,0:T(8,128)(2,1)S(1)}, u32[]{:S(2)}, u32[]{:S(2)}) collective-permute-start(bf16[15,30,128]{2,1,0:T(8,128)(2,1)S(1)} %collective-permute-done.2.refs_0_), channel_id=1, source_target_pairs={{16,24},{20,28},{8,0},{12,4},{17,25},{21,29},{9,1},{13,5},{18,26},... | collective-permute-start | bytes 345608 | tf_op jit(solution)/shard_map/ppermute | solution.py:380
  10.1 1.1 %shard_map.77 = (bf16[15,30,128]{2,1,0:T(8,128)(2,1)S(1)}, bf16[15,30,128]{2,1,0:T(8,128)(2,1)S(1)}, bf16[128,512]{1,0:T(8,128)(2,1)S(1)}, bf16[128,128]{1,0:T(8...) custom-call(s32[120]{0:T(128)} %refs_0_.1, bf16[15,30,128]{2,1,0:T(8,128)(2,1)} %refs_1_.1, ...), custom_call_target="tpu_custom_call" | custom-call | flops 10000000 | bytes 920032 | tf_op jit(solution)/shard_map/pallas_call | solution.py:360
  11.2 1.0 %shard_map.78 = (f32[960,128]{1,0:T(8,128)S(1)}, f32[960,128]{1,0:T(8,128)S(1)}, f32[480,128]{1,0:T(8,128)S(1)}, f32[480,128]{1,0:T(8,128)S(1)}) custom-call(f32[128,128]{1,0:T(8,128)S(1)} %get-tuple-element.38.live_ref, bf16[15,30,128]{2,1,0:T(8,128)(2,1)S(1)} %get-tuple-element.39.x_ref.refs_0_, bf16[15,30,128]{2,1,0:T(8,128)(2,1)S(1)} %collective-permute-done.xp_ref, ...), custom_call_target="tpu_custom_call" | custom-call | flops 10000000 | bytes 2164736 | tf_op jit(solution)/shard_map/pallas_call | solution.py:360
  12.2 1.0 %shard_map.79 = (bf16[480,128]{1,0:T(8,128)(2,1)S(1)}, bf16[480,128]{1,0:T(8,128)(2,1)S(1)}) custom-call(f32[128,128]{1,0:T(8,128)S(1)} %get-tuple-element.38.live_ref, f32[960,128]{1,0:T(8,128)S(1)} %get-tuple-element.44.lt_ref, bf16[128,512]{1,0:T(8,128)(2,1)S(1)} %get-tuple-element.41.w_ref.refs_6_, bf16[15,30,128]{2,1,0:T(8,128)(2,1)S(1)} %get-tuple-element.39.x_ref.refs_0_), custom_call_target="tpu_custom_call" | custom-call | flops 10000000 | bytes 1049088 | tf_op jit(solution)/shard_map/pallas_call | solution.py:360
  13.2 1.0 %shard_map.80 = (bf16[480,128]{1,0:T(8,128)(2,1)S(1)}, bf16[480,128]{1,0:T(8,128)(2,1)S(1)}) custom-call(f32[128,128]{1,0:T(8,128)S(1)} %get-tuple-element.38.live_ref, f32[960,128]{1,0:T(8,128)S(1)} %get-tuple-element.44.lt_ref, bf16[128,512]{1,0:T(8,128)(2,1)S(1)} %get-tuple-element.41.w_ref.refs_6_, bf16[15,30,128]{2,1,0:T(8,128)(2,1)S(1)} %collective-permute-done.2.refs_0_), custom_call_target="tpu_custom_call" | custom-call | flops 10000000 | bytes 1049088 | tf_op jit(solution)/shard_map/pallas_call | solution.py:360
  14.2 1.0 %shard_map.81 = (bf16[480,128]{1,0:T(8,128)(2,1)S(1)}, bf16[480,128]{1,0:T(8,128)(2,1)S(1)}) custom-call(f32[128,128]{1,0:T(8,128)S(1)} %get-tuple-element.38.live_ref, f32[960,128]{1,0:T(8,128)S(1)} %get-tuple-element.44.lt_ref, bf16[128,512]{1,0:T(8,128)(2,1)S(1)} %get-tuple-element.41.w_ref.refs_6_, bf16[15,30,128]{2,1,0:T(8,128)(2,1)S(1)} %collective-permute-done.3.refs_0_), custom_call_target="tpu_custom_call" | custom-call | flops 10000000 | bytes 1049088 | tf_op jit(solution)/shard_map/pallas_call | solution.py:360
  15.5 1.0 %shard_map.82 = (bf16[480,128]{1,0:T(8,128)(2,1)S(1)}, bf16[480,128]{1,0:T(8,128)(2,1)S(1)}, bf16[480,128]{1,0:T(8,128)(2,1)S(1)}, bf16[480,128]{1,0:T(8,128)(2,1)S(1)}, bf16[480,128]{1,0:T(8,128)(2,1)S(1)}) custom-call(f32[128,128]{1,0:T(8,128)S(1)} %get-tuple-element.38.live_ref, f32[960,128]{1,0:T(8,128)S(1)} %get-tuple-element.44.lt_ref, ...), custom_call_target="tpu_custom_call" | custom-call | flops 10000000 | bytes 1901568 | tf_op jit(solution)/shard_map/pallas_call | solution.py:360
  16.6 1.6 %collective-permute-start.6 = (bf16[480,128]{1,0:T(8,128)(2,1)S(1)}, bf16[480,128]{1,0:T(8,128)(2,1)S(1)}, u32[]{:S(2)}, u32[]{:S(2)}) collective-permute-start(bf16[480,128]{1,0:T(8,128)(2,1)S(1)} %get-tuple-element.49), channel_id=1, source_target_pairs={{0,1},{1,0},{2,3},{3,2},{4,5},{5,4},{6,7},{7,6},{8,9},{9,8},{10,11... | collective-permute-start | bytes 368648 | tf_op jit(solution)/shard_map/ppermute | solution.py:383
  18.1 1.5 %collective-permute-start.7 = (bf16[480,128]{1,0:T(8,128)(2,1)S(1)}, bf16[480,128]{1,0:T(8,128)(2,1)S(1)}, u32[]{:S(2)}, u32[]{:S(2)}) collective-permute-start(bf16[480,128]{1,0:T(8,128)(2,1)S(1)} %get-tuple-element.50), channel_id=1, source_target_pairs={{0,2},{1,3},{2,0},{3,1},{4,6},{5,7},{6,4},{7,5},{8,10},{9,11},{10,... | collective-permute-start | bytes 368648 | tf_op jit(solution)/shard_map/ppermute | solution.py:383
  20.1 2.1 %collective-permute-done.6.refs_1_ = bf16[480,128]{1,0:T(8,128)(2,1)S(1)} collective-permute-done((bf16[480,128]{1,0:T(8,128)(2,1)S(1)}, bf16[480,128]{1,0:T(8,128)(2,1)S(1)}, u32[]{:S(2)}, u32[]{:S(2)}) %collective-permute-start.6) | collective-permute-done | bytes 122912 | tf_op jit(solution)/shard_map/ppermute | solution.py:383
  22.2 1.2 %collective-permute-done.7.refs_2_ = bf16[480,128]{1,0:T(8,128)(2,1)S(1)} collective-permute-done((bf16[480,128]{1,0:T(8,128)(2,1)S(1)}, bf16[480,128]{1,0:T(8,128)(2,1)S(1)}, u32[]{:S(2)}, u32[]{:S(2)}) %collective-permute-start.7) | collective-permute-done | bytes 122912 | tf_op jit(solution)/shard_map/ppermute | solution.py:383
  23.5 1.9 %collective-permute-done.8.refs_3_ = bf16[480,128]{1,0:T(8,128)(2,1)S(1)} collective-permute-done((bf16[480,128]{1,0:T(8,128)(2,1)S(1)}, bf16[480,128]{1,0:T(8,128)(2,1)S(1)}, u32[]{:S(2)}, u32[]{:S(2)}) %collective-permute-start.8) | collective-permute-done | bytes 122912 | tf_op jit(solution)/shard_map/ppermute | solution.py:383
  26.4 1.5 %collective-permute-start.10 = (bf16[480,128]{1,0:T(8,128)(2,1)S(1)}, bf16[480,128]{1,0:T(8,128)(2,1)S(1)}, u32[]{:S(2)}, u32[]{:S(2)}) collective-permute-start(bf16[480,128]{1,0:T(8,128)(2,1)S(1)} %get-tuple-element.55.refs_1_), channel_id=1, source_target_pairs={{0,2},{1,3},{2,0},{3,1},{4,6},{5,7},{6,4},{7,5},{8,10},{9,11},{10,... | collective-permute-start | bytes 368648 | tf_op jit(solution)/shard_map/ppermute | solution.py:383
  28.0 1.5 %collective-permute-start.9 = (bf16[480,128]{1,0:T(8,128)(2,1)S(1)}, bf16[480,128]{1,0:T(8,128)(2,1)S(1)}, u32[]{:S(2)}, u32[]{:S(2)}) collective-permute-start(bf16[480,128]{1,0:T(8,128)(2,1)S(1)} %get-tuple-element.55.refs_1_), channel_id=1, source_target_pairs={{0,1},{1,0},{2,3},{3,2},{4,5},{5,4},{6,7},{7,6},{8,9},{9,8},{10,11... | collective-permute-start | bytes 368648 | tf_op jit(solution)/shard_map/ppermute | solution.py:383
  29.4 2.4 %collective-permute-done.11.refs_4_ = bf16[480,128]{1,0:T(8,128)(2,1)S(1)} collective-permute-done((bf16[480,128]{1,0:T(8,128)(2,1)S(1)}, bf16[480,128]{1,0:T(8,128)(2,1)S(1)}, u32[]{:S(2)}, u32[]{:S(2)}) %collective-permute-start.11) | collective-permute-done | bytes 122912 | tf_op jit(solution)/shard_map/ppermute | solution.py:383
  33.4 4.2 %collective-permute-start.16 = (bf16[480,128]{1,0:T(8,128)(2,1)S(1)}, bf16[480,128]{1,0:T(8,128)(2,1)S(1)}, u32[]{:S(2)}, u32[]{:S(2)}) collective-permute-start(bf16[480,128]{1,0:T(8,128)(2,1)S(1)} %shard_map.87), channel_id=1, source_target_pairs={{24,16},{28,20},{0,8},{4,12},{25,17},{29,21},{1,9},{5,13},{26,18},... | collective-permute-start | bytes 368648 | tf_op jit(solution)/shard_map/ppermute | solution.py:380
  38.4 2.9 %shard_map.84 = (f32[480,128]{1,0:T(8,128)S(1)}, bf16[480,128]{1,0:T(8,128)(2,1)S(1)}, f32[480,128]{1,0:T(8,128)S(1)}) custom-call(f32[960,128]{1,0:T(8,128)S(1)} %get-tuple-element.43.refs_0_, bf16[480,128]{1,0:T(8,128)(2,1)S(1)} %get-tuple-element.55.refs_1_, bf16[480,128]{1,0:T(8,128)(2,1)S(1)} %collective-permute-done.9.refs_2_, ...), custom_call_target="tpu_custom_call" | custom-call | flops 10000000 | bytes 2088960 | tf_op jit(solution)/shard_map/pallas_call | solution.py:360
  42.4 1.9 %collective-permute-start.15 = (bf16[480,128]{1,0:T(8,128)(2,1)S(1)}, bf16[480,128]{1,0:T(8,128)(2,1)S(1)}, u32[]{:S(2)}, u32[]{:S(2)}) collective-permute-start(bf16[480,128]{1,0:T(8,128)(2,1)S(1)} %shard_map.88), channel_id=1, source_target_pairs={{8,0},{12,4},{24,8},{28,12},{16,24},{20,28},{0,16},{4,20},{9,1},{1... | collective-permute-start | bytes 368648 | tf_op jit(solution)/shard_map/ppermute | solution.py:380
  45.8 0.9 %shard_map.86 = (bf16[15,30,128]{2,1,0:T(8,128)(2,1)}, f32[480,128]{1,0:T(8,128)S(1)}) custom-call(f32[480,128]{1,0:T(8,128)S(1)} %get-tuple-element.60.own_ref, bf16[480,128]{1,0:T(8,128)(2,1)S(1)} %collective-permute-done.12.got_ref, f32[480,128]{1,0:T(8,128)S(1)} %get-tuple-element.62.l1_ref, f32[480,128]{1,0:T(8,128)S(1)} %get-tuple-element.63.l2_ref, ...), custom_call_target="tpu_custom_call" | custom-call | flops 10000000 | bytes 1630720 | tf_op jit(solution)/shard_map/pallas_call | solution.py:360
  46.6 1.6 %collective-permute-done.15.refs_2_ = bf16[480,128]{1,0:T(8,128)(2,1)S(1)} collective-permute-done((bf16[480,128]{1,0:T(8,128)(2,1)S(1)}, bf16[480,128]{1,0:T(8,128)(2,1)S(1)}, u32[]{:S(2)}, u32[]{:S(2)}) %collective-permute-start.15) | collective-permute-done | bytes 122912 | tf_op jit(solution)/shard_map/ppermute | solution.py:380
  48.3 4.7 %collective-permute-done.17.refs_3_ = bf16[480,128]{1,0:T(8,128)(2,1)S(1)} collective-permute-done((bf16[480,128]{1,0:T(8,128)(2,1)S(1)}, bf16[480,128]{1,0:T(8,128)(2,1)S(1)}, u32[]{:S(2)}, u32[]{:S(2)}) %collective-permute-start.17) | collective-permute-done | bytes 122912 | tf_op jit(solution)/shard_map/ppermute | solution.py:380
  53.0 1.0 %shard_map.90 = bf16[15,30,128]{2,1,0:T(8,128)(2,1)} custom-call(f32[480,128]{1,0:T(8,128)S(1)} %get-tuple-element.68.refs_0_, bf16[480,128]{1,0:T(8,128)(2,1)S(1)} %collective-permute-done.14.refs_1_, bf16[480,128]{1,0:T(8,128)(2,1)S(1)} %collective-permute-done.15.refs_2_, bf16[480,128]{1,0:T(8,128)(2,1)S(1)} %collective-permute-done.17.refs_3_, ...), custom_call_target="tpu_custom_call" | custom-call | flops 10000000 | bytes 2089472 | tf_op jit(solution)/shard_map/pallas_call | solution.py:360
  (26 shorter events, 8.0 us)
Async XLA Ops:
  0.6 8.1 %collective-permute-start.2 = (bf16[15,30,128]{2,1,0:T(8,128)(2,1)}, bf16[15,30,128]{2,1,0:T(8,128)(2,1)S(1)}, u32[]{:S(2)}, u32[]{:S(2)}) collective-permute-start(bf16[15,30,128]{2,1,0:T(8,128)(2,1)} %refs_1_.1), channel_id=1, source_target_pairs={{0,16},{4,20},{24,8},{28,12},{8,0},{12,4},{16,24},{20,28},{1,17},{... | collective-permute-start | bytes 345608 | tf_op jit(solution)/shard_map/ppermute | solution.py:380
  4.7 6.4 %collective-permute-start.1 = (bf16[15,30,128]{2,1,0:T(8,128)(2,1)}, bf16[15,30,128]{2,1,0:T(8,128)(2,1)S(1)}, u32[]{:S(2)}, u32[]{:S(2)}) collective-permute-start(bf16[15,30,128]{2,1,0:T(8,128)(2,1)} %refs_2_.1), channel_id=1, source_target_pairs={{0,4},{4,0},{8,12},{12,8},{16,20},{20,16},{24,28},{28,24},{1,5},{5... | collective-permute-start | bytes 345608 | tf_op jit(solution)/shard_map/ppermute | solution.py:386
  4.8 6.4 %collective-permute-start = (bf16[15,30,128]{2,1,0:T(8,128)(2,1)}, bf16[15,30,128]{2,1,0:T(8,128)(2,1)S(1)}, u32[]{:S(2)}, u32[]{:S(2)}) collective-permute-start(bf16[15,30,128]{2,1,0:T(8,128)(2,1)} %refs_1_.1), channel_id=1, source_target_pairs={{0,4},{4,0},{8,12},{12,8},{16,20},{20,16},{24,28},{28,24},{1,5},{5... | collective-permute-start | bytes 345608 | tf_op jit(solution)/shard_map/ppermute | solution.py:386
  5.3 8.9 %collective-permute-start.3 = (bf16[15,30,128]{2,1,0:T(8,128)(2,1)}, bf16[15,30,128]{2,1,0:T(8,128)(2,1)S(1)}, u32[]{:S(2)}, u32[]{:S(2)}) collective-permute-start(bf16[15,30,128]{2,1,0:T(8,128)(2,1)} %refs_1_.1), channel_id=1, source_target_pairs={{0,8},{4,12},{8,24},{12,28},{24,16},{28,20},{16,0},{20,4},{1,9},{5... | collective-permute-start | bytes 345608 | tf_op jit(solution)/shard_map/ppermute | solution.py:380
  5.3 9.9 %collective-permute-start.4 = (bf16[15,30,128]{2,1,0:T(8,128)(2,1)}, bf16[15,30,128]{2,1,0:T(8,128)(2,1)S(1)}, u32[]{:S(2)}, u32[]{:S(2)}) collective-permute-start(bf16[15,30,128]{2,1,0:T(8,128)(2,1)} %refs_1_.1), channel_id=1, source_target_pairs={{8,16},{12,20},{16,8},{20,12},{9,17},{13,21},{17,9},{21,13},{10,18... | collective-permute-start | bytes 345608 | tf_op jit(solution)/shard_map/ppermute | solution.py:380
  8.8 6.8 %collective-permute-start.5 = (bf16[15,30,128]{2,1,0:T(8,128)(2,1)S(1)}, bf16[15,30,128]{2,1,0:T(8,128)(2,1)S(1)}, u32[]{:S(2)}, u32[]{:S(2)}) collective-permute-start(bf16[15,30,128]{2,1,0:T(8,128)(2,1)S(1)} %collective-permute-done.2.refs_0_), channel_id=1, source_target_pairs={{16,24},{20,28},{8,0},{12,4},{17,25},{21,29},{9,1},{13,5},{18,26},... | collective-permute-start | bytes 345608 | tf_op jit(solution)/shard_map/ppermute | solution.py:380
  16.6 5.7 %collective-permute-start.6 = (bf16[480,128]{1,0:T(8,128)(2,1)S(1)}, bf16[480,128]{1,0:T(8,128)(2,1)S(1)}, u32[]{:S(2)}, u32[]{:S(2)}) collective-permute-start(bf16[480,128]{1,0:T(8,128)(2,1)S(1)} %get-tuple-element.49), channel_id=1, source_target_pairs={{0,1},{1,0},{2,3},{3,2},{4,5},{5,4},{6,7},{7,6},{8,9},{9,8},{10,11... | collective-permute-start | bytes 368648 | tf_op jit(solution)/shard_map/ppermute | solution.py:383
  18.1 5.4 %collective-permute-start.7 = (bf16[480,128]{1,0:T(8,128)(2,1)S(1)}, bf16[480,128]{1,0:T(8,128)(2,1)S(1)}, u32[]{:S(2)}, u32[]{:S(2)}) collective-permute-start(bf16[480,128]{1,0:T(8,128)(2,1)S(1)} %get-tuple-element.50), channel_id=1, source_target_pairs={{0,2},{1,3},{2,0},{3,1},{4,6},{5,7},{6,4},{7,5},{8,10},{9,11},{10,... | collective-permute-start | bytes 368648 | tf_op jit(solution)/shard_map/ppermute | solution.py:383
  19.6 5.8 %collective-permute-start.8 = (bf16[480,128]{1,0:T(8,128)(2,1)S(1)}, bf16[480,128]{1,0:T(8,128)(2,1)S(1)}, u32[]{:S(2)}, u32[]{:S(2)}) collective-permute-start(bf16[480,128]{1,0:T(8,128)(2,1)S(1)} %get-tuple-element.51), channel_id=1, source_target_pairs={{0,3},{1,2},{2,1},{3,0},{4,7},{5,6},{6,5},{7,4},{8,11},{9,10},{10,... | collective-permute-start | bytes 368648 | tf_op jit(solution)/shard_map/ppermute | solution.py:383
  25.9 5.9 %collective-permute-start.11 = (bf16[480,128]{1,0:T(8,128)(2,1)S(1)}, bf16[480,128]{1,0:T(8,128)(2,1)S(1)}, u32[]{:S(2)}, u32[]{:S(2)}) collective-permute-start(bf16[480,128]{1,0:T(8,128)(2,1)S(1)} %get-tuple-element.55.refs_1_), channel_id=1, source_target_pairs={{0,3},{1,2},{2,1},{3,0},{4,7},{5,6},{6,5},{7,4},{8,11},{9,10},{10,... | collective-permute-start | bytes 368648 | tf_op jit(solution)/shard_map/ppermute | solution.py:383
  26.4 6.2 %collective-permute-start.10 = (bf16[480,128]{1,0:T(8,128)(2,1)S(1)}, bf16[480,128]{1,0:T(8,128)(2,1)S(1)}, u32[]{:S(2)}, u32[]{:S(2)}) collective-permute-start(bf16[480,128]{1,0:T(8,128)(2,1)S(1)} %get-tuple-element.55.refs_1_), channel_id=1, source_target_pairs={{0,2},{1,3},{2,0},{3,1},{4,6},{5,7},{6,4},{7,5},{8,10},{9,11},{10,... | collective-permute-start | bytes 368648 | tf_op jit(solution)/shard_map/ppermute | solution.py:383
  28.0 4.9 %collective-permute-start.9 = (bf16[480,128]{1,0:T(8,128)(2,1)S(1)}, bf16[480,128]{1,0:T(8,128)(2,1)S(1)}, u32[]{:S(2)}, u32[]{:S(2)}) collective-permute-start(bf16[480,128]{1,0:T(8,128)(2,1)S(1)} %get-tuple-element.55.refs_1_), channel_id=1, source_target_pairs={{0,1},{1,0},{2,3},{3,2},{4,5},{5,4},{6,7},{7,6},{8,9},{9,8},{10,11... | collective-permute-start | bytes 368648 | tf_op jit(solution)/shard_map/ppermute | solution.py:383
  33.4 10.8 %collective-permute-start.16 = (bf16[480,128]{1,0:T(8,128)(2,1)S(1)}, bf16[480,128]{1,0:T(8,128)(2,1)S(1)}, u32[]{:S(2)}, u32[]{:S(2)}) collective-permute-start(bf16[480,128]{1,0:T(8,128)(2,1)S(1)} %shard_map.87), channel_id=1, source_target_pairs={{24,16},{28,20},{0,8},{4,12},{25,17},{29,21},{1,9},{5,13},{26,18},... | collective-permute-start | bytes 368648 | tf_op jit(solution)/shard_map/ppermute | solution.py:380
  37.6 8.1 %collective-permute-start.13 = (bf16[480,128]{1,0:T(8,128)(2,1)S(1)}, bf16[480,128]{1,0:T(8,128)(2,1)S(1)}, u32[]{:S(2)}, u32[]{:S(2)}) collective-permute-start(bf16[480,128]{1,0:T(8,128)(2,1)S(1)} %get-tuple-element.66), channel_id=1, source_target_pairs={{0,4},{4,0},{8,12},{12,8},{16,20},{20,16},{24,28},{28,24},{1,5},{5... | collective-permute-start | bytes 368648 | tf_op jit(solution)/shard_map/ppermute | solution.py:386
  37.7 10.6 %collective-permute-start.14 = (bf16[480,128]{1,0:T(8,128)(2,1)S(1)}, bf16[480,128]{1,0:T(8,128)(2,1)S(1)}, u32[]{:S(2)}, u32[]{:S(2)}) collective-permute-start(bf16[480,128]{1,0:T(8,128)(2,1)S(1)} %shard_map.87), channel_id=1, source_target_pairs={{8,16},{12,20},{16,8},{20,12},{9,17},{13,21},{17,9},{21,13},{10,18... | collective-permute-start | bytes 368648 | tf_op jit(solution)/shard_map/ppermute | solution.py:380
  41.3 4.5 %collective-permute-start.12 = (bf16[480,128]{1,0:T(8,128)(2,1)S(1)}, bf16[480,128]{1,0:T(8,128)(2,1)S(1)}, u32[]{:S(2)}, u32[]{:S(2)}) collective-permute-start(bf16[480,128]{1,0:T(8,128)(2,1)S(1)} %get-tuple-element.61), channel_id=1, source_target_pairs={{0,4},{4,0},{8,12},{12,8},{16,20},{20,16},{24,28},{28,24},{1,5},{5... | collective-permute-start | bytes 368648 | tf_op jit(solution)/shard_map/ppermute | solution.py:386
  42.4 5.9 %collective-permute-start.15 = (bf16[480,128]{1,0:T(8,128)(2,1)S(1)}, bf16[480,128]{1,0:T(8,128)(2,1)S(1)}, u32[]{:S(2)}, u32[]{:S(2)}) collective-permute-start(bf16[480,128]{1,0:T(8,128)(2,1)S(1)} %shard_map.88), channel_id=1, source_target_pairs={{8,0},{12,4},{24,8},{28,12},{16,24},{20,28},{0,16},{4,20},{9,1},{1... | collective-permute-start | bytes 368648 | tf_op jit(solution)/shard_map/ppermute | solution.py:380
  44.8 8.1 %collective-permute-start.17 = (bf16[480,128]{1,0:T(8,128)(2,1)S(1)}, bf16[480,128]{1,0:T(8,128)(2,1)S(1)}, u32[]{:S(2)}, u32[]{:S(2)}) collective-permute-start(bf16[480,128]{1,0:T(8,128)(2,1)S(1)} %shard_map.89), channel_id=1, source_target_pairs={{16,0},{20,4},{8,24},{12,28},{0,8},{4,12},{24,16},{28,20},{17,1},{... | collective-permute-start | bytes 368648 | tf_op jit(solution)/shard_map/ppermute | solution.py:380

commit v5 on v4

--- a/solution.py
+++ b/solution.py
@@ -269,46 +269,48 @@
     grad_right_part(l_ref, gs, store, rows, cols)
 
 
-def grad_left_kernel(rows, cols, steps, *refs):
+def grad_left_part(piece_of, shard_of, first, blocks, ref, rows, cols):
+    pitch, half, channels = pad_to(cols, 16), pad_to(rows, 16), ref.shape[1]
+
+    def step(b, _):
+        def block_step(m, sums):
+            piece, shard = piece_of.at[m], shard_of.at[m]
+            sums = list(sums)
+            for j in range(rows):
+                right = tiles(shard[j * pitch : (j + 1) * pitch, :])
+                for n in range(JB):
+                    row = (first + b * JB + n) * half + j
+                    sums[n] = sums[n] + right * row_of(piece, row)[None]
+            return tuple(sums)
+
+        zero = jnp.zeros((pitch // 8, 8, channels), F32)
+        sums = lax.fori_loop(0, blocks, block_step, (zero,) * JB)
+        for n in range(JB):
+            at = pl.multiple_of((b * JB + n) * pitch, pitch)
+            ref[pl.ds(at, pitch), :] = sums[n].reshape(pitch, channels).astype(ref.dtype)
+        return 0
+
+    lax.fori_loop(0, rows // JB, step, 0)
+
+
+def pair_left_kernel(rows, cols, steps, *refs):
     blocks = len(steps)
-    l_ref, pieces, shards = refs[0], refs[1 : 1 + blocks], refs[1 + blocks : 1 + 2 * blocks]
-    own_ref, send_ref, right_ref, gs, rs = refs[1 + 2 * blocks :]
-    pitch, half = pad_to(cols, 16), pad_to(rows, 16)
-    chip = lax.axis_index("dap") // 2
-    column = lax.axis_index("ch")
+    pieces, shards, (send_ref, gs, rs) = refs[:blocks], refs[blocks : 2 * blocks], refs[2 * blocks :]
+    chip, column = this_chip(), lax.axis_index("ch")
     for t in range(blocks):
         gs[column ^ t] = pieces[t][...].astype(F32)
     for table, shard in zip(steps, shards):
         rs[chip ^ lookup(table, chip)] = shard[...].astype(F32)
-
-    def left_rows(first, ref):
-        def step(b, _):
-            def block_step(m, sums):
-                piece, shard = gs.at[m], rs.at[m]
-                sums = list(sums)
-                for j in range(rows):
-                    right = tiles(shard[j * pitch : (j + 1) * pitch, :])
-                    for n in range(JB):
-                        row = (first + b * JB + n) * half + j
-                        sums[n] = sums[n] + right * row_of(piece, row)[None]
-                return tuple(sums)
-
-            zero = jnp.zeros((pitch // 8, 8, gs.shape[2]), F32)
-            sums = lax.fori_loop(0, blocks, block_step, (zero,) * JB)
-            for n in range(JB):
-                at = pl.multiple_of((b * JB + n) * pitch, pitch)
-                ref[pl.ds(at, pitch), :] = sums[n].reshape(pitch, gs.shape[2]).astype(ref.dtype)
-            return 0
-
-        lax.fori_loop(0, rows // JB, step, 0)
-
-    left_rows(rows, send_ref)
-    left_rows(0, own_ref)
+    grad_left_part(gs, rs, rows, blocks, send_ref, rows, cols)
+
+
+def own_kernel(rows, cols, blocks, l_ref, gs, rs, left_ref, right_ref):
+    grad_left_part(gs, rs, 0, blocks, left_ref, rows, cols)
 
     def store(where, value):
         right_ref[where, :] = value
 
-    grad_right_part(l_ref, gs.at[chip], store, rows, cols)
+    grad_right_part(l_ref, gs.at[this_chip()], store, rows, cols)
 
 
 def finish_left_kernel(own_ref, got_ref, l1_ref, l2_ref, w_ref, wg_ref, upd_ref, logit_ref, back_ref,
@@ -430,11 +432,13 @@
         (send,) = call(functools.partial(send_right_kernel, rows, cols, blocks, table),
                        [((cells, hidden), BF16)], (left, *pieces, *more), [(mids, hidden)])
         got += [along_dap(send, pairs) for pairs in returns[n]]
-    left_own, left_send, right_own = call(
-        functools.partial(grad_left_kernel, rows, cols, steps),
-        [((cells, hidden), F32), ((cells, hidden), BF16), ((cells, hidden), F32)],
-        (left, *pieces, *rights), [(blocks, mids, hidden), (blocks, cells, hidden)])
+    left_send, staged, rights_staged = call(
+        functools.partial(pair_left_kernel, rows, cols, steps),
+        [((cells, hidden), BF16), ((blocks, mids, hidden), F32), ((blocks, cells, hidden), F32)], (*pieces, *rights))
     left_got = to_partner(left_send)
+    left_own, right_own = call(
+        functools.partial(own_kernel, rows, cols, blocks), [((cells, hidden), F32)] * 2,
+        (left, staged, rights_staged))
     normed, scale, l1, l2, r1, r2 = call(
         factor_kernel, [((cells, hidden), F32)] * 6, (live, xv, w_proj),
         [(cells, channels)])
@@ -448,14 +452,6 @@
 
 
 def gather_plan(blocks):
-    if blocks == 4:
-        moves = [
-            ([(0, 2), (3, 1), (1, 0), (2, 3)], None),
-            ([(0, 1), (1, 3), (3, 2), (2, 0)], None),
-            ([(1, 2), (2, 1)], None),
-            ([(2, 3), (1, 0)], 0),
-        ]
-        return moves, [([0], [1, 2, 2, 1]), ([1], [2, 1, 1, 2]), ([2, 3], [3] * 4)]
     order = [*range(2, blocks, 2), 1, *range(3, blocks, 2)]
     moves = []
     for s in order:
@@ -465,14 +461,6 @@
 
 
 def reduce_plan(blocks):
-    if blocks == 4:
-        sends = [([3] * 4, None), ([2, 1, 1, 2], None), ([1, 2, 2, 1], 0)]
-        returns = [
-            [[(3, 2), (0, 1)], [(1, 2), (2, 1)]],
-            [[(1, 0), (3, 1), (2, 3), (0, 2)]],
-            [[(2, 0), (1, 3), (0, 1), (3, 2)]],
-        ]
-        return sends, returns, [1, 2, 3]
     far = [*range(2, blocks), 1]
     sends = [([s] * blocks, None) for s in far]
     return sends, [[[(z, z ^ s) for z in range(blocks)]] for s in far], [*range(blocks - 1)]

time: 54.2 us -> 53.2 us (0.982)
  starting transfers between devices: 21.4 us -> 18.2 us
  waiting for transfers between devices: 18.2 us -> 20.2 us
    ppermute x8 -> x6, starting transfers between devices: 13.1 us -> 10.6 us  [along_dap(): lax.ppermute(value, 'dap', [(2 * a + c, 2 * b + c) for a, b in pairs for...]
    ppermute x8 -> x6, waiting for transfers between devices: 9.55 us -> 10.5 us  [along_dap(): lax.ppermute(value, 'dap', [(2 * a + c, 2 * b + c) for a, b in pairs for...]
    ppermute x6, waiting for transfers between devices: 8.69 us -> 9.66 us  [along_ch(): return lax.ppermute(value, 'ch', [(h, h ^ t) for h in range(blocks)])]
    ppermute x4, starting transfers between devices: 1.13 us -> 0.58 us  [to_partner(): return lax.ppermute(value, 'dap', [(d, d ^ 1) for d in range(devices)])]
    pallas_call x14 -> x15, Pallas kernels: 13.6 us -> 13.9 us  [call(): pl.pallas_call(body, out_shape=outs, in_specs=[specs] * len(args), out_sp...]
  transfers between devices with their start and end apart: 18 -> 16, of which waited for: 10 -> 8; matrix products, arithmetic and copies ran while one was open for 0% -> 0% of each run, Pallas kernels for 19% -> 21%
where the time goes in v5:
time: 53.2 us; the launch traced here: 53.1 us
  waiting for transfers between devices  20.2 us (38%)
  starting transfers between devices  18.2 us (34%)
  Pallas kernels  13.9 us (26%)
  between operations  0.79 us (1%)
    pallas_call x15, Pallas kernels, call(): pl.pallas_call(body, out_shape=outs, in_specs=[specs] * len(args), out_sp...  13.9 us
    ppermute x6, starting transfers between devices, along_dap(): lax.ppermute(value, 'dap', [(2 * a + c, 2 * b + c) for a, b in pairs for...  10.6 us
    ppermute x6, waiting for transfers between devices, along_dap(): lax.ppermute(value, 'dap', [(2 * a + c, 2 * b + c) for a, b in pairs for...  10.5 us
    ppermute x6, waiting for transfers between devices, along_ch(): return lax.ppermute(value, 'ch', [(h, h ^ t) for h in range(blocks)])  9.66 us
    ppermute x6, starting transfers between devices, along_ch(): return lax.ppermute(value, 'ch', [(h, h ^ t) for h in range(blocks)])  7.11 us
  transfers between devices with their start and end apart: 16, of which 8 were waited for; matrix products, arithmetic and copies ran while one was open for 0% of the time, Pallas kernels for 21%

profile of v5, /device:TPU:0, one launch (start us, length us, event | category | flops | bytes accessed | tf_op | source)
XLA Modules:
  0.0 53.1 jit_solution(16207572680878826385)
XLA Ops:
  0.6 4.1 %collective-permute-start.2 = (bf16[15,30,128]{2,1,0:T(8,128)(2,1)}, bf16[15,30,128]{2,1,0:T(8,128)(2,1)S(1)}, u32[]{:S(2)}, u32[]{:S(2)}) collective-permute-start(bf16[15,30,128]{2,1,0:T(8,128)(2,1)} %refs_1_.1), channel_id=1, source_target_pairs={{0,16},{4,20},{8,24},{12,28},{16,0},{20,4},{24,8},{28,12},{1,17},{... | collective-permute-start | bytes 345608 | tf_op jit(solution)/shard_map/ppermute | solution.py:382
  5.3 1.6 %collective-permute-start.3 = (bf16[15,30,128]{2,1,0:T(8,128)(2,1)}, bf16[15,30,128]{2,1,0:T(8,128)(2,1)S(1)}, u32[]{:S(2)}, u32[]{:S(2)}) collective-permute-start(bf16[15,30,128]{2,1,0:T(8,128)(2,1)} %refs_1_.1), channel_id=1, source_target_pairs={{0,8},{4,12},{8,0},{12,4},{16,24},{20,28},{24,16},{28,20},{1,9},{5... | collective-permute-start | bytes 345608 | tf_op jit(solution)/shard_map/ppermute | solution.py:382
  6.8 4.2 %collective-permute-done.2.refs_0_ = bf16[15,30,128]{2,1,0:T(8,128)(2,1)S(1)} collective-permute-done((bf16[15,30,128]{2,1,0:T(8,128)(2,1)}, bf16[15,30,128]{2,1,0:T(8,128)(2,1)S(1)}, u32[]{:S(2)}, u32[]{:S(2)}) %collective-permute-start.2) | collective-permute-done | bytes 115232 | tf_op jit(solution)/shard_map/ppermute | solution.py:382
  11.8 1.1 %shard_map.77 = (bf16[15,30,128]{2,1,0:T(8,128)(2,1)S(1)}, bf16[15,30,128]{2,1,0:T(8,128)(2,1)S(1)}, bf16[128,512]{1,0:T(8,128)(2,1)S(1)}, bf16[128,128]{1,0:T(8...) custom-call(s32[120]{0:T(128)} %refs_0_.1, bf16[15,30,128]{2,1,0:T(8,128)(2,1)} %refs_1_.1, ...), custom_call_target="tpu_custom_call" | custom-call | flops 10000000 | bytes 920032 | tf_op jit(solution)/shard_map/pallas_call | solution.py:362
  12.9 1.0 %shard_map.78 = (f32[960,128]{1,0:T(8,128)S(1)}, f32[960,128]{1,0:T(8,128)S(1)}, f32[480,128]{1,0:T(8,128)S(1)}, f32[480,128]{1,0:T(8,128)S(1)}) custom-call(f32[128,128]{1,0:T(8,128)S(1)} %get-tuple-element.40.live_ref, bf16[15,30,128]{2,1,0:T(8,128)(2,1)S(1)} %get-tuple-element.41.x_ref.refs_0_, bf16[15,30,128]{2,1,0:T(8,128)(2,1)S(1)} %collective-permute-done.xp_ref, ...), custom_call_target="tpu_custom_call" | custom-call | flops 10000000 | bytes 2164736 | tf_op jit(solution)/shard_map/pallas_call | solution.py:362
  13.9 1.0 %shard_map.79 = (bf16[480,128]{1,0:T(8,128)(2,1)S(1)}, bf16[480,128]{1,0:T(8,128)(2,1)S(1)}) custom-call(f32[128,128]{1,0:T(8,128)S(1)} %get-tuple-element.40.live_ref, f32[960,128]{1,0:T(8,128)S(1)} %get-tuple-element.46.lt_ref, bf16[128,512]{1,0:T(8,128)(2,1)S(1)} %get-tuple-element.43.w_ref.refs_6_, bf16[15,30,128]{2,1,0:T(8,128)(2,1)S(1)} %get-tuple-element.41.x_ref.refs_0_), custom_call_target="tpu_custom_call" | custom-call | flops 10000000 | bytes 1049088 | tf_op jit(solution)/shard_map/pallas_call | solution.py:362
  14.9 1.0 %shard_map.80 = (bf16[480,128]{1,0:T(8,128)(2,1)S(1)}, bf16[480,128]{1,0:T(8,128)(2,1)S(1)}) custom-call(f32[128,128]{1,0:T(8,128)S(1)} %get-tuple-element.40.live_ref, f32[960,128]{1,0:T(8,128)S(1)} %get-tuple-element.46.lt_ref, bf16[128,512]{1,0:T(8,128)(2,1)S(1)} %get-tuple-element.43.w_ref.refs_6_, bf16[15,30,128]{2,1,0:T(8,128)(2,1)S(1)} %collective-permute-done.2.refs_0_), custom_call_target="tpu_custom_call" | custom-call | flops 10000000 | bytes 1049088 | tf_op jit(solution)/shard_map/pallas_call | solution.py:362
  15.9 1.0 %shard_map.81 = (bf16[480,128]{1,0:T(8,128)(2,1)S(1)}, bf16[480,128]{1,0:T(8,128)(2,1)S(1)}) custom-call(f32[128,128]{1,0:T(8,128)S(1)} %get-tuple-element.40.live_ref, f32[960,128]{1,0:T(8,128)S(1)} %get-tuple-element.46.lt_ref, bf16[128,512]{1,0:T(8,128)(2,1)S(1)} %get-tuple-element.43.w_ref.refs_6_, bf16[15,30,128]{2,1,0:T(8,128)(2,1)S(1)} %collective-permute-done.3.refs_0_), custom_call_target="tpu_custom_call" | custom-call | flops 10000000 | bytes 1049088 | tf_op jit(solution)/shard_map/pallas_call | solution.py:362
  16.9 1.0 %shard_map.82 = (bf16[480,128]{1,0:T(8,128)(2,1)S(1)}, bf16[480,128]{1,0:T(8,128)(2,1)S(1)}, bf16[480,128]{1,0:T(8,128)(2,1)S(1)}, bf16[480,128]{1,0:T(8,128)(2,1)S(1)}, bf16[480,128]{1,0:T(8,128)(2,1)S(1)}) custom-call(f32[128,128]{1,0:T(8,128)S(1)} %get-tuple-element.40.live_ref, f32[960,128]{1,0:T(8,128)S(1)} %get-tuple-element.46.lt_ref, ...), custom_call_target="tpu_custom_call" | custom-call | flops 10000000 | bytes 1786368 | tf_op jit(solution)/shard_map/pallas_call | solution.py:362
  17.9 1.6 %collective-permute-start.5 = (bf16[480,128]{1,0:T(8,128)(2,1)S(1)}, bf16[480,128]{1,0:T(8,128)(2,1)S(1)}, u32[]{:S(2)}, u32[]{:S(2)}) collective-permute-start(bf16[480,128]{1,0:T(8,128)(2,1)S(1)} %get-tuple-element.51), channel_id=1, source_target_pairs={{0,1},{1,0},{2,3},{3,2},{4,5},{5,4},{6,7},{7,6},{8,9},{9,8},{10,11... | collective-permute-start | bytes 368648 | tf_op jit(solution)/shard_map/ppermute | solution.py:385
  19.5 1.5 %collective-permute-start.6 = (bf16[480,128]{1,0:T(8,128)(2,1)S(1)}, bf16[480,128]{1,0:T(8,128)(2,1)S(1)}, u32[]{:S(2)}, u32[]{:S(2)}) collective-permute-start(bf16[480,128]{1,0:T(8,128)(2,1)S(1)} %get-tuple-element.52), channel_id=1, source_target_pairs={{0,2},{1,3},{2,0},{3,1},{4,6},{5,7},{6,4},{7,5},{8,10},{9,11},{10,... | collective-permute-start | bytes 368648 | tf_op jit(solution)/shard_map/ppermute | solution.py:385
  21.5 1.7 %collective-permute-done.5.refs_1_ = bf16[480,128]{1,0:T(8,128)(2,1)S(1)} collective-permute-done((bf16[480,128]{1,0:T(8,128)(2,1)S(1)}, bf16[480,128]{1,0:T(8,128)(2,1)S(1)}, u32[]{:S(2)}, u32[]{:S(2)}) %collective-permute-start.5) | collective-permute-done | bytes 122912 | tf_op jit(solution)/shard_map/ppermute | solution.py:385
  23.2 3.8 %collective-permute-done.6.refs_2_ = bf16[480,128]{1,0:T(8,128)(2,1)S(1)} collective-permute-done((bf16[480,128]{1,0:T(8,128)(2,1)S(1)}, bf16[480,128]{1,0:T(8,128)(2,1)S(1)}, u32[]{:S(2)}, u32[]{:S(2)}) %collective-permute-start.6) | collective-permute-done | bytes 122912 | tf_op jit(solution)/shard_map/ppermute | solution.py:385
  27.5 1.1 %collective-permute-start.8 = (bf16[480,128]{1,0:T(8,128)(2,1)S(1)}, bf16[480,128]{1,0:T(8,128)(2,1)S(1)}, u32[]{:S(2)}, u32[]{:S(2)}) collective-permute-start(bf16[480,128]{1,0:T(8,128)(2,1)S(1)} %get-tuple-element.57.refs_0_.refs_1_), channel_id=1, source_target_pairs={{0,1},{1,0},{2,3},{3,2},{4,5},{5,4},{6,7},{7,6},{8,9},{9,8},{10,11... | collective-permute-start | bytes 368648 | tf_op jit(solution)/shard_map/ppermute | solution.py:385
  29.4 1.6 %collective-permute-start.10 = (bf16[480,128]{1,0:T(8,128)(2,1)S(1)}, bf16[480,128]{1,0:T(8,128)(2,1)S(1)}, u32[]{:S(2)}, u32[]{:S(2)}) collective-permute-start(bf16[480,128]{1,0:T(8,128)(2,1)S(1)} %get-tuple-element.57.refs_0_.refs_1_), channel_id=1, source_target_pairs={{0,3},{1,2},{2,1},{3,0},{4,7},{5,6},{6,5},{7,4},{8,11},{9,10},{10,... | collective-permute-start | bytes 368648 | tf_op jit(solution)/shard_map/ppermute | solution.py:385
  31.0 2.6 %collective-permute-done.8.refs_1_.refs_2_ = bf16[480,128]{1,0:T(8,128)(2,1)S(1)} collective-permute-done((bf16[480,128]{1,0:T(8,128)(2,1)S(1)}, bf16[480,128]{1,0:T(8,128)(2,1)S(1)}, u32[]{:S(2)}, u32[]{:S(2)}) %collective-permute-start.8) | collective-permute-done | bytes 122912 | tf_op jit(solution)/shard_map/ppermute | solution.py:385
  33.8 1.4 %collective-permute-done.10.refs_3_.refs_4_ = bf16[480,128]{1,0:T(8,128)(2,1)S(1)} collective-permute-done((bf16[480,128]{1,0:T(8,128)(2,1)S(1)}, bf16[480,128]{1,0:T(8,128)(2,1)S(1)}, u32[]{:S(2)}, u32[]{:S(2)}) %collective-permute-start.10) | collective-permute-done | bytes 122912 | tf_op jit(solution)/shard_map/ppermute | solution.py:385
  35.2 1.2 %shard_map.84 = (bf16[480,128]{1,0:T(8,128)(2,1)S(1)}, f32[4,480,128]{2,1,0:T(8,128)S(1)}, f32[4,480,128]{2,1,0:T(8,128)S(1)}) custom-call(bf16[480,128]{1,0:T(8,128)(2,1)S(1)} %get-tuple-element.57.refs_0_.refs_1_, bf16[480,128]{1,0:T(8,128)(2,1)S(1)} %collective-permute-done.8.refs_1_.refs_2_, bf16[480,128]{1,0:T(8,128)(2,1)S(1)} %collective-permute-done.9.refs_2_.refs_3_, ...), custom_call_target="tpu_custom_call" | custom-call | flops 10000000 | bytes 3072000 | tf_op jit(solution)/shard_map/pallas_call | solution.py:362
  37.1 3.4 %collective-permute-start.13 = (bf16[480,128]{1,0:T(8,128)(2,1)S(1)}, bf16[480,128]{1,0:T(8,128)(2,1)S(1)}, u32[]{:S(2)}, u32[]{:S(2)}) collective-permute-start(bf16[480,128]{1,0:T(8,128)(2,1)S(1)} %shard_map.88), channel_id=1, source_target_pairs={{0,16},{4,20},{8,24},{12,28},{16,0},{20,4},{24,8},{28,12},{1,17},{... | collective-permute-start | bytes 368648 | tf_op jit(solution)/shard_map/ppermute | solution.py:382
  43.1 1.7 %shard_map.85 = (f32[480,128]{1,0:T(8,128)S(1)}, f32[480,128]{1,0:T(8,128)S(1)}) custom-call(f32[960,128]{1,0:T(8,128)S(1)} %get-tuple-element.45.l_ref.refs_0_, f32[4,480,128]{2,1,0:T(8,128)S(1)} %get-tuple-element.62.gs, f32[4,480,128]{2,1,0:T(8,128)S(1)} %get-tuple-element.63.rs), custom_call_target="tpu_custom_call" | custom-call | flops 10000000 | bytes 2949120 | tf_op jit(solution)/shard_map/pallas_call | solution.py:362
  44.8 0.9 %shard_map.87 = (bf16[15,30,128]{2,1,0:T(8,128)(2,1)}, f32[480,128]{1,0:T(8,128)S(1)}) custom-call(f32[480,128]{1,0:T(8,128)S(1)} %get-tuple-element.64.own_ref, bf16[480,128]{1,0:T(8,128)(2,1)S(1)} %collective-permute-done.11.got_ref, f32[480,128]{1,0:T(8,128)S(1)} %get-tuple-element.66.l1_ref, f32[480,128]{1,0:T(8,128)S(1)} %get-tuple-element.67.l2_ref, ...), custom_call_target="tpu_custom_call" | custom-call | flops 10000000 | bytes 1630720 | tf_op jit(solution)/shard_map/pallas_call | solution.py:362
  45.7 3.8 %collective-permute-done.13.refs_1_ = bf16[480,128]{1,0:T(8,128)(2,1)S(1)} collective-permute-done((bf16[480,128]{1,0:T(8,128)(2,1)S(1)}, bf16[480,128]{1,0:T(8,128)(2,1)S(1)}, u32[]{:S(2)}, u32[]{:S(2)}) %collective-permute-start.13) | collective-permute-done | bytes 122912 | tf_op jit(solution)/shard_map/ppermute | solution.py:382
  49.5 2.5 %collective-permute-done.15.refs_3_ = bf16[480,128]{1,0:T(8,128)(2,1)S(1)} collective-permute-done((bf16[480,128]{1,0:T(8,128)(2,1)S(1)}, bf16[480,128]{1,0:T(8,128)(2,1)S(1)}, u32[]{:S(2)}, u32[]{:S(2)}) %collective-permute-start.15) | collective-permute-done | bytes 122912 | tf_op jit(solution)/shard_map/ppermute | solution.py:382
  52.0 1.0 %shard_map.91 = bf16[15,30,128]{2,1,0:T(8,128)(2,1)} custom-call(f32[480,128]{1,0:T(8,128)S(1)} %get-tuple-element.72.refs_0_, bf16[480,128]{1,0:T(8,128)(2,1)S(1)} %collective-permute-done.13.refs_1_, bf16[480,128]{1,0:T(8,128)(2,1)S(1)} %collective-permute-done.14.refs_2_, bf16[480,128]{1,0:T(8,128)(2,1)S(1)} %collective-permute-done.15.refs_3_, ...), custom_call_target="tpu_custom_call" | custom-call | flops 10000000 | bytes 2089472 | tf_op jit(solution)/shard_map/pallas_call | solution.py:362
  (23 shorter events, 6.5 us)
Async XLA Ops:
  0.6 10.4 %collective-permute-start.2 = (bf16[15,30,128]{2,1,0:T(8,128)(2,1)}, bf16[15,30,128]{2,1,0:T(8,128)(2,1)S(1)}, u32[]{:S(2)}, u32[]{:S(2)}) collective-permute-start(bf16[15,30,128]{2,1,0:T(8,128)(2,1)} %refs_1_.1), channel_id=1, source_target_pairs={{0,16},{4,20},{8,24},{12,28},{16,0},{20,4},{24,8},{28,12},{1,17},{... | collective-permute-start | bytes 345608 | tf_op jit(solution)/shard_map/ppermute | solution.py:382
  4.8 8.1 %collective-permute-start = (bf16[15,30,128]{2,1,0:T(8,128)(2,1)}, bf16[15,30,128]{2,1,0:T(8,128)(2,1)S(1)}, u32[]{:S(2)}, u32[]{:S(2)}) collective-permute-start(bf16[15,30,128]{2,1,0:T(8,128)(2,1)} %refs_1_.1), channel_id=1, source_target_pairs={{0,4},{4,0},{8,12},{12,8},{16,20},{20,16},{24,28},{28,24},{1,5},{5... | collective-permute-start | bytes 345608 | tf_op jit(solution)/shard_map/ppermute | solution.py:388
  4.8 8.1 %collective-permute-start.1 = (bf16[15,30,128]{2,1,0:T(8,128)(2,1)}, bf16[15,30,128]{2,1,0:T(8,128)(2,1)S(1)}, u32[]{:S(2)}, u32[]{:S(2)}) collective-permute-start(bf16[15,30,128]{2,1,0:T(8,128)(2,1)} %refs_2_.1), channel_id=1, source_target_pairs={{0,4},{4,0},{8,12},{12,8},{16,20},{20,16},{24,28},{28,24},{1,5},{5... | collective-permute-start | bytes 345608 | tf_op jit(solution)/shard_map/ppermute | solution.py:388
  5.3 10.6 %collective-permute-start.3 = (bf16[15,30,128]{2,1,0:T(8,128)(2,1)}, bf16[15,30,128]{2,1,0:T(8,128)(2,1)S(1)}, u32[]{:S(2)}, u32[]{:S(2)}) collective-permute-start(bf16[15,30,128]{2,1,0:T(8,128)(2,1)} %refs_1_.1), channel_id=1, source_target_pairs={{0,8},{4,12},{8,0},{12,4},{16,24},{20,28},{24,16},{28,20},{1,9},{5... | collective-permute-start | bytes 345608 | tf_op jit(solution)/shard_map/ppermute | solution.py:382
  11.0 5.9 %collective-permute-start.4 = (bf16[15,30,128]{2,1,0:T(8,128)(2,1)S(1)}, bf16[15,30,128]{2,1,0:T(8,128)(2,1)S(1)}, u32[]{:S(2)}, u32[]{:S(2)}) collective-permute-start(bf16[15,30,128]{2,1,0:T(8,128)(2,1)S(1)} %collective-permute-done.2.refs_0_), channel_id=1, source_target_pairs={{0,8},{4,12},{8,0},{12,4},{16,24},{20,28},{24,16},{28,20},{1,9},{5... | collective-permute-start | bytes 345608 | tf_op jit(solution)/shard_map/ppermute | solution.py:382
  17.9 5.2 %collective-permute-start.5 = (bf16[480,128]{1,0:T(8,128)(2,1)S(1)}, bf16[480,128]{1,0:T(8,128)(2,1)S(1)}, u32[]{:S(2)}, u32[]{:S(2)}) collective-permute-start(bf16[480,128]{1,0:T(8,128)(2,1)S(1)} %get-tuple-element.51), channel_id=1, source_target_pairs={{0,1},{1,0},{2,3},{3,2},{4,5},{5,4},{6,7},{7,6},{8,9},{9,8},{10,11... | collective-permute-start | bytes 368648 | tf_op jit(solution)/shard_map/ppermute | solution.py:385
  19.5 7.5 %collective-permute-start.6 = (bf16[480,128]{1,0:T(8,128)(2,1)S(1)}, bf16[480,128]{1,0:T(8,128)(2,1)S(1)}, u32[]{:S(2)}, u32[]{:S(2)}) collective-permute-start(bf16[480,128]{1,0:T(8,128)(2,1)S(1)} %get-tuple-element.52), channel_id=1, source_target_pairs={{0,2},{1,3},{2,0},{3,1},{4,6},{5,7},{6,4},{7,5},{8,10},{9,11},{10,... | collective-permute-start | bytes 368648 | tf_op jit(solution)/shard_map/ppermute | solution.py:385
  21.0 6.0 %collective-permute-start.7 = (bf16[480,128]{1,0:T(8,128)(2,1)S(1)}, bf16[480,128]{1,0:T(8,128)(2,1)S(1)}, u32[]{:S(2)}, u32[]{:S(2)}) collective-permute-start(bf16[480,128]{1,0:T(8,128)(2,1)S(1)} %get-tuple-element.53), channel_id=1, source_target_pairs={{0,3},{1,2},{2,1},{3,0},{4,7},{5,6},{6,5},{7,4},{8,11},{9,10},{10,... | collective-permute-start | bytes 368648 | tf_op jit(solution)/shard_map/ppermute | solution.py:385
  27.5 6.1 %collective-permute-start.8 = (bf16[480,128]{1,0:T(8,128)(2,1)S(1)}, bf16[480,128]{1,0:T(8,128)(2,1)S(1)}, u32[]{:S(2)}, u32[]{:S(2)}) collective-permute-start(bf16[480,128]{1,0:T(8,128)(2,1)S(1)} %get-tuple-element.57.refs_0_.refs_1_), channel_id=1, source_target_pairs={{0,1},{1,0},{2,3},{3,2},{4,5},{5,4},{6,7},{7,6},{8,9},{9,8},{10,11... | collective-permute-start | bytes 368648 | tf_op jit(solution)/shard_map/ppermute | solution.py:385
  28.6 5.2 %collective-permute-start.9 = (bf16[480,128]{1,0:T(8,128)(2,1)S(1)}, bf16[480,128]{1,0:T(8,128)(2,1)S(1)}, u32[]{:S(2)}, u32[]{:S(2)}) collective-permute-start(bf16[480,128]{1,0:T(8,128)(2,1)S(1)} %get-tuple-element.57.refs_0_.refs_1_), channel_id=1, source_target_pairs={{0,2},{1,3},{2,0},{3,1},{4,6},{5,7},{6,4},{7,5},{8,10},{9,11},{10,... | collective-permute-start | bytes 368648 | tf_op jit(solution)/shard_map/ppermute | solution.py:385
  29.4 5.8 %collective-permute-start.10 = (bf16[480,128]{1,0:T(8,128)(2,1)S(1)}, bf16[480,128]{1,0:T(8,128)(2,1)S(1)}, u32[]{:S(2)}, u32[]{:S(2)}) collective-permute-start(bf16[480,128]{1,0:T(8,128)(2,1)S(1)} %get-tuple-element.57.refs_0_.refs_1_), channel_id=1, source_target_pairs={{0,3},{1,2},{2,1},{3,0},{4,7},{5,6},{6,5},{7,4},{8,11},{9,10},{10,... | collective-permute-start | bytes 368648 | tf_op jit(solution)/shard_map/ppermute | solution.py:385
  31.0 13.8 %collective-permute-start.12 = (bf16[480,128]{1,0:T(8,128)(2,1)S(1)}, bf16[480,128]{1,0:T(8,128)(2,1)S(1)}, u32[]{:S(2)}, u32[]{:S(2)}) collective-permute-start(bf16[480,128]{1,0:T(8,128)(2,1)S(1)} %get-tuple-element.70), channel_id=1, source_target_pairs={{0,4},{4,0},{8,12},{12,8},{16,20},{20,16},{24,28},{28,24},{1,5},{5... | collective-permute-start | bytes 368648 | tf_op jit(solution)/shard_map/ppermute | solution.py:388
  36.4 8.4 %collective-permute-start.11 = (bf16[480,128]{1,0:T(8,128)(2,1)S(1)}, bf16[480,128]{1,0:T(8,128)(2,1)S(1)}, u32[]{:S(2)}, u32[]{:S(2)}) collective-permute-start(bf16[480,128]{1,0:T(8,128)(2,1)S(1)} %get-tuple-element.65), channel_id=1, source_target_pairs={{0,4},{4,0},{8,12},{12,8},{16,20},{20,16},{24,28},{28,24},{1,5},{5... | collective-permute-start | bytes 368648 | tf_op jit(solution)/shard_map/ppermute | solution.py:388
  37.1 12.4 %collective-permute-start.13 = (bf16[480,128]{1,0:T(8,128)(2,1)S(1)}, bf16[480,128]{1,0:T(8,128)(2,1)S(1)}, u32[]{:S(2)}, u32[]{:S(2)}) collective-permute-start(bf16[480,128]{1,0:T(8,128)(2,1)S(1)} %shard_map.88), channel_id=1, source_target_pairs={{0,16},{4,20},{8,24},{12,28},{16,0},{20,4},{24,8},{28,12},{1,17},{... | collective-permute-start | bytes 368648 | tf_op jit(solution)/shard_map/ppermute | solution.py:382
  41.1 8.4 %collective-permute-start.14 = (bf16[480,128]{1,0:T(8,128)(2,1)S(1)}, bf16[480,128]{1,0:T(8,128)(2,1)S(1)}, u32[]{:S(2)}, u32[]{:S(2)}) collective-permute-start(bf16[480,128]{1,0:T(8,128)(2,1)S(1)} %shard_map.89), channel_id=1, source_target_pairs={{0,24},{4,28},{8,16},{12,20},{16,8},{20,12},{24,0},{28,4},{1,25},{... | collective-permute-start | bytes 368648 | tf_op jit(solution)/shard_map/ppermute | solution.py:382
  41.9 10.2 %collective-permute-start.15 = (bf16[480,128]{1,0:T(8,128)(2,1)S(1)}, bf16[480,128]{1,0:T(8,128)(2,1)S(1)}, u32[]{:S(2)}, u32[]{:S(2)}) collective-permute-start(bf16[480,128]{1,0:T(8,128)(2,1)S(1)} %shard_map.90), channel_id=1, source_target_pairs={{0,8},{4,12},{8,0},{12,4},{16,24},{20,28},{24,16},{28,20},{1,9},{5... | collective-permute-start | bytes 368648 | tf_op jit(solution)/shard_map/ppermute | solution.py:382

commit v6 on v5

--- a/solution.py
+++ b/solution.py
@@ -166,6 +166,14 @@
     return value
 
 
+def turn_of(n, blocks, core):
+    return n if core == 0 or n == 0 else blocks - n
+
+
+def my_turn(n, blocks):
+    return jnp.where(lax.axis_index("dap") % 2 == 0, turn_of(n, blocks, 0), turn_of(n, blocks, 1))
+
+
 def this_chip():
     return lax.axis_index("dap") // 2
 
@@ -209,7 +217,7 @@
     held[last] = ps[: held.shape[1], :].astype(BF16)
     turn = chip ^ lax.axis_index("ch")
     for t in range(blocks):
-        outs[t][...] = held[turn ^ t]
+        outs[t][...] = held[turn ^ my_turn(t, blocks)]
 
 
 def middle_kernel(blocks, *refs):
@@ -257,7 +265,7 @@
     chip, column = this_chip(), lax.axis_index("ch")
     step = lookup(steps, chip)
     for t in range(blocks):
-        @pl.when(chip ^ column ^ step == t)
+        @pl.when(chip ^ column ^ step == my_turn(t, blocks))
         def _(t=t):
             gs[...] = pieces[t][...].astype(F32)
 
@@ -298,7 +306,7 @@
     pieces, shards, (send_ref, gs, rs) = refs[:blocks], refs[blocks : 2 * blocks], refs[2 * blocks :]
     chip, column = this_chip(), lax.axis_index("ch")
     for t in range(blocks):
-        gs[column ^ t] = pieces[t][...].astype(F32)
+        gs[column ^ my_turn(t, blocks)] = pieces[t][...].astype(F32)
     for table, shard in zip(steps, shards):
         rs[chip ^ lookup(table, chip)] = shard[...].astype(F32)
     grad_left_part(gs, rs, rows, blocks, send_ref, rows, cols)
@@ -382,7 +390,8 @@
         return lax.ppermute(value, "dap", [(2 * a + c, 2 * b + c) for a, b in pairs for c in range(2)])
 
     def along_ch(value, t):
-        return lax.ppermute(value, "ch", [(h, h ^ t) for h in range(blocks)])
+        return lax.ppermute(value, ("dap", "ch"), [
+            (d * blocks + h, d * blocks + (h ^ turn_of(t, blocks, d % 2))) for d in range(devices) for h in range(blocks)])
 
     def to_partner(value):
         return lax.ppermute(value, "dap", [(d, d ^ 1) for d in range(devices)])

time: 53.2 us -> 53.9 us (1.013)
  waiting for transfers between devices: 20.2 us -> 20.9 us
    ppermute x6, waiting for transfers between devices: 9.66 us -> 10.3 us  [along_ch(): lax.ppermute(value, ('dap', 'ch'), [(d * blocks + h, d * blocks + (h ^ tu...]
  transfers between devices with their start and end apart: 16 -> 16, of which waited for: 8 -> 9; matrix products, arithmetic and copies ran while one was open for 0% -> 0% of each run, Pallas kernels for 21% -> 21%
where the time goes in v6:
time: 53.9 us; the launch traced here: 53.7 us
  waiting for transfers between devices  20.9 us (39%)
  starting transfers between devices  18.2 us (34%)
  Pallas kernels  13.9 us (26%)
  between operations  0.79 us (1%)
    pallas_call x15, Pallas kernels, call(): pl.pallas_call(body, out_shape=outs, in_specs=[specs] * len(args), out_sp...  13.9 us
    ppermute x6, waiting for transfers between devices, along_dap(): lax.ppermute(value, 'dap', [(2 * a + c, 2 * b + c) for a, b in pairs for...  10.5 us
    ppermute x6, starting transfers between devices, along_dap(): lax.ppermute(value, 'dap', [(2 * a + c, 2 * b + c) for a, b in pairs for...  10.5 us
    ppermute x6, waiting for transfers between devices, along_ch(): lax.ppermute(value, ('dap', 'ch'), [(d * blocks + h, d * blocks + (h ^ tu...  10.3 us
    ppermute x6, starting transfers between devices, along_ch(): lax.ppermute(value, ('dap', 'ch'), [(d * blocks + h, d * blocks + (h ^ tu...  7.11 us
  transfers between devices with their start and end apart: 16, of which 9 were waited for; matrix products, arithmetic and copies ran while one was open for 0% of the time, Pallas kernels for 21%

profile of v6, /device:TPU:0, one launch (start us, length us, event | category | flops | bytes accessed | tf_op | source)
XLA Modules:
  0.0 53.7 jit_solution(10894754185512530006)
XLA Ops:
  0.6 4.1 %collective-permute-start.2 = (bf16[15,30,128]{2,1,0:T(8,128)(2,1)}, bf16[15,30,128]{2,1,0:T(8,128)(2,1)S(1)}, u32[]{:S(2)}, u32[]{:S(2)}) collective-permute-start(bf16[15,30,128]{2,1,0:T(8,128)(2,1)} %refs_1_.1), channel_id=1, source_target_pairs={{0,16},{4,20},{8,24},{12,28},{16,0},{20,4},{24,8},{28,12},{1,17},{... | collective-permute-start | bytes 345608 | tf_op jit(solution)/shard_map/ppermute | solution.py:390
  5.3 1.6 %collective-permute-start.3 = (bf16[15,30,128]{2,1,0:T(8,128)(2,1)}, bf16[15,30,128]{2,1,0:T(8,128)(2,1)S(1)}, u32[]{:S(2)}, u32[]{:S(2)}) collective-permute-start(bf16[15,30,128]{2,1,0:T(8,128)(2,1)} %refs_1_.1), channel_id=1, source_target_pairs={{0,8},{4,12},{8,0},{12,4},{16,24},{20,28},{24,16},{28,20},{1,9},{5... | collective-permute-start | bytes 345608 | tf_op jit(solution)/shard_map/ppermute | solution.py:390
  6.8 4.2 %collective-permute-done.2.refs_0_ = bf16[15,30,128]{2,1,0:T(8,128)(2,1)S(1)} collective-permute-done((bf16[15,30,128]{2,1,0:T(8,128)(2,1)}, bf16[15,30,128]{2,1,0:T(8,128)(2,1)S(1)}, u32[]{:S(2)}, u32[]{:S(2)}) %collective-permute-start.2) | collective-permute-done | bytes 115232 | tf_op jit(solution)/shard_map/ppermute | solution.py:390
  11.8 1.1 %shard_map.77 = (bf16[15,30,128]{2,1,0:T(8,128)(2,1)S(1)}, bf16[15,30,128]{2,1,0:T(8,128)(2,1)S(1)}, bf16[128,512]{1,0:T(8,128)(2,1)S(1)}, bf16[128,128]{1,0:T(8...) custom-call(s32[120]{0:T(128)} %refs_0_.1, bf16[15,30,128]{2,1,0:T(8,128)(2,1)} %refs_1_.1, ...), custom_call_target="tpu_custom_call" | custom-call | flops 10000000 | bytes 920032 | tf_op jit(solution)/shard_map/pallas_call | solution.py:370
  12.9 1.0 %shard_map.78 = (f32[960,128]{1,0:T(8,128)S(1)}, f32[960,128]{1,0:T(8,128)S(1)}, f32[480,128]{1,0:T(8,128)S(1)}, f32[480,128]{1,0:T(8,128)S(1)}) custom-call(f32[128,128]{1,0:T(8,128)S(1)} %get-tuple-element.40.live_ref, bf16[15,30,128]{2,1,0:T(8,128)(2,1)S(1)} %get-tuple-element.41.x_ref.refs_0_, bf16[15,30,128]{2,1,0:T(8,128)(2,1)S(1)} %collective-permute-done.xp_ref, ...), custom_call_target="tpu_custom_call" | custom-call | flops 10000000 | bytes 2164736 | tf_op jit(solution)/shard_map/pallas_call | solution.py:370
  13.9 1.0 %shard_map.79 = (bf16[480,128]{1,0:T(8,128)(2,1)S(1)}, bf16[480,128]{1,0:T(8,128)(2,1)S(1)}) custom-call(f32[128,128]{1,0:T(8,128)S(1)} %get-tuple-element.40.live_ref, f32[960,128]{1,0:T(8,128)S(1)} %get-tuple-element.46.lt_ref, bf16[128,512]{1,0:T(8,128)(2,1)S(1)} %get-tuple-element.43.w_ref.refs_6_, bf16[15,30,128]{2,1,0:T(8,128)(2,1)S(1)} %get-tuple-element.41.x_ref.refs_0_), custom_call_target="tpu_custom_call" | custom-call | flops 10000000 | bytes 1049088 | tf_op jit(solution)/shard_map/pallas_call | solution.py:370
  14.9 1.0 %shard_map.80 = (bf16[480,128]{1,0:T(8,128)(2,1)S(1)}, bf16[480,128]{1,0:T(8,128)(2,1)S(1)}) custom-call(f32[128,128]{1,0:T(8,128)S(1)} %get-tuple-element.40.live_ref, f32[960,128]{1,0:T(8,128)S(1)} %get-tuple-element.46.lt_ref, bf16[128,512]{1,0:T(8,128)(2,1)S(1)} %get-tuple-element.43.w_ref.refs_6_, bf16[15,30,128]{2,1,0:T(8,128)(2,1)S(1)} %collective-permute-done.2.refs_0_), custom_call_target="tpu_custom_call" | custom-call | flops 10000000 | bytes 1049088 | tf_op jit(solution)/shard_map/pallas_call | solution.py:370
  15.9 1.0 %shard_map.81 = (bf16[480,128]{1,0:T(8,128)(2,1)S(1)}, bf16[480,128]{1,0:T(8,128)(2,1)S(1)}) custom-call(f32[128,128]{1,0:T(8,128)S(1)} %get-tuple-element.40.live_ref, f32[960,128]{1,0:T(8,128)S(1)} %get-tuple-element.46.lt_ref, bf16[128,512]{1,0:T(8,128)(2,1)S(1)} %get-tuple-element.43.w_ref.refs_6_, bf16[15,30,128]{2,1,0:T(8,128)(2,1)S(1)} %collective-permute-done.3.refs_0_), custom_call_target="tpu_custom_call" | custom-call | flops 10000000 | bytes 1049088 | tf_op jit(solution)/shard_map/pallas_call | solution.py:370
  16.9 1.0 %shard_map.82 = (bf16[480,128]{1,0:T(8,128)(2,1)S(1)}, bf16[480,128]{1,0:T(8,128)(2,1)S(1)}, bf16[480,128]{1,0:T(8,128)(2,1)S(1)}, bf16[480,128]{1,0:T(8,128)(2,1)S(1)}, bf16[480,128]{1,0:T(8,128)(2,1)S(1)}) custom-call(f32[128,128]{1,0:T(8,128)S(1)} %get-tuple-element.40.live_ref, f32[960,128]{1,0:T(8,128)S(1)} %get-tuple-element.46.lt_ref, ...), custom_call_target="tpu_custom_call" | custom-call | flops 10000000 | bytes 1786368 | tf_op jit(solution)/shard_map/pallas_call | solution.py:370
  17.9 1.6 %collective-permute-start.5 = (bf16[480,128]{1,0:T(8,128)(2,1)S(1)}, bf16[480,128]{1,0:T(8,128)(2,1)S(1)}, u32[]{:S(2)}, u32[]{:S(2)}) collective-permute-start(bf16[480,128]{1,0:T(8,128)(2,1)S(1)} %get-tuple-element.51), channel_id=1, source_target_pairs={{0,1},{1,0},{2,3},{3,2},{4,7},{5,6},{6,5},{7,4},{8,9},{9,8},{10,11... | collective-permute-start | bytes 368648 | tf_op jit(solution)/shard_map/ppermute | solution.py:393
  19.5 1.5 %collective-permute-start.6 = (bf16[480,128]{1,0:T(8,128)(2,1)S(1)}, bf16[480,128]{1,0:T(8,128)(2,1)S(1)}, u32[]{:S(2)}, u32[]{:S(2)}) collective-permute-start(bf16[480,128]{1,0:T(8,128)(2,1)S(1)} %get-tuple-element.52), channel_id=1, source_target_pairs={{0,2},{1,3},{2,0},{3,1},{4,6},{5,7},{6,4},{7,5},{8,10},{9,11},{10,... | collective-permute-start | bytes 368648 | tf_op jit(solution)/shard_map/ppermute | solution.py:393
  21.5 2.7 %collective-permute-done.5.refs_1_ = bf16[480,128]{1,0:T(8,128)(2,1)S(1)} collective-permute-done((bf16[480,128]{1,0:T(8,128)(2,1)S(1)}, bf16[480,128]{1,0:T(8,128)(2,1)S(1)}, u32[]{:S(2)}, u32[]{:S(2)}) %collective-permute-start.5) | collective-permute-done | bytes 122912 | tf_op jit(solution)/shard_map/ppermute | solution.py:393
  25.2 1.6 %collective-permute-done.7.refs_3_ = bf16[480,128]{1,0:T(8,128)(2,1)S(1)} collective-permute-done((bf16[480,128]{1,0:T(8,128)(2,1)S(1)}, bf16[480,128]{1,0:T(8,128)(2,1)S(1)}, u32[]{:S(2)}, u32[]{:S(2)}) %collective-permute-start.7) | collective-permute-done | bytes 122912 | tf_op jit(solution)/shard_map/ppermute | solution.py:393
  27.3 1.3 %collective-permute-start.8 = (bf16[480,128]{1,0:T(8,128)(2,1)S(1)}, bf16[480,128]{1,0:T(8,128)(2,1)S(1)}, u32[]{:S(2)}, u32[]{:S(2)}) collective-permute-start(bf16[480,128]{1,0:T(8,128)(2,1)S(1)} %get-tuple-element.57.refs_0_.refs_1_), channel_id=1, source_target_pairs={{0,1},{1,0},{2,3},{3,2},{4,7},{5,6},{6,5},{7,4},{8,9},{9,8},{10,11... | collective-permute-start | bytes 368648 | tf_op jit(solution)/shard_map/ppermute | solution.py:393
  28.5 1.5 %collective-permute-start.9 = (bf16[480,128]{1,0:T(8,128)(2,1)S(1)}, bf16[480,128]{1,0:T(8,128)(2,1)S(1)}, u32[]{:S(2)}, u32[]{:S(2)}) collective-permute-start(bf16[480,128]{1,0:T(8,128)(2,1)S(1)} %get-tuple-element.57.refs_0_.refs_1_), channel_id=1, source_target_pairs={{0,2},{1,3},{2,0},{3,1},{4,6},{5,7},{6,4},{7,5},{8,10},{9,11},{10,... | collective-permute-start | bytes 368648 | tf_op jit(solution)/shard_map/ppermute | solution.py:393
  30.8 1.7 %collective-permute-done.8.refs_1_.refs_2_ = bf16[480,128]{1,0:T(8,128)(2,1)S(1)} collective-permute-done((bf16[480,128]{1,0:T(8,128)(2,1)S(1)}, bf16[480,128]{1,0:T(8,128)(2,1)S(1)}, u32[]{:S(2)}, u32[]{:S(2)}) %collective-permute-start.8) | collective-permute-done | bytes 122912 | tf_op jit(solution)/shard_map/ppermute | solution.py:393
  32.5 1.5 %collective-permute-done.9.refs_2_.refs_3_ = bf16[480,128]{1,0:T(8,128)(2,1)S(1)} collective-permute-done((bf16[480,128]{1,0:T(8,128)(2,1)S(1)}, bf16[480,128]{1,0:T(8,128)(2,1)S(1)}, u32[]{:S(2)}, u32[]{:S(2)}) %collective-permute-start.9) | collective-permute-done | bytes 122912 | tf_op jit(solution)/shard_map/ppermute | solution.py:393
  34.0 1.8 %collective-permute-done.10.refs_3_.refs_4_ = bf16[480,128]{1,0:T(8,128)(2,1)S(1)} collective-permute-done((bf16[480,128]{1,0:T(8,128)(2,1)S(1)}, bf16[480,128]{1,0:T(8,128)(2,1)S(1)}, u32[]{:S(2)}, u32[]{:S(2)}) %collective-permute-start.10) | collective-permute-done | bytes 122912 | tf_op jit(solution)/shard_map/ppermute | solution.py:393
  35.8 1.2 %shard_map.84 = (bf16[480,128]{1,0:T(8,128)(2,1)S(1)}, f32[4,480,128]{2,1,0:T(8,128)S(1)}, f32[4,480,128]{2,1,0:T(8,128)S(1)}) custom-call(bf16[480,128]{1,0:T(8,128)(2,1)S(1)} %get-tuple-element.57.refs_0_.refs_1_, bf16[480,128]{1,0:T(8,128)(2,1)S(1)} %collective-permute-done.8.refs_1_.refs_2_, bf16[480,128]{1,0:T(8,128)(2,1)S(1)} %collective-permute-done.9.refs_2_.refs_3_, ...), custom_call_target="tpu_custom_call" | custom-call | flops 10000000 | bytes 3072000 | tf_op jit(solution)/shard_map/pallas_call | solution.py:370
  37.8 3.3 %collective-permute-start.13 = (bf16[480,128]{1,0:T(8,128)(2,1)S(1)}, bf16[480,128]{1,0:T(8,128)(2,1)S(1)}, u32[]{:S(2)}, u32[]{:S(2)}) collective-permute-start(bf16[480,128]{1,0:T(8,128)(2,1)S(1)} %shard_map.88), channel_id=1, source_target_pairs={{0,16},{4,20},{8,24},{12,28},{16,0},{20,4},{24,8},{28,12},{1,17},{... | collective-permute-start | bytes 368648 | tf_op jit(solution)/shard_map/ppermute | solution.py:390
  43.7 1.7 %shard_map.85 = (f32[480,128]{1,0:T(8,128)S(1)}, f32[480,128]{1,0:T(8,128)S(1)}) custom-call(f32[960,128]{1,0:T(8,128)S(1)} %get-tuple-element.45.l_ref.refs_0_, f32[4,480,128]{2,1,0:T(8,128)S(1)} %get-tuple-element.62.gs, f32[4,480,128]{2,1,0:T(8,128)S(1)} %get-tuple-element.63.rs), custom_call_target="tpu_custom_call" | custom-call | flops 10000000 | bytes 2949120 | tf_op jit(solution)/shard_map/pallas_call | solution.py:370
  46.3 3.8 %collective-permute-done.13.refs_1_ = bf16[480,128]{1,0:T(8,128)(2,1)S(1)} collective-permute-done((bf16[480,128]{1,0:T(8,128)(2,1)S(1)}, bf16[480,128]{1,0:T(8,128)(2,1)S(1)}, u32[]{:S(2)}, u32[]{:S(2)}) %collective-permute-start.13) | collective-permute-done | bytes 122912 | tf_op jit(solution)/shard_map/ppermute | solution.py:390
  50.1 2.5 %collective-permute-done.15.refs_3_ = bf16[480,128]{1,0:T(8,128)(2,1)S(1)} collective-permute-done((bf16[480,128]{1,0:T(8,128)(2,1)S(1)}, bf16[480,128]{1,0:T(8,128)(2,1)S(1)}, u32[]{:S(2)}, u32[]{:S(2)}) %collective-permute-start.15) | collective-permute-done | bytes 122912 | tf_op jit(solution)/shard_map/ppermute | solution.py:390
  52.7 1.0 %shard_map.91 = bf16[15,30,128]{2,1,0:T(8,128)(2,1)} custom-call(f32[480,128]{1,0:T(8,128)S(1)} %get-tuple-element.72.refs_0_, bf16[480,128]{1,0:T(8,128)(2,1)S(1)} %collective-permute-done.13.refs_1_, bf16[480,128]{1,0:T(8,128)(2,1)S(1)} %collective-permute-done.14.refs_2_, bf16[480,128]{1,0:T(8,128)(2,1)S(1)} %collective-permute-done.15.refs_3_, ...), custom_call_target="tpu_custom_call" | custom-call | flops 10000000 | bytes 2089472 | tf_op jit(solution)/shard_map/pallas_call | solution.py:370
  (23 shorter events, 8.1 us)
Async XLA Ops:
  0.6 10.4 %collective-permute-start.2 = (bf16[15,30,128]{2,1,0:T(8,128)(2,1)}, bf16[15,30,128]{2,1,0:T(8,128)(2,1)S(1)}, u32[]{:S(2)}, u32[]{:S(2)}) collective-permute-start(bf16[15,30,128]{2,1,0:T(8,128)(2,1)} %refs_1_.1), channel_id=1, source_target_pairs={{0,16},{4,20},{8,24},{12,28},{16,0},{20,4},{24,8},{28,12},{1,17},{... | collective-permute-start | bytes 345608 | tf_op jit(solution)/shard_map/ppermute | solution.py:390
  4.8 8.1 %collective-permute-start = (bf16[15,30,128]{2,1,0:T(8,128)(2,1)}, bf16[15,30,128]{2,1,0:T(8,128)(2,1)S(1)}, u32[]{:S(2)}, u32[]{:S(2)}) collective-permute-start(bf16[15,30,128]{2,1,0:T(8,128)(2,1)} %refs_1_.1), channel_id=1, source_target_pairs={{0,4},{4,0},{8,12},{12,8},{16,20},{20,16},{24,28},{28,24},{1,5},{5... | collective-permute-start | bytes 345608 | tf_op jit(solution)/shard_map/ppermute | solution.py:397
  4.8 8.1 %collective-permute-start.1 = (bf16[15,30,128]{2,1,0:T(8,128)(2,1)}, bf16[15,30,128]{2,1,0:T(8,128)(2,1)S(1)}, u32[]{:S(2)}, u32[]{:S(2)}) collective-permute-start(bf16[15,30,128]{2,1,0:T(8,128)(2,1)} %refs_2_.1), channel_id=1, source_target_pairs={{0,4},{4,0},{8,12},{12,8},{16,20},{20,16},{24,28},{28,24},{1,5},{5... | collective-permute-start | bytes 345608 | tf_op jit(solution)/shard_map/ppermute | solution.py:397
  5.3 10.6 %collective-permute-start.3 = (bf16[15,30,128]{2,1,0:T(8,128)(2,1)}, bf16[15,30,128]{2,1,0:T(8,128)(2,1)S(1)}, u32[]{:S(2)}, u32[]{:S(2)}) collective-permute-start(bf16[15,30,128]{2,1,0:T(8,128)(2,1)} %refs_1_.1), channel_id=1, source_target_pairs={{0,8},{4,12},{8,0},{12,4},{16,24},{20,28},{24,16},{28,20},{1,9},{5... | collective-permute-start | bytes 345608 | tf_op jit(solution)/shard_map/ppermute | solution.py:390
  11.0 5.9 %collective-permute-start.4 = (bf16[15,30,128]{2,1,0:T(8,128)(2,1)S(1)}, bf16[15,30,128]{2,1,0:T(8,128)(2,1)S(1)}, u32[]{:S(2)}, u32[]{:S(2)}) collective-permute-start(bf16[15,30,128]{2,1,0:T(8,128)(2,1)S(1)} %collective-permute-done.2.refs_0_), channel_id=1, source_target_pairs={{0,8},{4,12},{8,0},{12,4},{16,24},{20,28},{24,16},{28,20},{1,9},{5... | collective-permute-start | bytes 345608 | tf_op jit(solution)/shard_map/ppermute | solution.py:390
  17.9 6.3 %collective-permute-start.5 = (bf16[480,128]{1,0:T(8,128)(2,1)S(1)}, bf16[480,128]{1,0:T(8,128)(2,1)S(1)}, u32[]{:S(2)}, u32[]{:S(2)}) collective-permute-start(bf16[480,128]{1,0:T(8,128)(2,1)S(1)} %get-tuple-element.51), channel_id=1, source_target_pairs={{0,1},{1,0},{2,3},{3,2},{4,7},{5,6},{6,5},{7,4},{8,9},{9,8},{10,11... | collective-permute-start | bytes 368648 | tf_op jit(solution)/shard_map/ppermute | solution.py:393
  19.5 5.7 %collective-permute-start.6 = (bf16[480,128]{1,0:T(8,128)(2,1)S(1)}, bf16[480,128]{1,0:T(8,128)(2,1)S(1)}, u32[]{:S(2)}, u32[]{:S(2)}) collective-permute-start(bf16[480,128]{1,0:T(8,128)(2,1)S(1)} %get-tuple-element.52), channel_id=1, source_target_pairs={{0,2},{1,3},{2,0},{3,1},{4,6},{5,7},{6,4},{7,5},{8,10},{9,11},{10,... | collective-permute-start | bytes 368648 | tf_op jit(solution)/shard_map/ppermute | solution.py:393
  21.0 5.8 %collective-permute-start.7 = (bf16[480,128]{1,0:T(8,128)(2,1)S(1)}, bf16[480,128]{1,0:T(8,128)(2,1)S(1)}, u32[]{:S(2)}, u32[]{:S(2)}) collective-permute-start(bf16[480,128]{1,0:T(8,128)(2,1)S(1)} %get-tuple-element.53), channel_id=1, source_target_pairs={{0,3},{1,2},{2,1},{3,0},{4,5},{5,4},{6,7},{7,6},{8,11},{9,10},{10,... | collective-permute-start | bytes 368648 | tf_op jit(solution)/shard_map/ppermute | solution.py:393
  27.3 5.2 %collective-permute-start.8 = (bf16[480,128]{1,0:T(8,128)(2,1)S(1)}, bf16[480,128]{1,0:T(8,128)(2,1)S(1)}, u32[]{:S(2)}, u32[]{:S(2)}) collective-permute-start(bf16[480,128]{1,0:T(8,128)(2,1)S(1)} %get-tuple-element.57.refs_0_.refs_1_), channel_id=1, source_target_pairs={{0,1},{1,0},{2,3},{3,2},{4,7},{5,6},{6,5},{7,4},{8,9},{9,8},{10,11... | collective-permute-start | bytes 368648 | tf_op jit(solution)/shard_map/ppermute | solution.py:393
  28.5 5.5 %collective-permute-start.9 = (bf16[480,128]{1,0:T(8,128)(2,1)S(1)}, bf16[480,128]{1,0:T(8,128)(2,1)S(1)}, u32[]{:S(2)}, u32[]{:S(2)}) collective-permute-start(bf16[480,128]{1,0:T(8,128)(2,1)S(1)} %get-tuple-element.57.refs_0_.refs_1_), channel_id=1, source_target_pairs={{0,2},{1,3},{2,0},{3,1},{4,6},{5,7},{6,4},{7,5},{8,10},{9,11},{10,... | collective-permute-start | bytes 368648 | tf_op jit(solution)/shard_map/ppermute | solution.py:393
  30.0 5.8 %collective-permute-start.10 = (bf16[480,128]{1,0:T(8,128)(2,1)S(1)}, bf16[480,128]{1,0:T(8,128)(2,1)S(1)}, u32[]{:S(2)}, u32[]{:S(2)}) collective-permute-start(bf16[480,128]{1,0:T(8,128)(2,1)S(1)} %get-tuple-element.57.refs_0_.refs_1_), channel_id=1, source_target_pairs={{0,3},{1,2},{2,1},{3,0},{4,5},{5,4},{6,7},{7,6},{8,11},{9,10},{10,... | collective-permute-start | bytes 368648 | tf_op jit(solution)/shard_map/ppermute | solution.py:393
  30.8 14.6 %collective-permute-start.12 = (bf16[480,128]{1,0:T(8,128)(2,1)S(1)}, bf16[480,128]{1,0:T(8,128)(2,1)S(1)}, u32[]{:S(2)}, u32[]{:S(2)}) collective-permute-start(bf16[480,128]{1,0:T(8,128)(2,1)S(1)} %get-tuple-element.70), channel_id=1, source_target_pairs={{0,4},{4,0},{8,12},{12,8},{16,20},{20,16},{24,28},{28,24},{1,5},{5... | collective-permute-start | bytes 368648 | tf_op jit(solution)/shard_map/ppermute | solution.py:397
  37.0 8.4 %collective-permute-start.11 = (bf16[480,128]{1,0:T(8,128)(2,1)S(1)}, bf16[480,128]{1,0:T(8,128)(2,1)S(1)}, u32[]{:S(2)}, u32[]{:S(2)}) collective-permute-start(bf16[480,128]{1,0:T(8,128)(2,1)S(1)} %get-tuple-element.65), channel_id=1, source_target_pairs={{0,4},{4,0},{8,12},{12,8},{16,20},{20,16},{24,28},{28,24},{1,5},{5... | collective-permute-start | bytes 368648 | tf_op jit(solution)/shard_map/ppermute | solution.py:397
  37.8 12.4 %collective-permute-start.13 = (bf16[480,128]{1,0:T(8,128)(2,1)S(1)}, bf16[480,128]{1,0:T(8,128)(2,1)S(1)}, u32[]{:S(2)}, u32[]{:S(2)}) collective-permute-start(bf16[480,128]{1,0:T(8,128)(2,1)S(1)} %shard_map.88), channel_id=1, source_target_pairs={{0,16},{4,20},{8,24},{12,28},{16,0},{20,4},{24,8},{28,12},{1,17},{... | collective-permute-start | bytes 368648 | tf_op jit(solution)/shard_map/ppermute | solution.py:390
  41.7 8.4 %collective-permute-start.14 = (bf16[480,128]{1,0:T(8,128)(2,1)S(1)}, bf16[480,128]{1,0:T(8,128)(2,1)S(1)}, u32[]{:S(2)}, u32[]{:S(2)}) collective-permute-start(bf16[480,128]{1,0:T(8,128)(2,1)S(1)} %shard_map.89), channel_id=1, source_target_pairs={{0,24},{4,28},{8,16},{12,20},{16,8},{20,12},{24,0},{28,4},{1,25},{... | collective-permute-start | bytes 368648 | tf_op jit(solution)/shard_map/ppermute | solution.py:390
  42.5 10.2 %collective-permute-start.15 = (bf16[480,128]{1,0:T(8,128)(2,1)S(1)}, bf16[480,128]{1,0:T(8,128)(2,1)S(1)}, u32[]{:S(2)}, u32[]{:S(2)}) collective-permute-start(bf16[480,128]{1,0:T(8,128)(2,1)S(1)} %shard_map.90), channel_id=1, source_target_pairs={{0,8},{4,12},{8,0},{12,4},{16,24},{20,28},{24,16},{28,20},{1,9},{5... | collective-permute-start | bytes 368648 | tf_op jit(solution)/shard_map/ppermute | solution.py:390

commit v7 on v6

--- a/solution.py
+++ b/solution.py
@@ -263,7 +263,7 @@
     l_ref, pieces = refs[0], refs[1 : 1 + blocks]
     more, (out_ref, gs) = refs[1 + blocks : -2], refs[-2:]
     chip, column = this_chip(), lax.axis_index("ch")
-    step = lookup(steps, chip)
+    step = lookup(steps, lax.axis_index("dap"))
     for t in range(blocks):
         @pl.when(chip ^ column ^ step == my_turn(t, blocks))
         def _(t=t):
@@ -440,7 +440,7 @@
         more = () if extra is None else (got[extra],)
         (send,) = call(functools.partial(send_right_kernel, rows, cols, blocks, table),
                        [((cells, hidden), BF16)], (left, *pieces, *more), [(mids, hidden)])
-        got += [along_dap(send, pairs) for pairs in returns[n]]
+        got.append(lax.ppermute(send, "dap", returns[n][0]))
     left_send, staged, rights_staged = call(
         functools.partial(pair_left_kernel, rows, cols, steps),
         [((cells, hidden), BF16), ((blocks, mids, hidden), F32), ((blocks, cells, hidden), F32)], (*pieces, *rights))
@@ -471,8 +471,9 @@
 
 def reduce_plan(blocks):
     far = [*range(2, blocks), 1]
-    sends = [([s] * blocks, None) for s in far]
-    return sends, [[[(z, z ^ s) for z in range(blocks)]] for s in far], [*range(blocks - 1)]
+    odd = [*range(blocks - 1, 0, -1)]
+    sends = [([a, b] * blocks, None) for a, b in zip(far, odd)]
+    return sends, [[[(2 * z + c, 2 * (z ^ s) + c) for z in range(blocks) for c, s in enumerate(pair)]] for pair in zip(far, odd)], [*range(blocks - 1)]
 
 
 def solution(mesh):

time: 53.9 us -> 53.4 us (level)
  the two profiles are of different devices: /device:TPU:0 before, /device:TPU:1 now
where the time goes in v7:
time: 53.4 us; the launch traced here: 53.3 us
  starting transfers between devices  21.2 us (40%)
  waiting for transfers between devices  17.5 us (33%)
  Pallas kernels  13.8 us (26%)
  between operations  0.77 us (1%)
    pallas_call x15, Pallas kernels, call(): pl.pallas_call(body, out_shape=outs, in_specs=[specs] * len(args), out_sp...  13.8 us
    ppermute x6, waiting for transfers between devices, along_ch(): lax.ppermute(value, ('dap', 'ch'), [(d * blocks + h, d * blocks + (h ^ tu...  7.99 us
    ppermute x3, waiting for transfers between devices, on_device(): got.append(lax.ppermute(send, 'dap', returns[n][0]))  6.27 us
    ppermute x3, starting transfers between devices, along_dap(): lax.ppermute(value, 'dap', [(2 * a + c, 2 * b + c) for a, b in pairs for...  6.26 us
    ppermute x4, starting transfers between devices, to_partner(): return lax.ppermute(value, 'dap', [(d, d ^ 1) for d in range(devices)])  5.73 us
    ppermute x6, starting transfers between devices, along_ch(): lax.ppermute(value, ('dap', 'ch'), [(d * blocks + h, d * blocks + (h ^ tu...  5.49 us
    ppermute x3, starting transfers between devices, on_device(): got.append(lax.ppermute(send, 'dap', returns[n][0]))  3.76 us
    ppermute x3, waiting for transfers between devices, along_dap(): lax.ppermute(value, 'dap', [(2 * a + c, 2 * b + c) for a, b in pairs for...  3.2 us
  transfers between devices with their start and end apart: 16, of which 7 were waited for; matrix products, arithmetic and copies ran while one was open for 0% of the time, Pallas kernels for 21%

profile of v7, /device:TPU:1, one launch (start us, length us, event | category | flops | bytes accessed | tf_op | source)
XLA Modules:
  0.0 53.3 jit_solution(10733216036386825177)
XLA Ops:
  0.6 3.2 %collective-permute-start.2 = (bf16[15,30,128]{2,1,0:T(8,128)(2,1)}, bf16[15,30,128]{2,1,0:T(8,128)(2,1)S(1)}, u32[]{:S(2)}, u32[]{:S(2)}) collective-permute-start(bf16[15,30,128]{2,1,0:T(8,128)(2,1)} %refs_1_.1), channel_id=1, source_target_pairs={{0,16},{4,20},{8,24},{12,28},{16,0},{20,4},{24,8},{28,12},{1,17},{... | collective-permute-start | bytes 345608 | tf_op jit(solution)/shard_map/ppermute | solution.py:390
  3.8 1.0 %collective-permute-start = (bf16[15,30,128]{2,1,0:T(8,128)(2,1)}, bf16[15,30,128]{2,1,0:T(8,128)(2,1)S(1)}, u32[]{:S(2)}, u32[]{:S(2)}) collective-permute-start(bf16[15,30,128]{2,1,0:T(8,128)(2,1)} %refs_1_.1), channel_id=1, source_target_pairs={{0,4},{4,0},{8,12},{12,8},{16,20},{20,16},{24,28},{28,24},{1,5},{5... | collective-permute-start | bytes 345608 | tf_op jit(solution)/shard_map/ppermute | solution.py:397
  4.8 1.3 %collective-permute-start.3 = (bf16[15,30,128]{2,1,0:T(8,128)(2,1)}, bf16[15,30,128]{2,1,0:T(8,128)(2,1)S(1)}, u32[]{:S(2)}, u32[]{:S(2)}) collective-permute-start(bf16[15,30,128]{2,1,0:T(8,128)(2,1)} %refs_1_.1), channel_id=1, source_target_pairs={{0,8},{4,12},{8,0},{12,4},{16,24},{20,28},{24,16},{28,20},{1,9},{5... | collective-permute-start | bytes 345608 | tf_op jit(solution)/shard_map/ppermute | solution.py:390
  6.1 3.2 %collective-permute-done.2.refs_0_ = bf16[15,30,128]{2,1,0:T(8,128)(2,1)S(1)} collective-permute-done((bf16[15,30,128]{2,1,0:T(8,128)(2,1)}, bf16[15,30,128]{2,1,0:T(8,128)(2,1)S(1)}, u32[]{:S(2)}, u32[]{:S(2)}) %collective-permute-start.2) | collective-permute-done | bytes 115232 | tf_op jit(solution)/shard_map/ppermute | solution.py:390
  9.3 1.8 %collective-permute-start.4 = (bf16[15,30,128]{2,1,0:T(8,128)(2,1)S(1)}, bf16[15,30,128]{2,1,0:T(8,128)(2,1)S(1)}, u32[]{:S(2)}, u32[]{:S(2)}) collective-permute-start(bf16[15,30,128]{2,1,0:T(8,128)(2,1)S(1)} %collective-permute-done.2.refs_0_), channel_id=1, source_target_pairs={{0,8},{4,12},{8,0},{12,4},{16,24},{20,28},{24,16},{28,20},{1,9},{5... | collective-permute-start | bytes 345608 | tf_op jit(solution)/shard_map/ppermute | solution.py:390
  11.0 1.1 %shard_map.77 = (bf16[15,30,128]{2,1,0:T(8,128)(2,1)S(1)}, bf16[15,30,128]{2,1,0:T(8,128)(2,1)S(1)}, bf16[128,512]{1,0:T(8,128)(2,1)S(1)}, bf16[128,128]{1,0:T(8...) custom-call(s32[120]{0:T(128)} %refs_0_.1, bf16[15,30,128]{2,1,0:T(8,128)(2,1)} %refs_1_.1, ...), custom_call_target="tpu_custom_call" | custom-call | flops 10000000 | bytes 920032 | tf_op jit(solution)/shard_map/pallas_call | solution.py:370
  12.1 1.0 %shard_map.78 = (f32[960,128]{1,0:T(8,128)S(1)}, f32[960,128]{1,0:T(8,128)S(1)}, f32[480,128]{1,0:T(8,128)S(1)}, f32[480,128]{1,0:T(8,128)S(1)}) custom-call(f32[128,128]{1,0:T(8,128)S(1)} %get-tuple-element.40.live_ref, bf16[15,30,128]{2,1,0:T(8,128)(2,1)S(1)} %get-tuple-element.41.x_ref.refs_0_, bf16[15,30,128]{2,1,0:T(8,128)(2,1)S(1)} %collective-permute-done.xp_ref, ...), custom_call_target="tpu_custom_call" | custom-call | flops 10000000 | bytes 2164736 | tf_op jit(solution)/shard_map/pallas_call | solution.py:370
  13.2 1.0 %shard_map.79 = (bf16[480,128]{1,0:T(8,128)(2,1)S(1)}, bf16[480,128]{1,0:T(8,128)(2,1)S(1)}) custom-call(f32[128,128]{1,0:T(8,128)S(1)} %get-tuple-element.40.live_ref, f32[960,128]{1,0:T(8,128)S(1)} %get-tuple-element.46.lt_ref, bf16[128,512]{1,0:T(8,128)(2,1)S(1)} %get-tuple-element.43.w_ref.refs_6_, bf16[15,30,128]{2,1,0:T(8,128)(2,1)S(1)} %get-tuple-element.41.x_ref.refs_0_), custom_call_target="tpu_custom_call" | custom-call | flops 10000000 | bytes 1049088 | tf_op jit(solution)/shard_map/pallas_call | solution.py:370
  14.1 1.0 %shard_map.80 = (bf16[480,128]{1,0:T(8,128)(2,1)S(1)}, bf16[480,128]{1,0:T(8,128)(2,1)S(1)}) custom-call(f32[128,128]{1,0:T(8,128)S(1)} %get-tuple-element.40.live_ref, f32[960,128]{1,0:T(8,128)S(1)} %get-tuple-element.46.lt_ref, bf16[128,512]{1,0:T(8,128)(2,1)S(1)} %get-tuple-element.43.w_ref.refs_6_, bf16[15,30,128]{2,1,0:T(8,128)(2,1)S(1)} %collective-permute-done.2.refs_0_), custom_call_target="tpu_custom_call" | custom-call | flops 10000000 | bytes 1049088 | tf_op jit(solution)/shard_map/pallas_call | solution.py:370
  15.1 1.0 %shard_map.81 = (bf16[480,128]{1,0:T(8,128)(2,1)S(1)}, bf16[480,128]{1,0:T(8,128)(2,1)S(1)}) custom-call(f32[128,128]{1,0:T(8,128)S(1)} %get-tuple-element.40.live_ref, f32[960,128]{1,0:T(8,128)S(1)} %get-tuple-element.46.lt_ref, bf16[128,512]{1,0:T(8,128)(2,1)S(1)} %get-tuple-element.43.w_ref.refs_6_, bf16[15,30,128]{2,1,0:T(8,128)(2,1)S(1)} %collective-permute-done.3.refs_0_), custom_call_target="tpu_custom_call" | custom-call | flops 10000000 | bytes 1049088 | tf_op jit(solution)/shard_map/pallas_call | solution.py:370
  16.1 1.0 %shard_map.82 = (bf16[480,128]{1,0:T(8,128)(2,1)S(1)}, bf16[480,128]{1,0:T(8,128)(2,1)S(1)}, bf16[480,128]{1,0:T(8,128)(2,1)S(1)}, bf16[480,128]{1,0:T(8,128)(2,1)S(1)}, bf16[480,128]{1,0:T(8,128)(2,1)S(1)}) custom-call(f32[128,128]{1,0:T(8,128)S(1)} %get-tuple-element.40.live_ref, f32[960,128]{1,0:T(8,128)S(1)} %get-tuple-element.46.lt_ref, ...), custom_call_target="tpu_custom_call" | custom-call | flops 10000000 | bytes 1786368 | tf_op jit(solution)/shard_map/pallas_call | solution.py:370
  17.2 2.2 %collective-permute-start.5 = (bf16[480,128]{1,0:T(8,128)(2,1)S(1)}, bf16[480,128]{1,0:T(8,128)(2,1)S(1)}, u32[]{:S(2)}, u32[]{:S(2)}) collective-permute-start(bf16[480,128]{1,0:T(8,128)(2,1)S(1)} %get-tuple-element.51), channel_id=1, source_target_pairs={{0,1},{1,0},{2,3},{3,2},{4,7},{5,6},{6,5},{7,4},{8,9},{9,8},{10,11... | collective-permute-start | bytes 368648 | tf_op jit(solution)/shard_map/ppermute | solution.py:393
  19.9 2.4 %collective-permute-done.5.refs_1_ = bf16[480,128]{1,0:T(8,128)(2,1)S(1)} collective-permute-done((bf16[480,128]{1,0:T(8,128)(2,1)S(1)}, bf16[480,128]{1,0:T(8,128)(2,1)S(1)}, u32[]{:S(2)}, u32[]{:S(2)}) %collective-permute-start.5) | collective-permute-done | bytes 122912 | tf_op jit(solution)/shard_map/ppermute | solution.py:393
  22.3 2.0 %collective-permute-done.6.refs_2_ = bf16[480,128]{1,0:T(8,128)(2,1)S(1)} collective-permute-done((bf16[480,128]{1,0:T(8,128)(2,1)S(1)}, bf16[480,128]{1,0:T(8,128)(2,1)S(1)}, u32[]{:S(2)}, u32[]{:S(2)}) %collective-permute-start.6) | collective-permute-done | bytes 122912 | tf_op jit(solution)/shard_map/ppermute | solution.py:393
  24.3 1.3 %collective-permute-done.7.refs_3_ = bf16[480,128]{1,0:T(8,128)(2,1)S(1)} collective-permute-done((bf16[480,128]{1,0:T(8,128)(2,1)S(1)}, bf16[480,128]{1,0:T(8,128)(2,1)S(1)}, u32[]{:S(2)}, u32[]{:S(2)}) %collective-permute-start.7) | collective-permute-done | bytes 122912 | tf_op jit(solution)/shard_map/ppermute | solution.py:393
  26.7 2.1 %collective-permute-start.9 = (bf16[480,128]{1,0:T(8,128)(2,1)S(1)}, bf16[480,128]{1,0:T(8,128)(2,1)S(1)}, u32[]{:S(2)}, u32[]{:S(2)}) collective-permute-start(bf16[480,128]{1,0:T(8,128)(2,1)S(1)} %get-tuple-element.57.refs_0_.refs_1_), channel_id=1, source_target_pairs={{0,2},{1,3},{2,0},{3,1},{4,6},{5,7},{6,4},{7,5},{8,10},{9,11},{10,... | collective-permute-start | bytes 368648 | tf_op jit(solution)/shard_map/ppermute | solution.py:393
  28.8 2.0 %collective-permute-start.12 = (bf16[480,128]{1,0:T(8,128)(2,1)S(1)}, bf16[480,128]{1,0:T(8,128)(2,1)S(1)}, u32[]{:S(2)}, u32[]{:S(2)}) collective-permute-start(bf16[480,128]{1,0:T(8,128)(2,1)S(1)} %get-tuple-element.70), channel_id=1, source_target_pairs={{0,4},{4,0},{8,12},{12,8},{16,20},{20,16},{24,28},{28,24},{1,5},{5... | collective-permute-start | bytes 368648 | tf_op jit(solution)/shard_map/ppermute | solution.py:397
  30.8 2.1 %collective-permute-done.9.refs_2_.refs_3_ = bf16[480,128]{1,0:T(8,128)(2,1)S(1)} collective-permute-done((bf16[480,128]{1,0:T(8,128)(2,1)S(1)}, bf16[480,128]{1,0:T(8,128)(2,1)S(1)}, u32[]{:S(2)}, u32[]{:S(2)}) %collective-permute-start.9) | collective-permute-done | bytes 122912 | tf_op jit(solution)/shard_map/ppermute | solution.py:393
  33.1 1.2 %shard_map.84 = (bf16[480,128]{1,0:T(8,128)(2,1)S(1)}, f32[4,480,128]{2,1,0:T(8,128)S(1)}, f32[4,480,128]{2,1,0:T(8,128)S(1)}) custom-call(bf16[480,128]{1,0:T(8,128)(2,1)S(1)} %get-tuple-element.57.refs_0_.refs_1_, bf16[480,128]{1,0:T(8,128)(2,1)S(1)} %collective-permute-done.8.refs_1_.refs_2_, bf16[480,128]{1,0:T(8,128)(2,1)S(1)} %collective-permute-done.9.refs_2_.refs_3_, ...), custom_call_target="tpu_custom_call" | custom-call | flops 10000000 | bytes 3072000 | tf_op jit(solution)/shard_map/pallas_call | solution.py:370
  34.4 2.8 %collective-permute-start.11 = (bf16[480,128]{1,0:T(8,128)(2,1)S(1)}, bf16[480,128]{1,0:T(8,128)(2,1)S(1)}, u32[]{:S(2)}, u32[]{:S(2)}) collective-permute-start(bf16[480,128]{1,0:T(8,128)(2,1)S(1)} %get-tuple-element.65), channel_id=1, source_target_pairs={{0,4},{4,0},{8,12},{12,8},{16,20},{20,16},{24,28},{28,24},{1,5},{5... | collective-permute-start | bytes 368648 | tf_op jit(solution)/shard_map/ppermute | solution.py:397
  37.7 2.8 %collective-permute-start.13 = (bf16[480,128]{1,0:T(8,128)(2,1)S(1)}, bf16[480,128]{1,0:T(8,128)(2,1)S(1)}, u32[]{:S(2)}, u32[]{:S(2)}) collective-permute-start(bf16[480,128]{1,0:T(8,128)(2,1)S(1)} %shard_map.88), channel_id=1, source_target_pairs={{0,16},{4,28},{8,24},{12,20},{16,0},{20,12},{24,8},{28,4},{1,17},{... | collective-permute-start | bytes 368648 | tf_op jit(solution)/shard_map/ppermute | solution.py:443
  43.3 1.7 %shard_map.85 = (f32[480,128]{1,0:T(8,128)S(1)}, f32[480,128]{1,0:T(8,128)S(1)}) custom-call(f32[960,128]{1,0:T(8,128)S(1)} %get-tuple-element.45.l_ref.refs_0_, f32[4,480,128]{2,1,0:T(8,128)S(1)} %get-tuple-element.62.gs, f32[4,480,128]{2,1,0:T(8,128)S(1)} %get-tuple-element.63.rs), custom_call_target="tpu_custom_call" | custom-call | flops 10000000 | bytes 2949120 | tf_op jit(solution)/shard_map/pallas_call | solution.py:370
  46.0 6.3 %collective-permute-done.14.refs_2_ = bf16[480,128]{1,0:T(8,128)(2,1)S(1)} collective-permute-done((bf16[480,128]{1,0:T(8,128)(2,1)S(1)}, bf16[480,128]{1,0:T(8,128)(2,1)S(1)}, u32[]{:S(2)}, u32[]{:S(2)}) %collective-permute-start.14) | collective-permute-done | bytes 122912 | tf_op jit(solution)/shard_map/ppermute | solution.py:443
  52.2 1.0 %shard_map.91 = bf16[15,30,128]{2,1,0:T(8,128)(2,1)} custom-call(f32[480,128]{1,0:T(8,128)S(1)} %get-tuple-element.72.refs_0_, bf16[480,128]{1,0:T(8,128)(2,1)S(1)} %collective-permute-done.13.refs_1_, bf16[480,128]{1,0:T(8,128)(2,1)S(1)} %collective-permute-done.14.refs_2_, bf16[480,128]{1,0:T(8,128)(2,1)S(1)} %collective-permute-done.15.refs_3_, ...), custom_call_target="tpu_custom_call" | custom-call | flops 10000000 | bytes 2089472 | tf_op jit(solution)/shard_map/pallas_call | solution.py:370
  (23 shorter events, 6.1 us)
Async XLA Ops:
  0.6 8.6 %collective-permute-start.2 = (bf16[15,30,128]{2,1,0:T(8,128)(2,1)}, bf16[15,30,128]{2,1,0:T(8,128)(2,1)S(1)}, u32[]{:S(2)}, u32[]{:S(2)}) collective-permute-start(bf16[15,30,128]{2,1,0:T(8,128)(2,1)} %refs_1_.1), channel_id=1, source_target_pairs={{0,16},{4,20},{8,24},{12,28},{16,0},{20,4},{24,8},{28,12},{1,17},{... | collective-permute-start | bytes 345608 | tf_op jit(solution)/shard_map/ppermute | solution.py:390
  3.8 8.3 %collective-permute-start = (bf16[15,30,128]{2,1,0:T(8,128)(2,1)}, bf16[15,30,128]{2,1,0:T(8,128)(2,1)S(1)}, u32[]{:S(2)}, u32[]{:S(2)}) collective-permute-start(bf16[15,30,128]{2,1,0:T(8,128)(2,1)} %refs_1_.1), channel_id=1, source_target_pairs={{0,4},{4,0},{8,12},{12,8},{16,20},{20,16},{24,28},{28,24},{1,5},{5... | collective-permute-start | bytes 345608 | tf_op jit(solution)/shard_map/ppermute | solution.py:397
  4.8 7.4 %collective-permute-start.1 = (bf16[15,30,128]{2,1,0:T(8,128)(2,1)}, bf16[15,30,128]{2,1,0:T(8,128)(2,1)S(1)}, u32[]{:S(2)}, u32[]{:S(2)}) collective-permute-start(bf16[15,30,128]{2,1,0:T(8,128)(2,1)} %refs_2_.1), channel_id=1, source_target_pairs={{0,4},{4,0},{8,12},{12,8},{16,20},{20,16},{24,28},{28,24},{1,5},{5... | collective-permute-start | bytes 345608 | tf_op jit(solution)/shard_map/ppermute | solution.py:397
  4.8 10.3 %collective-permute-start.3 = (bf16[15,30,128]{2,1,0:T(8,128)(2,1)}, bf16[15,30,128]{2,1,0:T(8,128)(2,1)S(1)}, u32[]{:S(2)}, u32[]{:S(2)}) collective-permute-start(bf16[15,30,128]{2,1,0:T(8,128)(2,1)} %refs_1_.1), channel_id=1, source_target_pairs={{0,8},{4,12},{8,0},{12,4},{16,24},{20,28},{24,16},{28,20},{1,9},{5... | collective-permute-start | bytes 345608 | tf_op jit(solution)/shard_map/ppermute | solution.py:390
  9.3 6.9 %collective-permute-start.4 = (bf16[15,30,128]{2,1,0:T(8,128)(2,1)S(1)}, bf16[15,30,128]{2,1,0:T(8,128)(2,1)S(1)}, u32[]{:S(2)}, u32[]{:S(2)}) collective-permute-start(bf16[15,30,128]{2,1,0:T(8,128)(2,1)S(1)} %collective-permute-done.2.refs_0_), channel_id=1, source_target_pairs={{0,8},{4,12},{8,0},{12,4},{16,24},{20,28},{24,16},{28,20},{1,9},{5... | collective-permute-start | bytes 345608 | tf_op jit(solution)/shard_map/ppermute | solution.py:390
  17.2 5.1 %collective-permute-start.5 = (bf16[480,128]{1,0:T(8,128)(2,1)S(1)}, bf16[480,128]{1,0:T(8,128)(2,1)S(1)}, u32[]{:S(2)}, u32[]{:S(2)}) collective-permute-start(bf16[480,128]{1,0:T(8,128)(2,1)S(1)} %get-tuple-element.51), channel_id=1, source_target_pairs={{0,1},{1,0},{2,3},{3,2},{4,7},{5,6},{6,5},{7,4},{8,9},{9,8},{10,11... | collective-permute-start | bytes 368648 | tf_op jit(solution)/shard_map/ppermute | solution.py:393
  19.4 4.9 %collective-permute-start.6 = (bf16[480,128]{1,0:T(8,128)(2,1)S(1)}, bf16[480,128]{1,0:T(8,128)(2,1)S(1)}, u32[]{:S(2)}, u32[]{:S(2)}) collective-permute-start(bf16[480,128]{1,0:T(8,128)(2,1)S(1)} %get-tuple-element.52), channel_id=1, source_target_pairs={{0,2},{1,3},{2,0},{3,1},{4,6},{5,7},{6,4},{7,5},{8,10},{9,11},{10,... | collective-permute-start | bytes 368648 | tf_op jit(solution)/shard_map/ppermute | solution.py:393
  19.6 5.9 %collective-permute-start.7 = (bf16[480,128]{1,0:T(8,128)(2,1)S(1)}, bf16[480,128]{1,0:T(8,128)(2,1)S(1)}, u32[]{:S(2)}, u32[]{:S(2)}) collective-permute-start(bf16[480,128]{1,0:T(8,128)(2,1)S(1)} %get-tuple-element.53), channel_id=1, source_target_pairs={{0,3},{1,2},{2,1},{3,0},{4,5},{5,4},{6,7},{7,6},{8,11},{9,10},{10,... | collective-permute-start | bytes 368648 | tf_op jit(solution)/shard_map/ppermute | solution.py:393
  26.0 4.8 %collective-permute-start.8 = (bf16[480,128]{1,0:T(8,128)(2,1)S(1)}, bf16[480,128]{1,0:T(8,128)(2,1)S(1)}, u32[]{:S(2)}, u32[]{:S(2)}) collective-permute-start(bf16[480,128]{1,0:T(8,128)(2,1)S(1)} %get-tuple-element.57.refs_0_.refs_1_), channel_id=1, source_target_pairs={{0,1},{1,0},{2,3},{3,2},{4,7},{5,6},{6,5},{7,4},{8,9},{9,8},{10,11... | collective-permute-start | bytes 368648 | tf_op jit(solution)/shard_map/ppermute | solution.py:393
  26.7 6.3 %collective-permute-start.9 = (bf16[480,128]{1,0:T(8,128)(2,1)S(1)}, bf16[480,128]{1,0:T(8,128)(2,1)S(1)}, u32[]{:S(2)}, u32[]{:S(2)}) collective-permute-start(bf16[480,128]{1,0:T(8,128)(2,1)S(1)} %get-tuple-element.57.refs_0_.refs_1_), channel_id=1, source_target_pairs={{0,2},{1,3},{2,0},{3,1},{4,6},{5,7},{6,4},{7,5},{8,10},{9,11},{10,... | collective-permute-start | bytes 368648 | tf_op jit(solution)/shard_map/ppermute | solution.py:393
  28.8 4.3 %collective-permute-start.10 = (bf16[480,128]{1,0:T(8,128)(2,1)S(1)}, bf16[480,128]{1,0:T(8,128)(2,1)S(1)}, u32[]{:S(2)}, u32[]{:S(2)}) collective-permute-start(bf16[480,128]{1,0:T(8,128)(2,1)S(1)} %get-tuple-element.57.refs_0_.refs_1_), channel_id=1, source_target_pairs={{0,3},{1,2},{2,1},{3,0},{4,5},{5,4},{6,7},{7,6},{8,11},{9,10},{10,... | collective-permute-start | bytes 368648 | tf_op jit(solution)/shard_map/ppermute | solution.py:393
  28.8 16.2 %collective-permute-start.12 = (bf16[480,128]{1,0:T(8,128)(2,1)S(1)}, bf16[480,128]{1,0:T(8,128)(2,1)S(1)}, u32[]{:S(2)}, u32[]{:S(2)}) collective-permute-start(bf16[480,128]{1,0:T(8,128)(2,1)S(1)} %get-tuple-element.70), channel_id=1, source_target_pairs={{0,4},{4,0},{8,12},{12,8},{16,20},{20,16},{24,28},{28,24},{1,5},{5... | collective-permute-start | bytes 368648 | tf_op jit(solution)/shard_map/ppermute | solution.py:397
  34.4 10.7 %collective-permute-start.11 = (bf16[480,128]{1,0:T(8,128)(2,1)S(1)}, bf16[480,128]{1,0:T(8,128)(2,1)S(1)}, u32[]{:S(2)}, u32[]{:S(2)}) collective-permute-start(bf16[480,128]{1,0:T(8,128)(2,1)S(1)} %get-tuple-element.65), channel_id=1, source_target_pairs={{0,4},{4,0},{8,12},{12,8},{16,20},{20,16},{24,28},{28,24},{1,5},{5... | collective-permute-start | bytes 368648 | tf_op jit(solution)/shard_map/ppermute | solution.py:397
  37.7 8.2 %collective-permute-start.13 = (bf16[480,128]{1,0:T(8,128)(2,1)S(1)}, bf16[480,128]{1,0:T(8,128)(2,1)S(1)}, u32[]{:S(2)}, u32[]{:S(2)}) collective-permute-start(bf16[480,128]{1,0:T(8,128)(2,1)S(1)} %shard_map.88), channel_id=1, source_target_pairs={{0,16},{4,28},{8,24},{12,20},{16,0},{20,12},{24,8},{28,4},{1,17},{... | collective-permute-start | bytes 368648 | tf_op jit(solution)/shard_map/ppermute | solution.py:443
  41.2 11.1 %collective-permute-start.14 = (bf16[480,128]{1,0:T(8,128)(2,1)S(1)}, bf16[480,128]{1,0:T(8,128)(2,1)S(1)}, u32[]{:S(2)}, u32[]{:S(2)}) collective-permute-start(bf16[480,128]{1,0:T(8,128)(2,1)S(1)} %shard_map.89), channel_id=1, source_target_pairs={{0,24},{4,20},{8,16},{12,28},{16,8},{20,4},{24,0},{28,12},{1,25},{... | collective-permute-start | bytes 368648 | tf_op jit(solution)/shard_map/ppermute | solution.py:443
  42.2 10.1 %collective-permute-start.15 = (bf16[480,128]{1,0:T(8,128)(2,1)S(1)}, bf16[480,128]{1,0:T(8,128)(2,1)S(1)}, u32[]{:S(2)}, u32[]{:S(2)}) collective-permute-start(bf16[480,128]{1,0:T(8,128)(2,1)S(1)} %shard_map.90), channel_id=1, source_target_pairs={{0,8},{4,12},{8,0},{12,4},{16,24},{20,28},{24,16},{28,20},{1,9},{5... | collective-permute-start | bytes 368648 | tf_op jit(solution)/shard_map/ppermute | solution.py:443
